TPU v7x, 256 devices: a whole 4x4x8 slice. The times are simulated.
256 devices in a mesh: cell: 64 (over y, z, core), view: 4 (over x).
Axes of the slice: x: 4, y: 4, z: 8, core: 2. Of those that a mesh axis runs over, the one named last changes fastest.
Arguments:
- gaussians: float32 [1024, 9, 256], P('cell'), as said below
- seg_count: int32 [4, 64], P('view', 'cell'), may hold values from 1 to 3, as said below
- seg_block: int32 [4, 64, 3], P('view', 'cell'), may hold values from 0 to 1023, as said below
- ray_count: int32 [4, 64], P('view', 'cell'), may hold values from 576 to 2304
- camera_shift: float32 [4, 2], P('view'), may hold values from -6 to 6
- target: float32 [4, 64, 3, 2304], P('view', 'cell'), may hold values from 0 to 1
Outputs:
- image: float32 [4, 64, 3, 2304], P('view', 'cell')
- gauss_grad: float32 [1024, 9, 256], P('cell')
Inputs may be any that keep to these rules, and one draw needn't show every extreme that they name: `gaussians`: each column of a block is one Gaussian: a mean, the entries a, b, c of a positive definite inverse covariance, an opacity in (0, 1), three colours. `seg_count`: tiles 2m and 2m + 1 of a view hold 4 segments together; in every view some tile holds 3. Segment k of tile t uses a block stored in cell seg_block // 16, which is t + e modulo 64 for some e from -2 to 2; entries at k >= seg_count are not used.
All inputs are finite; a program needn't handle non-finite values.
Results may differ from a plain program's by a relative error of at most 0.0003.
Values sent between devices are 32-bit elements; how exact they have to be, the bound alone decides.
No kernel may reach another device: no remote copies, remote signals or barrier semaphores. Data moves between devices by JAX's collectives and lax.ppermute only.
A program may use at most 64 MiB of HBM per device.

v0:
```python
import jax
import jax.numpy as jnp
from jax import lax
from jax.sharding import PartitionSpec as P

TILE = 48
REACH = 2


precise = lax.Precision.HIGHEST


def shifted(block, axis, distance):
    devices = range(lax.axis_size(axis))
    route = [((i - distance) % len(devices), i) for i in devices]
    return lax.ppermute(block, axis, route)


def pixel_frame(shift, pixels):
    pixel_ids = jnp.arange(pixels)
    centre = (TILE - 1) / 2.0
    pix_x = (pixel_ids % TILE).astype(jnp.float32) - centre - shift[0]
    pix_y = (pixel_ids // TILE).astype(jnp.float32) - centre - shift[1]
    return (pix_x, pix_y)


def triangles(length):
    row_ids = lax.broadcasted_iota(jnp.int32, (length, length), 0)
    col_ids = lax.broadcasted_iota(jnp.int32, (length, length), 1)
    return ((col_ids < row_ids).astype(jnp.float32), (col_ids > row_ids).astype(jnp.float32))


def splat(params, pix_x, pix_y):
    delta_x = pix_x[None, :] - params[0][:, None]
    delta_y = pix_y[None, :] - params[1][:, None]
    quad_form = (
        params[2][:, None] * delta_x * delta_x
        + 2.0 * params[3][:, None] * delta_x * delta_y
        + params[4][:, None] * delta_y * delta_y
    )
    alphas = params[5][:, None] * jnp.exp(-0.5 * quad_form)
    return (alphas, jnp.log1p(-alphas))


def forward_task(params, pix_x, pix_y, lower_tri):
    alphas, log_trans = splat(params, pix_x, pix_y)
    prefix = jnp.dot(lower_tri, log_trans, precision=precise, preferred_element_type=jnp.float32)
    weights = alphas * jnp.exp(prefix)
    colour = jnp.dot(params[6:9], weights, precision=precise, preferred_element_type=jnp.float32)
    totals = jnp.sum(log_trans, axis=0)
    return jnp.concatenate([colour, totals[None, :]], axis=0)


def gradient_rows(params, pix_x, pix_y, weighted, weights, weight_cot):
    features = jnp.stack(
        [jnp.ones_like(pix_x), pix_x, pix_y, pix_x * pix_x, pix_x * pix_y, pix_y * pix_y]
    )
    moments = lax.dot_general(
        features,
        weighted,
        (((1,), (1,)), ((), ())),
        precision=precise,
        preferred_element_type=jnp.float32,
    )
    colour_grad = lax.dot_general(
        weight_cot,
        weights,
        (((1,), (1,)), ((), ())),
        precision=precise,
        preferred_element_type=jnp.float32,
    )
    mean_x, mean_y, conic_a, conic_b, conic_c, opacity = (
        params[0],
        params[1],
        params[2],
        params[3],
        params[4],
        params[5],
    )
    moment_zero = moments[0]
    along_x = moments[1] - mean_x * moment_zero
    along_y = moments[2] - mean_y * moment_zero
    square_x = moments[3] - 2.0 * mean_x * moments[1] + mean_x * mean_x * moment_zero
    cross_xy = (
        moments[4] - mean_x * moments[2] - mean_y * moments[1] + mean_x * mean_y * moment_zero
    )
    square_y = moments[5] - 2.0 * mean_y * moments[2] + mean_y * mean_y * moment_zero
    grad_rows = jnp.stack(
        [
            conic_a * along_x + conic_b * along_y,
            conic_b * along_x + conic_c * along_y,
            -0.5 * square_x,
            -cross_xy,
            -0.5 * square_y,
            moment_zero / opacity,
        ]
    )
    return jnp.concatenate([grad_rows, colour_grad], axis=0)


def backward_task(params, cotangent, pix_x, pix_y, lower_tri, upper_tri):
    alphas, log_trans = splat(params, pix_x, pix_y)
    transmit = jnp.exp(
        jnp.dot(lower_tri, log_trans, precision=precise, preferred_element_type=jnp.float32)
    )
    weights = alphas * transmit
    weight_cot = cotangent[:3]
    shaded = lax.dot_general(
        params[6:9],
        weight_cot,
        (((0,), (0,)), ((), ())),
        precision=precise,
        preferred_element_type=jnp.float32,
    )
    later_sum = jnp.dot(
        upper_tri, weights * shaded, precision=precise, preferred_element_type=jnp.float32
    )
    dalpha = transmit * shaded - (later_sum + cotangent[3][None, :]) / (1.0 - alphas)
    return gradient_rows(params, pix_x, pix_y, dalpha * alphas, weights, weight_cot)


def composite(partials, live_mask, target_tile, valid_slot):
    slot_total = partials.shape[0]
    running = jnp.zeros(partials.shape[2:], jnp.float32)
    transmit = []
    for slot_index in range(slot_total):
        transmit.append(jnp.exp(running))
        running = running + partials[slot_index, 3]
    transmit = jnp.stack(transmit)
    shaded = transmit[:, None, :] * partials[:, :3]
    rendered = jnp.sum(shaded, axis=0) * live_mask
    residual = (rendered - target_tile) * live_mask
    behind = []
    running_sum = jnp.zeros_like(rendered)
    for slot_index in range(slot_total - 1, -1, -1):
        behind.insert(0, running_sum)
        running_sum = running_sum + shaded[slot_index]
    behind = jnp.stack(behind)
    valid_weight = valid_slot.astype(jnp.float32)
    weight_cot = transmit[:, None, :] * residual[None] * valid_weight[:, None, None]
    after_cot = jnp.sum(residual[None] * behind, axis=1) * valid_weight[:, None]
    return (rendered, jnp.concatenate([weight_cot, after_cot[:, None, :]], axis=1))


def shards(gaussians, seg_count, seg_block, ray_count, camera_shift, target):
    cell_count = lax.axis_size("cell")
    cell_index = lax.axis_index("cell")
    per_block = gaussians.shape[0]
    pixels = target.shape[3]
    lower_tri, upper_tri = triangles(gaussians.shape[2])
    blocks = seg_block[0, 0]
    slot_count = blocks.shape[0]
    own_count = seg_count[0, 0]
    home_cell = blocks // per_block
    local_block = blocks % per_block
    offset = (home_cell - cell_index + REACH) % cell_count - REACH
    pix_x, pix_y = pixel_frame(camera_shift[0], pixels)
    valid_slot = jnp.arange(slot_count) < own_count

    def run_forward(params):
        return forward_task(params, pix_x, pix_y, lower_tri)

    def run_backward(bundle):
        return backward_task(bundle[0], bundle[1], pix_x, pix_y, lower_tri, upper_tri)

    near_list = []
    for shift_by in range(-REACH, REACH + 1):
        if shift_by == 0:
            near_list.append(gaussians)
        else:
            near_list.append(shifted(gaussians, "cell", -shift_by))
    near_stack = jnp.concatenate(near_list, axis=0)
    pick_index = (offset + REACH) * per_block + local_block
    own_params = jnp.take(near_stack, pick_index, axis=0)
    partials = lax.map(run_forward, own_params)
    partials = jnp.where(valid_slot[:, None, None], partials, 0.0)
    live_mask = (jnp.arange(pixels) < ray_count[0, 0]).astype(jnp.float32)
    rendered, cotangent = composite(partials, live_mask, target[0, 0], valid_slot)
    own_grads = lax.map(run_backward, (own_params, cotangent))
    spot_count = (2 * REACH + 1) * per_block
    onehot = (pick_index[:, None] == jnp.arange(spot_count)[None, :]).astype(jnp.float32)
    spread = jnp.einsum("sk,sjg->kjg", onehot, own_grads, precision=precise)
    spread = spread.reshape((2 * REACH + 1, per_block) + gaussians.shape[1:])
    block_grads = spread[REACH]
    for shift_by in range(-REACH, REACH + 1):
        if shift_by != 0:
            block_grads = block_grads + shifted(spread[shift_by + REACH], "cell", shift_by)
    gauss_grad = lax.psum(block_grads, "view")
    return (rendered[None, None], gauss_grad)


def solution(mesh):
    placed = (
        P("cell", None, None),
        P("view", "cell"),
        P("view", "cell", None),
        P("view", "cell"),
        P("view", None),
        P("view", "cell", None, None),
    )
    return jax.shard_map(
        shards,
        mesh=mesh,
        in_specs=placed,
        out_specs=(P("view", "cell", None, None), P("cell", None, None)),
        check_vma=False,
    )
```

profile of v0, /device:TPU:1, one launch (start us, length us, event | category | flops | bytes accessed | tf_op | source)
XLA Modules:
  0.0 182.8 jit_solution(16609155894614825310)
XLA Ops:
  8.2 2.5 %collective-permute-start = (f32[16,9,256]{2,1,0:T(8,128)S(1)}, f32[16,9,256]{2,1,0:T(8,128)S(1)}, u32[]{:S(2)}, u32[]{:S(2)}) collective-permute-start(f32[16,9,256]{2,1,0:T(8,128)S(1)} %copy.22), channel_id=1, source_target_pairs={{248,0},{252,4},{0,8},{4,12},{8,16},{12,20},{16,24},{20,28},{24,32... | collective-permute-start | bytes 442376 | tf_op jit(solution)/shard_map/ppermute | solution.py:16
  10.7 2.5 %collective-permute-start.1 = (f32[16,9,256]{2,1,0:T(8,128)S(1)}, f32[16,9,256]{2,1,0:T(8,128)S(1)}, u32[]{:S(2)}, u32[]{:S(2)}) collective-permute-start(f32[16,9,256]{2,1,0:T(8,128)S(1)} %copy.22), channel_id=1, source_target_pairs={{252,0},{0,4},{4,8},{8,12},{12,16},{16,20},{20,24},{24,28},{28,32}... | collective-permute-start | bytes 442376 | tf_op jit(solution)/shard_map/ppermute | solution.py:16
  13.2 4.8 %collective-permute-start.3 = (f32[16,9,256]{2,1,0:T(8,128)S(1)}, f32[16,9,256]{2,1,0:T(8,128)S(1)}, u32[]{:S(2)}, u32[]{:S(2)}) collective-permute-start(f32[16,9,256]{2,1,0:T(8,128)S(1)} %copy.22), channel_id=1, source_target_pairs={{8,0},{12,4},{16,8},{20,12},{24,16},{28,20},{32,24},{36,28},{40,32... | collective-permute-start | bytes 442376 | tf_op jit(solution)/shard_map/ppermute | solution.py:16
  27.8 1.9 %gather_fusion = f32[3,9,256]{2,1,0:T(8,128)S(1)} fusion(f32[80,9,256]{2,1,0:T(8,128)} %constant_dynamic-update-slice_fusion, s32[1024]{0:T(1024)S(1)} %pad_clamp_fusion), kind=kCustom, calls=%fused_computation | custom fusion | bytes 55308 | tf_op jit(solution)/shard_map/jit(_take)/gather | solution.py:174
  29.7 30.8 %while.26 = (s32[]{:T(128)}, f32[3,4,2304]{2,1,0:T(4,128)S(1)}, f32[3,9,256]{2,1,0:T(8,128)S(1)}, f32[]{:T(128)}, f32[]{:T(128)}) while((s32[]{:T(128)}, f32[3,4,2304]{2,1,0:T(4,128)S(1)}, f32[3,9,256]{2,1,0:T(8,128)S(1)}, f32[]{:T(128)}, f32[]{:T(128)}) %tuple.102), condition=%wide.region_2.3_spmd.clone.clone, body=%wide.region_0.2_spmd.clone.sunk.clone | while | flops 1856945664 | bytes 4940977 | solution.py:175
  30.9 4.6 %fusion.187 = f32[256,2304]{0,1:T(8,128)S(1)} fusion(f32[256]{0:T(256)S(1)} %bitcast.284, f32[256]{0:T(256)S(1)} %bitcast.276, f32[2304]{0:T(1024)S(1)} %get-tuple-element.382, f32[256]{0:T(256)S(1)} %bitcast.278, f32[256]{0:T(256)S(1)} %bitcast.280, f32[2304]{0:T(1024)S(1)} %get-tuple-element.385, f32[256]{0:T(256)S(1)} %bitcast.282, ...), kind=kOutput, calls=%fused_computation.19.clone.1.clone | convolution fusion | flops 1827405824 | bytes 2383872 | tf_op jit(solution)/shard_map/while/body/eval_jaxpr/dot_general | solution.py:47
  35.6 2.0 %fusion.188 = f32[3,2304]{1,0:T(4,128)S(1)} fusion(f32[256,2304]{0,1:T(8,128)S(1)} %fusion.187, f32[3,9,256]{2,1,0:T(8,128)S(1)} %get-tuple-element.451, s32[]{:T(128)} %get-tuple-element.444, s32[]{:T(128)S(6)} %add.582), kind=kOutput, calls=%fused_computation.48.clone.1.clone | convolution fusion | flops 21233664 | bytes 2391048 | tf_op jit(solution)/shard_map/while/body/eval_jaxpr/dot_general | solution.py:49
  37.6 2.3 %fusion.186 = f32[2304]{0:T(1024)S(1)} fusion(f32[256]{0:T(256)S(1)} %bitcast.285, f32[256]{0:T(256)S(1)} %bitcast.277, f32[2304]{0:T(1024)S(1)} %get-tuple-element.382, f32[256]{0:T(256)S(1)} %bitcast.279, f32[256]{0:T(256)S(1)} %bitcast.281, f32[2304]{0:T(1024)S(1)} %get-tuple-element.385, f32[256]{0:T(256)S(1)} %bitcast.283, f32[256]{0:T(256)S(1)} %bitcast.275), kind=kLoop, calls=%fused_computation.26.clone.1.clone | loop fusion | flops 8255232 | bytes 33792 | tf_op jit(solution)/shard_map/while/body/eval_jaxpr/reduce_sum | solution.py:50
  41.2 4.6 %fusion.187 = f32[256,2304]{0,1:T(8,128)S(1)} fusion(f32[256]{0:T(256)S(1)} %bitcast.284, f32[256]{0:T(256)S(1)} %bitcast.276, f32[2304]{0:T(1024)S(1)} %get-tuple-element.382, f32[256]{0:T(256)S(1)} %bitcast.278, f32[256]{0:T(256)S(1)} %bitcast.280, f32[2304]{0:T(1024)S(1)} %get-tuple-element.385, f32[256]{0:T(256)S(1)} %bitcast.282, ...), kind=kOutput, calls=%fused_computation.19.clone.1.clone | convolution fusion | flops 1827405824 | bytes 2383872 | tf_op jit(solution)/shard_map/while/body/eval_jaxpr/dot_general | solution.py:47
  45.8 2.0 %fusion.188 = f32[3,2304]{1,0:T(4,128)S(1)} fusion(f32[256,2304]{0,1:T(8,128)S(1)} %fusion.187, f32[3,9,256]{2,1,0:T(8,128)S(1)} %get-tuple-element.451, s32[]{:T(128)} %get-tuple-element.444, s32[]{:T(128)S(6)} %add.582), kind=kOutput, calls=%fused_computation.48.clone.1.clone | convolution fusion | flops 21233664 | bytes 2391048 | tf_op jit(solution)/shard_map/while/body/eval_jaxpr/dot_general | solution.py:49
  47.9 2.3 %fusion.186 = f32[2304]{0:T(1024)S(1)} fusion(f32[256]{0:T(256)S(1)} %bitcast.285, f32[256]{0:T(256)S(1)} %bitcast.277, f32[2304]{0:T(1024)S(1)} %get-tuple-element.382, f32[256]{0:T(256)S(1)} %bitcast.279, f32[256]{0:T(256)S(1)} %bitcast.281, f32[2304]{0:T(1024)S(1)} %get-tuple-element.385, f32[256]{0:T(256)S(1)} %bitcast.283, f32[256]{0:T(256)S(1)} %bitcast.275), kind=kLoop, calls=%fused_computation.26.clone.1.clone | loop fusion | flops 8255232 | bytes 33792 | tf_op jit(solution)/shard_map/while/body/eval_jaxpr/reduce_sum | solution.py:50
  51.5 4.6 %fusion.187 = f32[256,2304]{0,1:T(8,128)S(1)} fusion(f32[256]{0:T(256)S(1)} %bitcast.284, f32[256]{0:T(256)S(1)} %bitcast.276, f32[2304]{0:T(1024)S(1)} %get-tuple-element.382, f32[256]{0:T(256)S(1)} %bitcast.278, f32[256]{0:T(256)S(1)} %bitcast.280, f32[2304]{0:T(1024)S(1)} %get-tuple-element.385, f32[256]{0:T(256)S(1)} %bitcast.282, ...), kind=kOutput, calls=%fused_computation.19.clone.1.clone | convolution fusion | flops 1827405824 | bytes 2383872 | tf_op jit(solution)/shard_map/while/body/eval_jaxpr/dot_general | solution.py:47
  56.1 2.0 %fusion.188 = f32[3,2304]{1,0:T(4,128)S(1)} fusion(f32[256,2304]{0,1:T(8,128)S(1)} %fusion.187, f32[3,9,256]{2,1,0:T(8,128)S(1)} %get-tuple-element.451, s32[]{:T(128)} %get-tuple-element.444, s32[]{:T(128)S(6)} %add.582), kind=kOutput, calls=%fused_computation.48.clone.1.clone | convolution fusion | flops 21233664 | bytes 2391048 | tf_op jit(solution)/shard_map/while/body/eval_jaxpr/dot_general | solution.py:49
  58.1 2.3 %fusion.186 = f32[2304]{0:T(1024)S(1)} fusion(f32[256]{0:T(256)S(1)} %bitcast.285, f32[256]{0:T(256)S(1)} %bitcast.277, f32[2304]{0:T(1024)S(1)} %get-tuple-element.382, f32[256]{0:T(256)S(1)} %bitcast.279, f32[256]{0:T(256)S(1)} %bitcast.281, f32[2304]{0:T(1024)S(1)} %get-tuple-element.385, f32[256]{0:T(256)S(1)} %bitcast.283, f32[256]{0:T(256)S(1)} %bitcast.275), kind=kLoop, calls=%fused_computation.26.clone.1.clone | loop fusion | flops 8255232 | bytes 33792 | tf_op jit(solution)/shard_map/while/body/eval_jaxpr/reduce_sum | solution.py:50
  61.1 57.0 %while.27 = (s32[]{:T(128)}, f32[3,9,256]{2,0,1:T(4,128)S(1)}, f32[3,9,256]{2,1,0:T(8,128)S(1)}, f32[3,4,2304]{2,1,0:T(4,128)S(1)}, f32[]{:T(128)}, /*index=5*/f32[]{:T(128)}) while((s32[]{:T(128)}, f32[3,9,256]{2,0,1:T(4,128)S(1)}, f32[3,9,256]{2,1,0:T(8,128)S(1)}, f32[3,4,2304]{2,1,0:T(4,128)S(1)}, ...), condition=%wide.region_6.7_spmd.clone.clone.clone, body=%wide.region_5.6_spmd.clone.clone.sunk.clone | while | flops 3743404544 | bytes 35934480 | solution.py:179
  62.5 4.9 %fusion.201 = f32[256,2304]{0,1:T(8,128)} fusion(f32[256]{0:T(256)S(1)} %bitcast.265, f32[256]{0:T(256)S(1)} %bitcast.256, f32[2304]{0:T(1024)S(1)} %get-tuple-element.410, f32[256]{0:T(256)S(1)} %bitcast.271, f32[256]{0:T(256)S(1)} %bitcast.259, f32[2304]{0:T(1024)S(1)} %get-tuple-element.409, f32[256]{0:T(256)S(1)} %bitcast.268, ...), kind=kOutput, calls=%fused_computation.66.clone.1.clone | convolution fusion | flops 1819738112 | bytes 2383872 | tf_op jit(solution)/shard_map/while/body/eval_jaxpr/dot_general | solution.py:104
  67.5 2.1 %fusion.200 = f32[256,2304]{0,1:T(8,128)S(1)} fusion(f32[3,4,2304]{2,1,0:T(4,128)S(1)} %get-tuple-element.469, s32[]{:T(128)} %get-tuple-element.460, f32[3,9,256]{2,1,0:T(8,128)S(1)} %get-tuple-element.468, s32[]{:T(128)S(6)} %add.601), kind=kOutput, calls=%fused_computation.88.clone.1.clone | convolution fusion | flops 21233664 | bytes 2401284 | tf_op jit(solution)/shard_map/while/body/eval_jaxpr/dot_general | solution.py:108
  69.6 4.4 %fusion.202 = f32[256,2304]{0,1:T(8,128)S(1)} fusion(f32[256,2304]{0,1:T(8,128)S(1)} %fusion.200, f32[256,2304]{0,1:T(8,128)S(1)} %copy-done.1, f32[2304]{0:T(1024)S(1)} %dynamic-slice_reduce_fusion.3, f32[256]{0:T(256)S(1)} %bitcast.266, f32[256]{0:T(256)S(1)} %bitcast.257, f32[2304]{0:T(1024)S(1)} %get-tuple-element.410, ...), kind=kOutput, calls=%fused_computation.70.clone.1.clone | convolution fusion | flops 1830944768 | bytes 7111680 | tf_op jit(solution)/shard_map/while/body/eval_jaxpr/dot_general | solution.py:115
  77.7 2.2 %fusion.205 = f32[3,256]{1,0:T(4,128)S(1)} fusion(f32[256,2304]{0,1:T(8,128)S(1)} %copy-done.2, f32[256]{0:T(256)S(1)} %bitcast.267, f32[256]{0:T(256)S(1)} %bitcast.258, f32[2304]{0:T(1024)S(1)} %get-tuple-element.410, f32[256]{0:T(256)S(1)} %bitcast.273, f32[256]{0:T(256)S(1)} %bitcast.261, f32[2304]{0:T(1024)S(1)} %get-tuple-element.409, ...), kind=kOutput, calls=%fused_computation.80.clone.1.clone | convolution fusion | flops 28901376 | bytes 2429956 | tf_op jit(solution)/shard_map/while/body/eval_jaxpr/dot_general | solution.py:65
  81.4 4.9 %fusion.201 = f32[256,2304]{0,1:T(8,128)} fusion(f32[256]{0:T(256)S(1)} %bitcast.265, f32[256]{0:T(256)S(1)} %bitcast.256, f32[2304]{0:T(1024)S(1)} %get-tuple-element.410, f32[256]{0:T(256)S(1)} %bitcast.271, f32[256]{0:T(256)S(1)} %bitcast.259, f32[2304]{0:T(1024)S(1)} %get-tuple-element.409, f32[256]{0:T(256)S(1)} %bitcast.268, ...), kind=kOutput, calls=%fused_computation.66.clone.1.clone | convolution fusion | flops 1819738112 | bytes 2383872 | tf_op jit(solution)/shard_map/while/body/eval_jaxpr/dot_general | solution.py:104
  86.3 2.1 %fusion.200 = f32[256,2304]{0,1:T(8,128)S(1)} fusion(f32[3,4,2304]{2,1,0:T(4,128)S(1)} %get-tuple-element.469, s32[]{:T(128)} %get-tuple-element.460, f32[3,9,256]{2,1,0:T(8,128)S(1)} %get-tuple-element.468, s32[]{:T(128)S(6)} %add.601), kind=kOutput, calls=%fused_computation.88.clone.1.clone | convolution fusion | flops 21233664 | bytes 2401284 | tf_op jit(solution)/shard_map/while/body/eval_jaxpr/dot_general | solution.py:108
  88.5 4.4 %fusion.202 = f32[256,2304]{0,1:T(8,128)S(1)} fusion(f32[256,2304]{0,1:T(8,128)S(1)} %fusion.200, f32[256,2304]{0,1:T(8,128)S(1)} %copy-done.1, f32[2304]{0:T(1024)S(1)} %dynamic-slice_reduce_fusion.3, f32[256]{0:T(256)S(1)} %bitcast.266, f32[256]{0:T(256)S(1)} %bitcast.257, f32[2304]{0:T(1024)S(1)} %get-tuple-element.410, ...), kind=kOutput, calls=%fused_computation.70.clone.1.clone | convolution fusion | flops 1830944768 | bytes 7111680 | tf_op jit(solution)/shard_map/while/body/eval_jaxpr/dot_general | solution.py:115
  96.6 2.2 %fusion.205 = f32[3,256]{1,0:T(4,128)S(1)} fusion(f32[256,2304]{0,1:T(8,128)S(1)} %copy-done.2, f32[256]{0:T(256)S(1)} %bitcast.267, f32[256]{0:T(256)S(1)} %bitcast.258, f32[2304]{0:T(1024)S(1)} %get-tuple-element.410, f32[256]{0:T(256)S(1)} %bitcast.273, f32[256]{0:T(256)S(1)} %bitcast.261, f32[2304]{0:T(1024)S(1)} %get-tuple-element.409, ...), kind=kOutput, calls=%fused_computation.80.clone.1.clone | convolution fusion | flops 28901376 | bytes 2429956 | tf_op jit(solution)/shard_map/while/body/eval_jaxpr/dot_general | solution.py:65
  100.3 4.9 %fusion.201 = f32[256,2304]{0,1:T(8,128)} fusion(f32[256]{0:T(256)S(1)} %bitcast.265, f32[256]{0:T(256)S(1)} %bitcast.256, f32[2304]{0:T(1024)S(1)} %get-tuple-element.410, f32[256]{0:T(256)S(1)} %bitcast.271, f32[256]{0:T(256)S(1)} %bitcast.259, f32[2304]{0:T(1024)S(1)} %get-tuple-element.409, f32[256]{0:T(256)S(1)} %bitcast.268, ...), kind=kOutput, calls=%fused_computation.66.clone.1.clone | convolution fusion | flops 1819738112 | bytes 2383872 | tf_op jit(solution)/shard_map/while/body/eval_jaxpr/dot_general | solution.py:104
  105.2 2.1 %fusion.200 = f32[256,2304]{0,1:T(8,128)S(1)} fusion(f32[3,4,2304]{2,1,0:T(4,128)S(1)} %get-tuple-element.469, s32[]{:T(128)} %get-tuple-element.460, f32[3,9,256]{2,1,0:T(8,128)S(1)} %get-tuple-element.468, s32[]{:T(128)S(6)} %add.601), kind=kOutput, calls=%fused_computation.88.clone.1.clone | convolution fusion | flops 21233664 | bytes 2401284 | tf_op jit(solution)/shard_map/while/body/eval_jaxpr/dot_general | solution.py:108
  107.4 4.4 %fusion.202 = f32[256,2304]{0,1:T(8,128)S(1)} fusion(f32[256,2304]{0,1:T(8,128)S(1)} %fusion.200, f32[256,2304]{0,1:T(8,128)S(1)} %copy-done.1, f32[2304]{0:T(1024)S(1)} %dynamic-slice_reduce_fusion.3, f32[256]{0:T(256)S(1)} %bitcast.266, f32[256]{0:T(256)S(1)} %bitcast.257, f32[2304]{0:T(1024)S(1)} %get-tuple-element.410, ...), kind=kOutput, calls=%fused_computation.70.clone.1.clone | convolution fusion | flops 1830944768 | bytes 7111680 | tf_op jit(solution)/shard_map/while/body/eval_jaxpr/dot_general | solution.py:115
  115.5 2.2 %fusion.205 = f32[3,256]{1,0:T(4,128)S(1)} fusion(f32[256,2304]{0,1:T(8,128)S(1)} %copy-done.2, f32[256]{0:T(256)S(1)} %bitcast.267, f32[256]{0:T(256)S(1)} %bitcast.258, f32[2304]{0:T(1024)S(1)} %get-tuple-element.410, f32[256]{0:T(256)S(1)} %bitcast.273, f32[256]{0:T(256)S(1)} %bitcast.261, f32[2304]{0:T(1024)S(1)} %get-tuple-element.409, ...), kind=kOutput, calls=%fused_computation.80.clone.1.clone | convolution fusion | flops 28901376 | bytes 2429956 | tf_op jit(solution)/shard_map/while/body/eval_jaxpr/dot_general | solution.py:65
  118.7 2.9 %collective-permute-start.4 = (f32[16,9,256]{2,0,1:T(8,128)S(1)}, f32[16,9,256]{2,0,1:T(8,128)S(1)}, u32[]{:S(2)}, u32[]{:S(2)}) collective-permute-start(f32[16,9,256]{2,0,1:T(8,128)S(1)} %get-tuple-element.244), channel_id=1, source_target_pairs={{8,0},{12,4},{16,8},{20,12},{24,16},{28,20},{32,24},{36,28},{40,32... | collective-permute-start | bytes 442376 | tf_op jit(solution)/shard_map/ppermute | solution.py:16
  121.7 3.2 %collective-permute-start.5 = (f32[16,9,256]{2,0,1:T(8,128)S(1)}, f32[16,9,256]{2,0,1:T(8,128)S(1)}, u32[]{:S(2)}, u32[]{:S(2)}) collective-permute-start(f32[16,9,256]{2,0,1:T(8,128)S(1)} %get-tuple-element.247), channel_id=1, source_target_pairs={{4,0},{8,4},{12,8},{16,12},{20,16},{24,20},{28,24},{32,28},{36,32}... | collective-permute-start | bytes 442376 | tf_op jit(solution)/shard_map/ppermute | solution.py:16
  124.8 3.4 %collective-permute-done.5 = f32[16,9,256]{2,0,1:T(8,128)S(1)} collective-permute-done((f32[16,9,256]{2,0,1:T(8,128)S(1)}, f32[16,9,256]{2,0,1:T(8,128)S(1)}, u32[]{:S(2)}, u32[]{:S(2)}) %collective-permute-start.5) | collective-permute-done | bytes 147488 | tf_op jit(solution)/shard_map/ppermute | solution.py:16
  128.2 7.0 %collective-permute-done.7 = f32[16,9,256]{2,0,1:T(8,128)S(1)} collective-permute-done((f32[16,9,256]{2,0,1:T(8,128)S(1)}, f32[16,9,256]{2,0,1:T(8,128)S(1)}, u32[]{:S(2)}, u32[]{:S(2)}) %collective-permute-start.7) | collective-permute-done | bytes 147488 | tf_op jit(solution)/shard_map/ppermute | solution.py:16
  136.6 37.8 %all-reduce.2.cloned.1.call-done = f32[16,9,256]{2,0,1:T(8,128)} async-done(((f32[16,9,256]{2,0,1:T(8,128)}), f32[16,9,256]{2,0,1:T(8,128)}) %all-reduce.2.cloned.1.call-update) | async-done | bytes 147472 | tf_op jit(solution)/shard_map/psum | solution.py:188
  (113 shorter events, 32.7 us)
Async XLA Ops:
  7.2 167.2 %all-reduce.2.cloned.1.call-start = ((), (), s32[]{:S(2)}) async-start(), calls=%async_computation | async-start | bytes 294912 | tf_op jit(solution)/shard_map/psum | solution.py:188
  8.2 14.9 %collective-permute-start = (f32[16,9,256]{2,1,0:T(8,128)S(1)}, f32[16,9,256]{2,1,0:T(8,128)S(1)}, u32[]{:S(2)}, u32[]{:S(2)}) collective-permute-start(f32[16,9,256]{2,1,0:T(8,128)S(1)} %copy.22), channel_id=1, source_target_pairs={{248,0},{252,4},{0,8},{4,12},{8,16},{12,20},{16,24},{20,28},{24,32... | collective-permute-start | bytes 442376 | tf_op jit(solution)/shard_map/ppermute | solution.py:16
  10.7 13.1 %collective-permute-start.1 = (f32[16,9,256]{2,1,0:T(8,128)S(1)}, f32[16,9,256]{2,1,0:T(8,128)S(1)}, u32[]{:S(2)}, u32[]{:S(2)}) collective-permute-start(f32[16,9,256]{2,1,0:T(8,128)S(1)} %copy.22), channel_id=1, source_target_pairs={{252,0},{0,4},{4,8},{8,12},{12,16},{16,20},{20,24},{24,28},{28,32}... | collective-permute-start | bytes 442376 | tf_op jit(solution)/shard_map/ppermute | solution.py:16
  13.2 13.1 %collective-permute-start.2 = (f32[16,9,256]{2,1,0:T(8,128)S(1)}, f32[16,9,256]{2,1,0:T(8,128)S(1)}, u32[]{:S(2)}, u32[]{:S(2)}) collective-permute-start(f32[16,9,256]{2,1,0:T(8,128)S(1)} %copy.22), channel_id=1, source_target_pairs={{4,0},{8,4},{12,8},{16,12},{20,16},{24,20},{28,24},{32,28},{36,32}... | collective-permute-start | bytes 442376 | tf_op jit(solution)/shard_map/ppermute | solution.py:16
  13.2 13.8 %collective-permute-start.3 = (f32[16,9,256]{2,1,0:T(8,128)S(1)}, f32[16,9,256]{2,1,0:T(8,128)S(1)}, u32[]{:S(2)}, u32[]{:S(2)}) collective-permute-start(f32[16,9,256]{2,1,0:T(8,128)S(1)} %copy.22), channel_id=1, source_target_pairs={{8,0},{12,4},{16,8},{20,12},{24,16},{28,20},{32,24},{36,28},{40,32... | collective-permute-start | bytes 442376 | tf_op jit(solution)/shard_map/ppermute | solution.py:16
  29.7 31.1 %copy-start = (f32[1,1,3,2304]{3,1,2,0:T(1,128)S(1)}, f32[1,1,3,2304]{3,1,2,0:T(1,128)}, u32[]{:S(2)}) copy-start(f32[1,1,3,2304]{3,1,2,0:T(1,128)} %param.15) | copy-start | bytes 82948
  67.5 2.2 %copy-start.1 = (f32[256,2304]{0,1:T(8,128)S(1)}, f32[256,2304]{0,1:T(8,128)}, u32[]{:S(2)}) copy-start(f32[256,2304]{0,1:T(8,128)} %fusion.201) | copy-start | bytes 7077892 | tf_op jit(solution)/shard_map/while
  76.1 1.7 copy-start.2
  86.3 2.2 %copy-start.1 = (f32[256,2304]{0,1:T(8,128)S(1)}, f32[256,2304]{0,1:T(8,128)}, u32[]{:S(2)}) copy-start(f32[256,2304]{0,1:T(8,128)} %fusion.201) | copy-start | bytes 7077892 | tf_op jit(solution)/shard_map/while
  94.9 1.7 copy-start.2
  105.2 2.2 %copy-start.1 = (f32[256,2304]{0,1:T(8,128)S(1)}, f32[256,2304]{0,1:T(8,128)}, u32[]{:S(2)}) copy-start(f32[256,2304]{0,1:T(8,128)} %fusion.201) | copy-start | bytes 7077892 | tf_op jit(solution)/shard_map/while
  113.8 1.7 copy-start.2
  118.7 6.1 %collective-permute-start.4 = (f32[16,9,256]{2,0,1:T(8,128)S(1)}, f32[16,9,256]{2,0,1:T(8,128)S(1)}, u32[]{:S(2)}, u32[]{:S(2)}) collective-permute-start(f32[16,9,256]{2,0,1:T(8,128)S(1)} %get-tuple-element.244), channel_id=1, source_target_pairs={{8,0},{12,4},{16,8},{20,12},{24,16},{28,20},{32,24},{36,28},{40,32... | collective-permute-start | bytes 442376 | tf_op jit(solution)/shard_map/ppermute | solution.py:16
  121.7 6.5 %collective-permute-start.5 = (f32[16,9,256]{2,0,1:T(8,128)S(1)}, f32[16,9,256]{2,0,1:T(8,128)S(1)}, u32[]{:S(2)}, u32[]{:S(2)}) collective-permute-start(f32[16,9,256]{2,0,1:T(8,128)S(1)} %get-tuple-element.247), channel_id=1, source_target_pairs={{4,0},{8,4},{12,8},{16,12},{20,16},{24,20},{28,24},{32,28},{36,32}... | collective-permute-start | bytes 442376 | tf_op jit(solution)/shard_map/ppermute | solution.py:16
  124.8 3.4 %collective-permute-start.6 = (f32[16,9,256]{2,0,1:T(8,128)S(1)}, f32[16,9,256]{2,0,1:T(8,128)S(1)}, u32[]{:S(2)}, u32[]{:S(2)}) collective-permute-start(f32[16,9,256]{2,0,1:T(8,128)S(1)} %get-tuple-element.246), channel_id=1, source_target_pairs={{252,0},{0,4},{4,8},{8,12},{12,16},{16,20},{20,24},{24,28},{28,32}... | collective-permute-start | bytes 442376 | tf_op jit(solution)/shard_map/ppermute | solution.py:16
  124.8 10.4 %collective-permute-start.7 = (f32[16,9,256]{2,0,1:T(8,128)S(1)}, f32[16,9,256]{2,0,1:T(8,128)S(1)}, u32[]{:S(2)}, u32[]{:S(2)}) collective-permute-start(f32[16,9,256]{2,0,1:T(8,128)S(1)} %get-tuple-element.245), channel_id=1, source_target_pairs={{248,0},{252,4},{0,8},{4,12},{8,16},{12,20},{16,24},{20,28},{24,32... | collective-permute-start | bytes 442376 | tf_op jit(solution)/shard_map/ppermute | solution.py:16
Sparse Core Ops, SparseCore 0:
  136.0 38.2 all-reduce.1
where the time goes:
time: 184 us; the launch traced here: 183 us
  matrix products  64.5 us (35%)
  waiting for transfers between devices  49.2 us (27%)
  other arithmetic  23.4 us (13%)
  starting transfers between devices  15.9 us (9%)
  between operations  15.5 us (8%)
  local copies, waits for them, and re-layouts  13.4 us (7%)
    psum x1, waiting for transfers between devices, shards(): gauss_grad = lax.psum(block_grads, 'view')  37.8 us
    ppermute x8, starting transfers between devices, shifted(): return lax.ppermute(block, axis, route)  15.9 us
    dot_general x3, matrix products, backward_task(): jnp.dot(lower_tri, log_trans, precision=precise, preferred_element_type=j...  14.8 us
    dot_general x3, matrix products, forward_task(): jnp.dot(lower_tri, log_trans, precision=precise, preferred_element_type=j...  13.9 us
    dot_general x3, matrix products, backward_task(): jnp.dot(upper_tri, weights * shaded, precision=precise, preferred_element...  13.2 us
    ppermute x8, waiting for transfers between devices, shifted(): return lax.ppermute(block, axis, route)  11.3 us
    sub x6, other arithmetic, pixel_frame(): pix_y = (pixel_ids // TILE).astype(jnp.float32) - centre - shift[1]  7.23 us
    reduce_sum x3, other arithmetic, forward_task(): totals = jnp.sum(log_trans, axis=0)  6.89 us
  transfers between devices with their start and end apart: 9, of which 4 were waited for; matrix products, arithmetic and copies ran while one was open for 4% of the time, Pallas kernels for 0%

commit v1 on v0

v1 whole, which is shorter than its diff:
```python
import math
import jax
import jax.numpy as jnp
import numpy as np
from jax import lax
from jax.experimental import pallas as pl
from jax.experimental.pallas import tpu as pltpu
from jax.sharding import PartitionSpec as P

TILE = 48
PIX = TILE * TILE
GB = 256
SEGS = 4
SEG_MAX = 3
GRP = 384
GROUPS = PIX // GRP
LANES = GRP // 128
CHAINS = 8
STEPS = GB // CHAINS
LOG2E = math.log2(math.e)
F32 = jnp.float32
BF16 = jnp.bfloat16


def as_bf16(x):
    return x.astype(BF16)


def pixel_features():
    ids = np.arange(PIX)
    x = (ids % TILE).astype(np.float64) - (TILE - 1) / 2.0
    y = (ids // TILE).astype(np.float64) - (TILE - 1) / 2.0
    zero = np.zeros_like(x)

    def split(v):
        high = v.astype(jnp.bfloat16).astype(np.float64)
        return high, v - high

    xx, xy, yy = split(x * x), split(x * y), split(y * y)
    first = np.stack([np.ones_like(x), x, y, xx[0], xy[0], yy[0], zero, zero])
    second = np.stack([zero, zero, zero, xx[1], xy[1], yy[1], zero, zero])
    feats = np.concatenate([first] * 3 + [second] * 3)
    moments = np.concatenate([first, second])
    return feats.astype(jnp.bfloat16), moments.astype(jnp.bfloat16)


def pieces(x):
    one = as_bf16(x).astype(F32)
    rest = x - one
    two = as_bf16(rest).astype(F32)
    return one, two, rest - two


def dot(a, b, dims):
    return lax.dot_general(a, b, (dims, ((), ())), preferred_element_type=F32)


def down(x, n, fill):
    rows = lax.broadcasted_iota(jnp.int32, x.shape, 0)
    return jnp.where(rows >= n, pltpu.roll(x, n, 0), fill)


def up(x, n, fill):
    rows = lax.broadcasted_iota(jnp.int32, x.shape, 0)
    return jnp.where(rows < CHAINS - n, pltpu.roll(x, CHAINS - n, 0), fill)


def row_of(x, i):
    return jnp.broadcast_to(x[i : i + 1], x.shape)


def total_rows(x):
    return jnp.sum(x, axis=0, keepdims=True)


def pick_kernel(where_ref, own_meta, mate_meta, own_ref, prev_ref, next_ref, out_ref):
    core = where_ref[0]
    chip = where_ref[1]
    chips = where_ref[2]
    per_block = own_ref.shape[0]
    even_count = jnp.where(core == 0, own_meta[0], mate_meta[0])
    for q in range(SEGS):
        tile = (q >= even_count).astype(jnp.int32)
        slot = q - tile * even_count
        slot = jnp.clip(slot, 0, SEG_MAX - 1)
        block = jnp.where(tile == core, own_meta[1 + slot], mate_meta[1 + slot])
        home = block // per_block
        local = block % per_block
        ahead = (home // 2 - chip + chips) % chips
        held = home % 2 == core
        out_ref[q] = jnp.zeros(out_ref.shape[1:], F32)

        @pl.when(held & (ahead == 0))
        def _():
            out_ref[q, 0:9] = own_ref[local]

        @pl.when(held & (ahead == 1))
        def _():
            out_ref[q, 0:9] = next_ref[local]

        @pl.when(held & (ahead == chips - 1))
        def _():
            out_ref[q, 0:9] = prev_ref[local]

        out_ref[q, 9:10] = jnp.full((1, GB), block.astype(F32))


def main_kernel(
    where_ref,
    own_meta,
    mate_meta,
    shift_ref,
    own_pick,
    mate_pick,
    own_target,
    mate_target,
    feats_ref,
    mom_ref,
    own_image,
    mate_image,
    keep_ref,
    send_ref,
    par_ref,
    exp_ref,
    col_ref,
    colb_ref,
    tgt_ref,
    img_ref,
    e_ref,
    alpha_ref,
    w_ref,
    chain_ref,
    r_ref,
    hh_ref,
    hl_ref,
    wh_ref,
    wl_ref,
    mom_acc,
    col_acc,
    grad_ref,
):
    core = where_ref[0]
    own_count = own_meta[0]
    mate_count = mate_meta[0]
    own_rays = own_meta[4]
    mate_rays = mate_meta[4]
    even_count = jnp.where(core == 0, own_count, mate_count)
    shift_x = shift_ref[0, 0]
    shift_y = shift_ref[0, 1]

    tgt_ref[core] = own_target[0, 0]
    tgt_ref[1 - core] = mate_target[0, 0]
    img_ref[...] = jnp.zeros(img_ref.shape, F32)
    mom_acc[...] = jnp.zeros(mom_acc.shape, F32)
    col_acc[...] = jnp.zeros(col_acc.shape, F32)
    r_ref[...] = jnp.zeros(r_ref.shape, F32)

    row = lax.broadcasted_iota(jnp.int32, (GB, GB), 0)
    col = lax.broadcasted_iota(jnp.int32, (GB, GB), 1)
    perm = as_bf16((col == (row & (CHAINS - 1)) * STEPS + (row >> 3)).astype(F32))

    def prepare(q, carry):
        par = own_pick[q] + mate_pick[q]
        par_ref[q] = par
        mx = par[0:1] + shift_x
        my = par[1:2] + shift_y
        a, b, c, o = par[2:3], par[3:4], par[4:5], par[5:6]
        k0 = jnp.log2(o) - (0.5 * LOG2E) * (a * mx * mx + 2.0 * b * mx * my + c * my * my)
        k1 = LOG2E * (a * mx + b * my)
        k2 = LOG2E * (b * mx + c * my)
        zero = jnp.zeros_like(k0)
        k = jnp.concatenate(
            [k0, k1, k2, (-0.5 * LOG2E) * a, -LOG2E * b, (-0.5 * LOG2E) * c, zero, zero], axis=0
        )
        ka, kb, kc = pieces(k)
        coef = as_bf16(jnp.concatenate([ka, kb, kc, ka, kb, kc], axis=0))
        exp_ref[q] = as_bf16(dot(perm, coef, ((1,), (1,))))
        colour = jnp.concatenate([par[6:9], jnp.zeros((5, GB), F32)], axis=0)
        ca, cb, cc = pieces(colour)
        coef = as_bf16(jnp.concatenate([ca, cb, cc] * 3, axis=0))
        cols = dot(perm, coef, ((1,), (1,)))
        col_ref[q] = as_bf16(cols)
        for ch in range(3):
            one = cols[:, ch : ch + 1] + cols[:, 8 + ch : 9 + ch] + cols[:, 16 + ch : 17 + ch]
            colb_ref[q, ch] = jnp.broadcast_to(one, (GB, 128))
        return carry

    lax.fori_loop(0, SEGS, prepare, 0)

    def task(index, carry):
        tile = index // (GROUPS // 2)
        group = core + 2 * (index % (GROUPS // 2))
        first = tile * even_count
        count = jnp.where(tile == 0, even_count, SEGS - even_count)
        rays = jnp.where(tile == core, own_rays, mate_rays)
        start = pl.multiple_of(group * GRP, 128)

        @pl.when(start < rays)
        def _():
            feats = feats_ref[:, pl.ds(start, GRP)]

            def forward(k, carry):
                before, i0, i1, i2 = carry
                q = first + k
                e_ref[...] = dot(exp_ref[q], feats, ((1,), (0,)))
                t = [jnp.ones((8, 128), F32)] * LANES
                acc = [[jnp.zeros((8, 128), F32)] * LANES for _ in range(3)]
                for j in range(STEPS):
                    cols = [colb_ref[q, ch, 8 * j : 8 * j + 8] for ch in range(3)]
                    for v in range(LANES):
                        at = (slice(8 * j, 8 * j + 8), slice(128 * v, 128 * v + 128))
                        alpha = jnp.exp2(e_ref[at])
                        w = alpha * t[v]
                        t[v] = t[v] - w
                        alpha_ref[(k,) + at] = alpha
                        w_ref[(k,) + at] = w
                        for ch in range(3):
                            acc[ch][v] = acc[ch][v] + w * cols[ch]
                through = jnp.concatenate(t, axis=1)
                scan = through
                for n in (1, 2, 4):
                    scan = scan * down(scan, n, 1.0)
                begin = before * down(scan, 1, 1.0)
                chain_ref[k, 3] = through
                chain_ref[k, 4] = begin
                out = []
                for ch in range(3):
                    local = jnp.concatenate(acc[ch], axis=1)
                    chain_ref[k, ch] = local
                    out.append((i0, i1, i2)[ch] + total_rows(local * begin))
                return before * row_of(scan, CHAINS - 1), out[0], out[1], out[2]

            blank = jnp.zeros((1, GRP), F32)
            _, i0, i1, i2 = lax.fori_loop(
                0, count, forward, (jnp.ones((8, GRP), F32), blank, blank, blank)
            )
            pixel = start + lax.broadcasted_iota(jnp.int32, (1, GRP), 1)
            live = (pixel < rays).astype(F32)
            resid = []
            for ch, value in enumerate((i0, i1, i2)):
                value = value * live
                img_ref[tile, ch : ch + 1, pl.ds(start, GRP)] = value
                r = (value - tgt_ref[tile, ch : ch + 1, pl.ds(start, GRP)]) * live
                resid.append(jnp.broadcast_to(r, (8, GRP)))
                for n, piece in enumerate(pieces(r)):
                    for m in range(3):
                        r_ref[24 * n + 8 * m + ch : 24 * n + 8 * m + ch + 1] = piece
            rmat = as_bf16(r_ref[...])
            rsum = jnp.concatenate([rmat[0:8], rmat[24:32], rmat[48:56]], axis=0)
            moments = mom_ref[:, pl.ds(start, GRP)]

            def backward(index, after):
                k = count - 1 - index
                q = first + k
                e_ref[...] = dot(col_ref[q], rmat, ((1,), (0,)))
                value = (
                    resid[0] * chain_ref[k, 0]
                    + resid[1] * chain_ref[k, 1]
                    + resid[2] * chain_ref[k, 2]
                )
                scale = chain_ref[k, 3]
                for n in (1, 2, 4):
                    value = value + scale * up(value, n, 0.0)
                    scale = scale * up(scale, n, 1.0)
                entry = value + scale * after
                rows = lax.broadcasted_iota(jnp.int32, entry.shape, 0)
                leave = jnp.where(rows < CHAINS - 1, pltpu.roll(entry, CHAINS - 1, 0), after)
                begin = chain_ref[k, 4]
                behind = [leave[:, 128 * v : 128 * v + 128] for v in range(LANES)]
                scale = [begin[:, 128 * v : 128 * v + 128] for v in range(LANES)]
                for j in range(STEPS - 1, 0, -2):
                    for v in range(LANES):
                        ws, hs = [None, None], [None, None]
                        for i in (1, 0):
                            jj = j - 1 + i
                            at = (slice(8 * jj, 8 * jj + 8), slice(128 * v, 128 * v + 128))
                            d = e_ref[at] - behind[v]
                            ws[i] = w_ref[(k,) + at] * scale[v]
                            hs[i] = ws[i] * d
                            behind[v] = behind[v] + alpha_ref[(k,) + at] * d
                        at = (slice(8 * j - 8, 8 * j + 8), slice(128 * v, 128 * v + 128))
                        w2 = jnp.concatenate(ws, axis=0)
                        h2 = jnp.concatenate(hs, axis=0)
                        wh = as_bf16(w2)
                        hh = as_bf16(h2)
                        wh_ref[at] = wh
                        hh_ref[at] = hh
                        wl_ref[at] = as_bf16(w2 - wh.astype(F32))
                        hl_ref[at] = as_bf16(h2 - hh.astype(F32))
                mom_acc[q] += dot(hh_ref[...], moments, ((1,), (1,))) + dot(
                    hl_ref[...], moments, ((1,), (1,))
                )
                col_acc[q] += dot(wh_ref[...], rsum, ((1,), (1,))) + dot(
                    wl_ref[...], rsum, ((1,), (1,))
                )
                return row_of(entry, 0)

            lax.fori_loop(0, count, backward, jnp.zeros((8, GRP), F32))

        return carry

    lax.fori_loop(0, GROUPS, task, 0)

    def finish(q, carry):
        par = par_ref[q]
        m = sum(dot(as_bf16(p), perm, ((0,), (0,))) for p in pieces(mom_acc[q]))
        g = sum(dot(as_bf16(p), perm, ((0,), (0,))) for p in pieces(col_acc[q]))
        mx = par[0:1] + shift_x
        my = par[1:2] + shift_y
        a, b, c, o = par[2:3], par[3:4], par[4:5], par[5:6]
        m0, m1, m2 = m[0:1], m[1:2], m[2:3]
        m3, m4, m5 = m[3:4] + m[11:12], m[4:5] + m[12:13], m[5:6] + m[13:14]
        along_x = m1 - mx * m0
        along_y = m2 - my * m0
        square_x = m3 - 2.0 * mx * m1 + mx * mx * m0
        cross = m4 - mx * m2 - my * m1 + mx * my * m0
        square_y = m5 - 2.0 * my * m2 + my * my * m0
        rows = [
            a * along_x + b * along_y,
            b * along_x + c * along_y,
            -0.5 * square_x,
            -cross,
            -0.5 * square_y,
            m0 / o,
        ]
        for i, value in enumerate(rows):
            grad_ref[q, i : i + 1] = value
        grad_ref[q, 6:9] = g[0:3] + g[8:11] + g[16:19]
        grad_ref[q, 9:10] = own_pick[q, 9:10]
        grad_ref[q, 10:16] = jnp.zeros((6, GB), F32)
        return carry

    lax.fori_loop(0, SEGS, finish, 0)
    own_image[...] = img_ref[core]
    mate_image[...] = img_ref[1 - core]
    for n in range(SEGS // 2):
        keep_ref[n] = grad_ref[core * 2 + n]
        send_ref[n] = grad_ref[(1 - core) * 2 + n]
        send_ref[n, 9:10] = jnp.zeros((1, GB), F32)


def gather_kernel(where_ref, own_ref, prev_ref, next_ref, own_out, mate_out, acc_ref):
    core = where_ref[0]
    cell = where_ref[3]
    per_block = own_out.shape[0]
    own_first = cell * per_block
    even_first = (cell - core) * per_block
    acc_ref[...] = jnp.zeros(acc_ref.shape, F32)
    names = []
    for ref in (own_ref, prev_ref, next_ref):
        for s in range(ref.shape[0]):
            block = ref[s, 9:10, 0:1][0, 0].astype(jnp.int32)
            names.append((ref, s, block - even_first))
    for ref, s, spot in names:

        @pl.when((spot >= 0) & (spot < 2 * per_block))
        def _():
            acc_ref[spot] += ref[s, 0:9]

    own_out[...] = acc_ref[pl.ds(core * per_block, per_block)]
    mate_out[...] = acc_ref[pl.ds((1 - core) * per_block, per_block)]


def smem():
    return pl.BlockSpec(memory_space=pltpu.SMEM)


def vmem():
    return pl.BlockSpec(memory_space=pltpu.VMEM)


def shifted(block, axis, distance):
    size = lax.axis_size(axis)
    return lax.ppermute(block, axis, [((i - distance) % size, i) for i in range(size)])


def mate(block):
    return lax.ppermute(block, "cell", [(i ^ 1, i) for i in range(lax.axis_size("cell"))])


def shape(*dims):
    return jax.ShapeDtypeStruct(dims, F32)


def pick_call(where, own_meta, mate_meta, own, prev, after):
    return pl.pallas_call(
        pick_kernel,
        out_shape=shape(SEGS, 16, GB),
        in_specs=[smem()] * 3 + [vmem()] * 3,
        out_specs=vmem(),
        name="pick",
    )(where, own_meta, mate_meta, own, prev, after)


def main_call(where, own_meta, mate_meta, shift, own_pick, mate_pick, own_target, mate_target):
    feats, moments = pixel_features()
    return pl.pallas_call(
        main_kernel,
        out_shape=(shape(3, PIX), shape(3, PIX), shape(2, 16, GB), shape(2, 16, GB)),
        in_specs=[smem()] * 4 + [vmem()] * 6,
        out_specs=(vmem(),) * 4,
        scratch_shapes=[
            pltpu.VMEM((SEGS, 16, GB), F32),
            pltpu.VMEM((SEGS, GB, 48), BF16),
            pltpu.VMEM((SEGS, GB, 72), BF16),
            pltpu.VMEM((SEGS, 3, GB, 128), F32),
            pltpu.VMEM((2, 3, PIX), F32),
            pltpu.VMEM((2, 3, PIX), F32),
            pltpu.VMEM((GB, GRP), F32),
            pltpu.VMEM((SEG_MAX, GB, GRP), F32),
            pltpu.VMEM((SEG_MAX, GB, GRP), F32),
            pltpu.VMEM((SEG_MAX, 5, 8, GRP), F32),
            pltpu.VMEM((72, GRP), F32),
            pltpu.VMEM((GB, GRP), BF16),
            pltpu.VMEM((GB, GRP), BF16),
            pltpu.VMEM((GB, GRP), BF16),
            pltpu.VMEM((GB, GRP), BF16),
            pltpu.VMEM((SEGS, GB, 16), F32),
            pltpu.VMEM((SEGS, GB, 24), F32),
            pltpu.VMEM((SEGS, 16, GB), F32),
        ],
        name="splat",
    )(
        where,
        own_meta,
        mate_meta,
        shift,
        own_pick,
        mate_pick,
        own_target,
        mate_target,
        jnp.asarray(feats),
        jnp.asarray(moments),
    )


def gather_call(where, own, prev, after, per_block):
    return pl.pallas_call(
        gather_kernel,
        out_shape=(shape(per_block, 9, GB), shape(per_block, 9, GB)),
        in_specs=[smem()] + [vmem()] * 3,
        out_specs=(vmem(),) * 2,
        scratch_shapes=[pltpu.VMEM((2 * per_block, 9, GB), F32)],
        name="gather",
    )(where, own, prev, after)


def shards(gaussians, seg_count, seg_block, ray_count, camera_shift, target):
    cell = lax.axis_index("cell")
    chips = lax.axis_size("cell") // 2
    where = jnp.stack([cell % 2, cell // 2, jnp.int32(chips), cell]).astype(jnp.int32)
    own_meta = jnp.concatenate([seg_count[0], seg_block[0, 0], ray_count[0]])
    mate_meta = mate(own_meta)
    prev = shifted(gaussians, "cell", 2)
    after = shifted(gaussians, "cell", -2)
    mate_target = mate(target)
    own_pick = pick_call(where, own_meta, mate_meta, gaussians, prev, after)
    mate_pick = mate(own_pick)
    own_image, mate_image, keep, send = main_call(
        where, own_meta, mate_meta, camera_shift, own_pick, mate_pick, target, mate_target
    )
    grads = keep + mate(send)
    image = own_image + mate(mate_image)
    views = [grads] + [shifted(grads, "view", d) for d in (1, 2, 3)]
    stack = jnp.concatenate(views, axis=0)
    own_out, mate_out = gather_call(
        where, stack, shifted(stack, "cell", 2), shifted(stack, "cell", -2), gaussians.shape[0]
    )
    return image[None, None], own_out + mate(mate_out)


def solution(mesh):
    placed = (
        P("cell", None, None),
        P("view", "cell"),
        P("view", "cell", None),
        P("view", "cell"),
        P("view", None),
        P("view", "cell", None, None),
    )
    return jax.shard_map(
        shards,
        mesh=mesh,
        in_specs=placed,
        out_specs=(P("view", "cell", None, None), P("cell", None, None)),
        check_vma=False,
    )
```

time: 184 us -> 70.5 us (0.38)
  matrix products: 64.5 us -> 0 us
  waiting for transfers between devices: 49.2 us -> 16.8 us
  other arithmetic: 23.4 us -> 2.45 us
  Pallas kernels: 0 us -> 19.5 us
  between operations: 15.5 us -> 2.03 us
  starting transfers between devices: 15.9 us -> 23.7 us
  local copies, waits for them, and re-layouts: 13.4 us -> 5.67 us
    dot_general x22 -> x0, matrix products: 64.5 us -> none  [the longest x3 14.8 us: backward_task(): jnp.dot(lower_tri, log_trans, precision=precise, preferred_element_type=j...]
    psum x1 -> x0, waiting for transfers between devices: 37.8 us -> none  [shards(): gauss_grad = lax.psum(block_grads, 'view')]
    pallas_call x0 -> x3, Pallas kernels: none -> 19.5 us  [the longest x1 15.4 us: main_call(): pl.pallas_call(main_kernel, out_shape=(shape(3, PIX), shape(3, PIX), shap...]
    ppermute x8 -> x13, starting transfers between devices: 15.9 us -> 23.7 us  [the longest x7 14.1 us: shifted(): lax.ppermute(block, axis, [((i - distance) % size, i) for i in range(size)])]
    sub x6 -> x0, other arithmetic: 7.23 us -> none  [pixel_frame(): pix_y = (pixel_ids // TILE).astype(jnp.float32) - centre - shift[1]]
    reduce_sum x4 -> x0, other arithmetic: 6.93 us -> none  [the longest x3 6.89 us: forward_task(): totals = jnp.sum(log_trans, axis=0)]
    mul x10 -> x0, other arithmetic: 6.44 us -> none  [the longest x3 3.73 us: gradient_rows(): pix_y * pix_y]
    ppermute x8 -> x13, waiting for transfers between devices: 11.3 us -> 16.8 us  [the longest x7 13.6 us: shifted(): lax.ppermute(block, axis, [((i - distance) % size, i) for i in range(size)])]
  transfers between devices with their start and end apart: 9 -> 13, of which waited for: 4 -> 9; matrix products, arithmetic and copies ran while one was open for 4% -> 2% of each run, Pallas kernels for 0% -> 3%
where the time goes in v1:
time: 70.5 us; the launch traced here: 70.2 us
  starting transfers between devices  23.7 us (34%)
  Pallas kernels  19.5 us (28%)
  waiting for transfers between devices  16.8 us (24%)
  local copies, waits for them, and re-layouts  5.67 us (8%)
  other arithmetic  2.45 us (3%)
  between operations  2.03 us (3%)
    pallas_call x1, Pallas kernels, main_call(): pl.pallas_call(main_kernel, out_shape=(shape(3, PIX), shape(3, PIX), shap...  15.4 us
    ppermute x7, starting transfers between devices, shifted(): lax.ppermute(block, axis, [((i - distance) % size, i) for i in range(size)])  14.1 us
    ppermute x7, waiting for transfers between devices, shifted(): lax.ppermute(block, axis, [((i - distance) % size, i) for i in range(size)])  13.6 us
    ppermute x6, starting transfers between devices, mate(): lax.ppermute(block, 'cell', [(i ^ 1, i) for i in range(lax.axis_size('cel...  9.62 us
    unnamed x34, local copies, waits for them, and re-layouts  5.67 us
    ppermute x6, waiting for transfers between devices, mate(): lax.ppermute(block, 'cell', [(i ^ 1, i) for i in range(lax.axis_size('cel...  3.2 us
    pallas_call x1, Pallas kernels, gather_call(): pl.pallas_call(gather_kernel, out_shape=(shape(per_block, 9, GB), shape(p...  2.16 us
    pallas_call x1, Pallas kernels, pick_call(): pl.pallas_call(pick_kernel, out_shape=shape(SEGS, 16, GB), in_specs=[smem...  1.96 us
  transfers between devices with their start and end apart: 13, of which 9 were waited for; matrix products, arithmetic and copies ran while one was open for 2% of the time, Pallas kernels for 3%

profile of v1, /device:TPU:1, one launch (start us, length us, event | category | flops | bytes accessed | tf_op | source)
XLA Modules:
  0.0 70.2 jit_solution(2031954424268443350)
XLA Ops:
  0.6 1.0 %copy.12.own_ref = f32[16,9,256]{2,1,0:T(8,128)S(1)} copy(f32[16,9,256]{2,0,1:T(8,128)} %param.8) | data formatting | bytes 294912 | tf_op args[0]
  1.6 8.9 %collective-permute-start.2 = (f32[16,9,256]{2,1,0:T(8,128)S(1)}, f32[16,9,256]{2,1,0:T(8,128)S(1)}, u32[]{:S(2)}, u32[]{:S(2)}) collective-permute-start(f32[16,9,256]{2,1,0:T(8,128)S(1)} %copy.12.own_ref), channel_id=1, source_target_pairs={{8,0},{12,4},{16,8},{20,12},{24,16},{28,20},{32,24},{36,28},{40,32... | collective-permute-start | bytes 442376 | tf_op jit(solution)/shard_map/ppermute | solution.py:374
  11.9 0.6 copy-done.13
  12.6 1.0 %collective-permute-start = (s32[5]{0:T(128)S(1)}, s32[5]{0:T(128)S(1)}, u32[]{:S(2)}, u32[]{:S(2)}) collective-permute-start(s32[5]{0:T(128)S(1)} %pad_add_fusion.1.own_meta), channel_id=1, source_target_pairs={{4,0},{0,4},{12,8},{8,12},{20,16},{16,20},{28,24},{24,28},{36,32},... | collective-permute-start | bytes 68 | tf_op jit(solution)/shard_map/ppermute | solution.py:378
  13.6 0.6 pad_add_fusion.where_ref
  14.4 1.1 %collective-permute-done.2.next_ref = f32[16,9,256]{2,1,0:T(8,128)S(1)} collective-permute-done((f32[16,9,256]{2,1,0:T(8,128)S(1)}, f32[16,9,256]{2,1,0:T(8,128)S(1)}, u32[]{:S(2)}, u32[]{:S(2)}) %collective-permute-start.2) | collective-permute-done | bytes 147488 | tf_op jit(solution)/shard_map/ppermute | solution.py:374
  15.6 5.2 %collective-permute-done.1.prev_ref = f32[16,9,256]{2,1,0:T(8,128)S(1)} collective-permute-done((f32[16,9,256]{2,1,0:T(8,128)S(1)}, f32[16,9,256]{2,1,0:T(8,128)S(1)}, u32[]{:S(2)}, u32[]{:S(2)}) %collective-permute-start.1) | collective-permute-done | bytes 147488 | tf_op jit(solution)/shard_map/ppermute | solution.py:374
  20.8 0.7 copy-done.3
  21.5 2.0 %pick.1.own_pick = f32[4,16,256]{2,1,0:T(8,128)} custom-call(s32[4]{0:T(128)} %pad_add_fusion.where_ref, s32[5]{0:T(128)} %copy-done.11, s32[5]{0:T(128)} %copy-done.12, f32[16,9,256]{2,1,0:T(8,128)} %copy-done, f32[16,9,256]{2,1,0:T(8,128)} %copy-done.3, f32[16,9,256]{2,1,0:T(8,128)} %copy-done.2), custom_call_target="tpu_custom_call" | custom-call | tf_op jit(solution)/shard_map/pick/pallas_call | solution.py:386
  23.5 1.8 %collective-permute-start.3 = (f32[4,16,256]{2,1,0:T(8,128)}, f32[4,16,256]{2,1,0:T(8,128)S(1)}, u32[]{:S(2)}, u32[]{:S(2)}) collective-permute-start(f32[4,16,256]{2,1,0:T(8,128)} %pick.1.own_pick), channel_id=1, source_target_pairs={{4,0},{0,4},{12,8},{8,12},{20,16},{16,20},{28,24},{24,28},{36,32},... | collective-permute-start | bytes 196616 | tf_op jit(solution)/shard_map/ppermute | solution.py:378
  25.4 1.2 %collective-permute-done.4.mate_target = f32[1,1,3,2304]{3,2,1,0:T(4,128)S(1)} collective-permute-done((f32[1,1,3,2304]{3,2,1,0:T(4,128)S(1)}, f32[1,1,3,2304]{3,2,1,0:T(4,128)S(1)}, u32[]{:S(2)}, u32[]{:S(2)}) %collective-permute-start.4) | collective-permute-done | bytes 27680 | tf_op jit(solution)/shard_map/ppermute | solution.py:378
  26.6 0.6 copy-done.9
  27.2 0.6 copy-done.7
  27.8 15.4 %splat.1 = (f32[3,2304]{1,0:T(4,128)}, f32[3,2304]{1,0:T(4,128)}, f32[2,16,256]{2,1,0:T(8,128)}, f32[2,16,256]{2,1,0:T(8,128)}) custom-call(s32[4]{0:T(128)} %pad_add_fusion.where_ref, s32[5]{0:T(128)} %copy-done.11, s32[5]{0:T(128)} %copy-done.12, f32[1,2]{1,0:T(1,128)} %shift_ref.1, f32[4,16,256]{2,1,0:T(8,128)} %pick.1.own_pick, f32[4,16,256]{2,1,0:T(8,128)} %copy-done.7, ...), custom_call_target="tpu_custom_call" | custom-call | tf_op jit(solution)/shard_map/splat/pallas_call | solution.py:397
  43.3 1.2 %collective-permute-start.6 = (f32[2,16,256]{2,1,0:T(8,128)}, f32[2,16,256]{2,1,0:T(8,128)S(1)}, u32[]{:S(2)}, u32[]{:S(2)}) collective-permute-start(f32[2,16,256]{2,1,0:T(8,128)} %get-tuple-element.11), channel_id=1, source_target_pairs={{4,0},{0,4},{12,8},{8,12},{20,16},{16,20},{28,24},{24,28},{36,32},... | collective-permute-start | bytes 98312 | tf_op jit(solution)/shard_map/ppermute | solution.py:378
  44.4 1.1 %collective-permute-done.6 = f32[2,16,256]{2,1,0:T(8,128)S(1)} collective-permute-done((f32[2,16,256]{2,1,0:T(8,128)}, f32[2,16,256]{2,1,0:T(8,128)S(1)}, u32[]{:S(2)}, u32[]{:S(2)}) %collective-permute-start.6) | collective-permute-done | bytes 32800 | tf_op jit(solution)/shard_map/ppermute | solution.py:378
  45.5 0.8 %add.16 = f32[2,16,256]{2,1,0:T(8,128)S(1)} add(f32[2,16,256]{2,1,0:T(8,128)} %get-tuple-element.10, f32[2,16,256]{2,1,0:T(8,128)S(1)} %collective-permute-done.6) | non-fusion elementwise | flops 8192 | bytes 98304 | tf_op jit(solution)/shard_map/add | solution.py:462
  46.3 2.8 %collective-permute-start.8 = (f32[2,16,256]{2,1,0:T(8,128)S(1)}, f32[2,16,256]{2,1,0:T(8,128)S(1)}, u32[]{:S(2)}, u32[]{:S(2)}) collective-permute-start(f32[2,16,256]{2,1,0:T(8,128)S(1)} %add.16), channel_id=1, source_target_pairs={{2,0},{3,1},{0,2},{1,3},{6,4},{7,5},{4,6},{5,7},{10,8},{11,9},{8,1... | collective-permute-start | bytes 98312 | tf_op jit(solution)/shard_map/ppermute | solution.py:374
  49.1 0.8 %collective-permute-start.7 = (f32[2,16,256]{2,1,0:T(8,128)S(1)}, f32[2,16,256]{2,1,0:T(8,128)S(1)}, u32[]{:S(2)}, u32[]{:S(2)}) collective-permute-start(f32[2,16,256]{2,1,0:T(8,128)S(1)} %add.16), channel_id=1, source_target_pairs={{3,0},{0,1},{1,2},{2,3},{7,4},{4,5},{5,6},{6,7},{11,8},{8,9},{9,10... | collective-permute-start | bytes 98312 | tf_op jit(solution)/shard_map/ppermute | solution.py:374
  49.9 0.8 %collective-permute-done.8 = f32[2,16,256]{2,1,0:T(8,128)S(1)} collective-permute-done((f32[2,16,256]{2,1,0:T(8,128)S(1)}, f32[2,16,256]{2,1,0:T(8,128)S(1)}, u32[]{:S(2)}, u32[]{:S(2)}) %collective-permute-start.8) | collective-permute-done | bytes 32800 | tf_op jit(solution)/shard_map/ppermute | solution.py:374
  50.6 2.5 %collective-permute-done.7 = f32[2,16,256]{2,1,0:T(8,128)S(1)} collective-permute-done((f32[2,16,256]{2,1,0:T(8,128)S(1)}, f32[2,16,256]{2,1,0:T(8,128)S(1)}, u32[]{:S(2)}, u32[]{:S(2)}) %collective-permute-start.7) | collective-permute-done | bytes 32800 | tf_op jit(solution)/shard_map/ppermute | solution.py:374
  53.1 0.8 %collective-permute-start.11 = (f32[8,16,256]{2,1,0:T(8,128)S(1)}, f32[8,16,256]{2,1,0:T(8,128)S(1)}, u32[]{:S(2)}, u32[]{:S(2)}) collective-permute-start(f32[8,16,256]{2,1,0:T(8,128)S(1)} %pad_maximum_fusion.own_ref), channel_id=1, source_target_pairs={{8,0},{12,4},{16,8},{20,12},{24,16},{28,20},{32,24},{36,28},{40,32... | collective-permute-start | bytes 393224 | tf_op jit(solution)/shard_map/ppermute | solution.py:374
  53.9 0.8 %collective-permute-start.10 = (f32[8,16,256]{2,1,0:T(8,128)S(1)}, f32[8,16,256]{2,1,0:T(8,128)S(1)}, u32[]{:S(2)}, u32[]{:S(2)}) collective-permute-start(f32[8,16,256]{2,1,0:T(8,128)S(1)} %pad_maximum_fusion.own_ref), channel_id=1, source_target_pairs={{248,0},{252,4},{0,8},{4,12},{8,16},{12,20},{16,24},{20,28},{24,32... | collective-permute-start | bytes 393224 | tf_op jit(solution)/shard_map/ppermute | solution.py:374
  54.7 2.3 %collective-permute-start.5 = (f32[3,2304]{1,0:T(4,128)S(1)}, f32[3,2304]{1,0:T(4,128)S(1)}, u32[]{:S(2)}, u32[]{:S(2)}) collective-permute-start(f32[3,2304]{1,0:T(4,128)S(1)} %copy-done.14), channel_id=1, source_target_pairs={{4,0},{0,4},{12,8},{8,12},{20,16},{16,20},{28,24},{24,28},{36,32},... | collective-permute-start | bytes 82952 | tf_op jit(solution)/shard_map/ppermute | solution.py:378
  57.0 4.0 %collective-permute-done.10.prev_ref = f32[8,16,256]{2,1,0:T(8,128)S(1)} collective-permute-done((f32[8,16,256]{2,1,0:T(8,128)S(1)}, f32[8,16,256]{2,1,0:T(8,128)S(1)}, u32[]{:S(2)}, u32[]{:S(2)}) %collective-permute-start.10) | collective-permute-done | bytes 131104 | tf_op jit(solution)/shard_map/ppermute | solution.py:374
  61.0 0.7 copy-done.6
  61.7 2.2 %gather.1 = (f32[16,9,256]{2,1,0:T(8,128)}, f32[16,9,256]{2,1,0:T(8,128)}) custom-call(s32[4]{0:T(128)} %pad_add_fusion.where_ref, f32[8,16,256]{2,1,0:T(8,128)} %copy-done.1, f32[8,16,256]{2,1,0:T(8,128)} %copy-done.6, f32[8,16,256]{2,1,0:T(8,128)} %copy-done.5), custom_call_target="tpu_custom_call" | custom-call | tf_op jit(solution)/shard_map/gather/pallas_call | solution.py:438
  63.9 3.2 %collective-permute-start.12 = (f32[16,9,256]{2,1,0:T(8,128)}, f32[16,9,256]{2,1,0:T(8,128)S(1)}, u32[]{:S(2)}, u32[]{:S(2)}) collective-permute-start(f32[16,9,256]{2,1,0:T(8,128)} %get-tuple-element.13), channel_id=1, source_target_pairs={{4,0},{0,4},{12,8},{8,12},{20,16},{16,20},{28,24},{24,28},{36,32},... | collective-permute-start | bytes 442376 | tf_op jit(solution)/shard_map/ppermute | solution.py:378
  67.1 0.6 copy.15
  67.7 0.7 %collective-permute-done.12 = f32[16,9,256]{2,1,0:T(8,128)S(1)} collective-permute-done((f32[16,9,256]{2,1,0:T(8,128)}, f32[16,9,256]{2,1,0:T(8,128)S(1)}, u32[]{:S(2)}, u32[]{:S(2)}) %collective-permute-start.12) | collective-permute-done | bytes 147488 | tf_op jit(solution)/shard_map/ppermute | solution.py:378
  68.4 1.0 %add.17 = f32[16,9,256]{2,1,0:T(8,128)S(1)} add(f32[16,9,256]{2,1,0:T(8,128)} %get-tuple-element.12, f32[16,9,256]{2,1,0:T(8,128)S(1)} %collective-permute-done.12) | non-fusion elementwise | flops 36864 | bytes 442368 | tf_op jit(solution)/shard_map/add | solution.py:469
  69.4 0.8 %copy.16 = f32[16,9,256]{2,0,1:T(8,128)} copy(f32[16,9,256]{2,1,0:T(8,128)S(1)} %add.17) | data formatting | bytes 294912
  (37 shorter events, 0.5 us)
Async XLA Ops:
  1.6 19.2 %copy-start = (f32[16,9,256]{2,1,0:T(8,128)}, f32[16,9,256]{2,1,0:T(8,128)S(1)}, u32[]{:S(2)}) copy-start(f32[16,9,256]{2,1,0:T(8,128)S(1)} %copy.12.own_ref) | copy-start | bytes 442372
  1.6 13.9 %collective-permute-start.2 = (f32[16,9,256]{2,1,0:T(8,128)S(1)}, f32[16,9,256]{2,1,0:T(8,128)S(1)}, u32[]{:S(2)}, u32[]{:S(2)}) collective-permute-start(f32[16,9,256]{2,1,0:T(8,128)S(1)} %copy.12.own_ref), channel_id=1, source_target_pairs={{8,0},{12,4},{16,8},{20,12},{24,16},{28,20},{32,24},{36,28},{40,32... | collective-permute-start | bytes 442376 | tf_op jit(solution)/shard_map/ppermute | solution.py:374
  10.6 10.2 %collective-permute-start.1 = (f32[16,9,256]{2,1,0:T(8,128)S(1)}, f32[16,9,256]{2,1,0:T(8,128)S(1)}, u32[]{:S(2)}, u32[]{:S(2)}) collective-permute-start(f32[16,9,256]{2,1,0:T(8,128)S(1)} %copy.12.own_ref), channel_id=1, source_target_pairs={{248,0},{252,4},{0,8},{4,12},{8,16},{12,20},{16,24},{20,28},{24,32... | collective-permute-start | bytes 442376 | tf_op jit(solution)/shard_map/ppermute | solution.py:374
  11.9 0.7 copy-start.13
  12.6 1.0 %copy-start.11 = (s32[5]{0:T(128)}, s32[5]{0:T(128)S(1)}, u32[]{:S(2)}) copy-start(s32[5]{0:T(128)S(1)} %pad_add_fusion.1.own_meta) | copy-start | bytes 64
  12.6 1.8 %collective-permute-start = (s32[5]{0:T(128)S(1)}, s32[5]{0:T(128)S(1)}, u32[]{:S(2)}, u32[]{:S(2)}) collective-permute-start(s32[5]{0:T(128)S(1)} %pad_add_fusion.1.own_meta), channel_id=1, source_target_pairs={{4,0},{0,4},{12,8},{8,12},{20,16},{16,20},{28,24},{24,28},{36,32},... | collective-permute-start | bytes 68 | tf_op jit(solution)/shard_map/ppermute | solution.py:378
  14.2 11.1 %copy-start.10 = (f32[1,1,3,2304]{3,1,2,0:T(1,128)S(1)}, f32[1,1,3,2304]{3,1,2,0:T(1,128)}, u32[]{:S(2)}) copy-start(f32[1,1,3,2304]{3,1,2,0:T(1,128)} %param.13) | copy-start | bytes 82948
  14.4 6.4 %copy-start.12 = (s32[5]{0:T(128)}, s32[5]{0:T(128)S(1)}, u32[]{:S(2)}) copy-start(s32[5]{0:T(128)S(1)} %collective-permute-done.mate_meta) | copy-start | bytes 64
  15.6 5.2 %copy-start.2 = (f32[16,9,256]{2,1,0:T(8,128)}, f32[16,9,256]{2,1,0:T(8,128)S(1)}, u32[]{:S(2)}) copy-start(f32[16,9,256]{2,1,0:T(8,128)S(1)} %collective-permute-done.2.next_ref) | copy-start | bytes 442372
  20.8 0.7 %copy-start.3 = (f32[16,9,256]{2,1,0:T(8,128)}, f32[16,9,256]{2,1,0:T(8,128)S(1)}, u32[]{:S(2)}) copy-start(f32[16,9,256]{2,1,0:T(8,128)S(1)} %collective-permute-done.1.prev_ref) | copy-start | bytes 442372
  23.5 3.1 %collective-permute-start.3 = (f32[4,16,256]{2,1,0:T(8,128)}, f32[4,16,256]{2,1,0:T(8,128)S(1)}, u32[]{:S(2)}, u32[]{:S(2)}) collective-permute-start(f32[4,16,256]{2,1,0:T(8,128)} %pick.1.own_pick), channel_id=1, source_target_pairs={{4,0},{0,4},{12,8},{8,12},{20,16},{16,20},{28,24},{24,28},{36,32},... | collective-permute-start | bytes 196616 | tf_op jit(solution)/shard_map/ppermute | solution.py:378
  25.3 1.3 %copy-start.4 = (f32[1,1,3,2304]{3,2,1,0:T(4,128)}, f32[1,1,3,2304]{3,2,1,0:T(4,128)S(1)}, u32[]{:S(2)}) copy-start(f32[1,1,3,2304]{3,2,1,0:T(4,128)S(1)} %copy.14.own_target) | copy-start | bytes 82948
  25.3 1.3 %collective-permute-start.4 = (f32[1,1,3,2304]{3,2,1,0:T(4,128)S(1)}, f32[1,1,3,2304]{3,2,1,0:T(4,128)S(1)}, u32[]{:S(2)}, u32[]{:S(2)}) collective-permute-start(f32[1,1,3,2304]{3,2,1,0:T(4,128)S(1)} %copy.14.own_target), channel_id=1, source_target_pairs={{4,0},{0,4},{12,8},{8,12},{20,16},{16,20},{28,24},{24,28},{36,32},... | collective-permute-start | bytes 82952 | tf_op jit(solution)/shard_map/ppermute | solution.py:378
  26.6 0.6 copy-start.9
  27.2 0.6 copy-start.7
  43.3 2.2 %collective-permute-start.6 = (f32[2,16,256]{2,1,0:T(8,128)}, f32[2,16,256]{2,1,0:T(8,128)S(1)}, u32[]{:S(2)}, u32[]{:S(2)}) collective-permute-start(f32[2,16,256]{2,1,0:T(8,128)} %get-tuple-element.11), channel_id=1, source_target_pairs={{4,0},{0,4},{12,8},{8,12},{20,16},{16,20},{28,24},{24,28},{36,32},... | collective-permute-start | bytes 98312 | tf_op jit(solution)/shard_map/ppermute | solution.py:378
  46.3 8.4 %copy-start.14 = (f32[3,2304]{1,0:T(4,128)S(1)}, f32[3,2304]{1,0:T(4,128)}, u32[]{:S(2)}) copy-start(f32[3,2304]{1,0:T(4,128)} %get-tuple-element.9) | copy-start | bytes 82948
  46.3 3.6 %collective-permute-start.9 = (f32[2,16,256]{2,1,0:T(8,128)S(1)}, f32[2,16,256]{2,1,0:T(8,128)S(1)}, u32[]{:S(2)}, u32[]{:S(2)}) collective-permute-start(f32[2,16,256]{2,1,0:T(8,128)S(1)} %add.16), channel_id=1, source_target_pairs={{1,0},{2,1},{3,2},{0,3},{5,4},{6,5},{7,6},{4,7},{9,8},{10,9},{11,1... | collective-permute-start | bytes 98312 | tf_op jit(solution)/shard_map/ppermute | solution.py:374
  46.3 4.4 %collective-permute-start.8 = (f32[2,16,256]{2,1,0:T(8,128)S(1)}, f32[2,16,256]{2,1,0:T(8,128)S(1)}, u32[]{:S(2)}, u32[]{:S(2)}) collective-permute-start(f32[2,16,256]{2,1,0:T(8,128)S(1)} %add.16), channel_id=1, source_target_pairs={{2,0},{3,1},{0,2},{1,3},{6,4},{7,5},{4,6},{5,7},{10,8},{11,9},{8,1... | collective-permute-start | bytes 98312 | tf_op jit(solution)/shard_map/ppermute | solution.py:374
  49.1 4.0 %collective-permute-start.7 = (f32[2,16,256]{2,1,0:T(8,128)S(1)}, f32[2,16,256]{2,1,0:T(8,128)S(1)}, u32[]{:S(2)}, u32[]{:S(2)}) collective-permute-start(f32[2,16,256]{2,1,0:T(8,128)S(1)} %add.16), channel_id=1, source_target_pairs={{3,0},{0,1},{1,2},{2,3},{7,4},{4,5},{5,6},{6,7},{11,8},{8,9},{9,10... | collective-permute-start | bytes 98312 | tf_op jit(solution)/shard_map/ppermute | solution.py:374
  53.1 7.9 %copy-start.1 = (f32[8,16,256]{2,1,0:T(8,128)}, f32[8,16,256]{2,1,0:T(8,128)S(1)}, u32[]{:S(2)}) copy-start(f32[8,16,256]{2,1,0:T(8,128)S(1)} %pad_maximum_fusion.own_ref) | copy-start | bytes 393220
  53.1 3.9 %collective-permute-start.11 = (f32[8,16,256]{2,1,0:T(8,128)S(1)}, f32[8,16,256]{2,1,0:T(8,128)S(1)}, u32[]{:S(2)}, u32[]{:S(2)}) collective-permute-start(f32[8,16,256]{2,1,0:T(8,128)S(1)} %pad_maximum_fusion.own_ref), channel_id=1, source_target_pairs={{8,0},{12,4},{16,8},{20,12},{24,16},{28,20},{32,24},{36,28},{40,32... | collective-permute-start | bytes 393224 | tf_op jit(solution)/shard_map/ppermute | solution.py:374
  53.9 7.1 %collective-permute-start.10 = (f32[8,16,256]{2,1,0:T(8,128)S(1)}, f32[8,16,256]{2,1,0:T(8,128)S(1)}, u32[]{:S(2)}, u32[]{:S(2)}) collective-permute-start(f32[8,16,256]{2,1,0:T(8,128)S(1)} %pad_maximum_fusion.own_ref), channel_id=1, source_target_pairs={{248,0},{252,4},{0,8},{4,12},{8,16},{12,20},{16,24},{20,28},{24,32... | collective-permute-start | bytes 393224 | tf_op jit(solution)/shard_map/ppermute | solution.py:374
  54.7 12.4 %copy-start.8 = (f32[3,2304]{1,0:T(4,128)S(1)}, f32[3,2304]{1,0:T(4,128)}, u32[]{:S(2)}) copy-start(f32[3,2304]{1,0:T(4,128)} %get-tuple-element.8) | copy-start | bytes 82948
  54.7 12.4 %collective-permute-start.5 = (f32[3,2304]{1,0:T(4,128)S(1)}, f32[3,2304]{1,0:T(4,128)S(1)}, u32[]{:S(2)}, u32[]{:S(2)}) collective-permute-start(f32[3,2304]{1,0:T(4,128)S(1)} %copy-done.14), channel_id=1, source_target_pairs={{4,0},{0,4},{12,8},{8,12},{20,16},{16,20},{28,24},{24,28},{36,32},... | collective-permute-start | bytes 82952 | tf_op jit(solution)/shard_map/ppermute | solution.py:378
  57.0 4.0 %copy-start.5 = (f32[8,16,256]{2,1,0:T(8,128)}, f32[8,16,256]{2,1,0:T(8,128)S(1)}, u32[]{:S(2)}) copy-start(f32[8,16,256]{2,1,0:T(8,128)S(1)} %collective-permute-done.11.next_ref) | copy-start | bytes 393220
  61.0 0.7 copy-start.6
  63.9 4.6 %collective-permute-start.12 = (f32[16,9,256]{2,1,0:T(8,128)}, f32[16,9,256]{2,1,0:T(8,128)S(1)}, u32[]{:S(2)}, u32[]{:S(2)}) collective-permute-start(f32[16,9,256]{2,1,0:T(8,128)} %get-tuple-element.13), channel_id=1, source_target_pairs={{4,0},{0,4},{12,8},{8,12},{20,16},{16,20},{28,24},{24,28},{36,32},... | collective-permute-start | bytes 442376 | tf_op jit(solution)/shard_map/ppermute | solution.py:378

commit v2 on v1

--- a/solution.py
+++ b/solution.py
@@ -12,8 +12,11 @@
 GB = 256
 SEGS = 4
 SEG_MAX = 3
+BLOCKS_DEV = 16
 GRP = 384
 GROUPS = PIX // GRP
+ROWS = 3 * PIX // 128
+CHUNKS = PIX // 128
 LANES = GRP // 128
 CHAINS = 8
 STEPS = GB // CHAINS
@@ -73,47 +76,80 @@
     return jnp.sum(x, axis=0, keepdims=True)
 
 
-def pick_kernel(where_ref, own_meta, mate_meta, own_ref, prev_ref, next_ref, out_ref):
-    core = where_ref[0]
-    chip = where_ref[1]
-    chips = where_ref[2]
-    per_block = own_ref.shape[0]
-    even_count = jnp.where(core == 0, own_meta[0], mate_meta[0])
+def my_core():
+    return lax.axis_index("cell") % 2
+
+
+def pack_kernel(count_ref, block_ref, rays_ref, shift_ref, target_ref, tile_ref):
+    for ch in range(3):
+        for n in range(CHUNKS):
+            at = CHUNKS * ch + n
+            tile_ref[at : at + 1] = target_ref[ch, :, 128 * n : 128 * n + 128]
+    lane = lax.broadcasted_iota(jnp.int32, (1, 128), 1)
+    values = [count_ref[0, 0].astype(F32)]
+    values += [block_ref[0, 0, k].astype(F32) for k in range(SEG_MAX)]
+    values += [rays_ref[0, 0].astype(F32), shift_ref[0, 0], shift_ref[0, 1]]
+    row = jnp.zeros((1, 128), F32)
+    for i, value in enumerate(values):
+        row = jnp.where(lane == i, value, row)
+    tile_ref[ROWS : ROWS + 1] = row
+    tile_ref[ROWS + 1 :] = jnp.zeros((1, 128), F32)
+
+
+def meta_of(ref):
+    row = ref[ROWS : ROWS + 1]
+    return [row[0, i] for i in range(7)]
+
+
+def integer(x):
+    return x.astype(jnp.int32)
+
+
+def pick_kernel(own_tile, mate_tile, own_ref, prev_ref, next_ref, out_ref):
+    core = my_core()
+    chips = lax.axis_size("cell") // 2
+    chip = lax.axis_index("cell") // 2
+    per_block = own_ref.shape[1]
+    own_meta = [integer(v) for v in meta_of(own_tile)[:4]]
+    mate_meta = [integer(v) for v in meta_of(mate_tile)[:4]]
+    first = [jnp.where(core == 0, o, m) for o, m in zip(own_meta, mate_meta)]
+    second = [jnp.where(core == 0, m, o) for o, m in zip(own_meta, mate_meta)]
     for q in range(SEGS):
-        tile = (q >= even_count).astype(jnp.int32)
-        slot = q - tile * even_count
-        slot = jnp.clip(slot, 0, SEG_MAX - 1)
-        block = jnp.where(tile == core, own_meta[1 + slot], mate_meta[1 + slot])
+        odd = q >= first[0]
+        block = jnp.where(odd, second[1], first[1 + min(q, 2)])
+        for k in (1, 2):
+            block = jnp.where(odd & (q - first[0] == k), second[1 + k], block)
         home = block // per_block
         local = block % per_block
         ahead = (home // 2 - chip + chips) % chips
         held = home % 2 == core
-        out_ref[q] = jnp.zeros(out_ref.shape[1:], F32)
+        out_ref[q : q + 1, PIX:] = jnp.full((1, GB), block.astype(F32))
+
+        @pl.when(jnp.logical_not(held))
+        def _():
+            out_ref[q : q + 1, :PIX] = jnp.zeros((1, PIX), F32)
 
         @pl.when(held & (ahead == 0))
         def _():
-            out_ref[q, 0:9] = own_ref[local]
+            for p in range(9):
+                out_ref[q : q + 1, GB * p : GB * p + GB] = own_ref[p, pl.ds(local, 1), :]
 
         @pl.when(held & (ahead == 1))
         def _():
-            out_ref[q, 0:9] = next_ref[local]
+            for p in range(9):
+                out_ref[q : q + 1, GB * p : GB * p + GB] = next_ref[p, pl.ds(local, 1), :]
 
         @pl.when(held & (ahead == chips - 1))
         def _():
-            out_ref[q, 0:9] = prev_ref[local]
-
-        out_ref[q, 9:10] = jnp.full((1, GB), block.astype(F32))
+            for p in range(9):
+                out_ref[q : q + 1, GB * p : GB * p + GB] = prev_ref[p, pl.ds(local, 1), :]
 
 
 def main_kernel(
-    where_ref,
-    own_meta,
-    mate_meta,
-    shift_ref,
     own_pick,
     mate_pick,
-    own_target,
-    mate_target,
+    own_tile,
+    mate_tile,
     feats_ref,
     mom_ref,
     own_image,
@@ -137,19 +173,18 @@
     wl_ref,
     mom_acc,
     col_acc,
-    grad_ref,
 ):
-    core = where_ref[0]
-    own_count = own_meta[0]
-    mate_count = mate_meta[0]
-    own_rays = own_meta[4]
-    mate_rays = mate_meta[4]
-    even_count = jnp.where(core == 0, own_count, mate_count)
-    shift_x = shift_ref[0, 0]
-    shift_y = shift_ref[0, 1]
-
-    tgt_ref[core] = own_target[0, 0]
-    tgt_ref[1 - core] = mate_target[0, 0]
+    core = my_core()
+    own_meta = meta_of(own_tile)
+    mate_meta = meta_of(mate_tile)
+    own_rays = integer(own_meta[4])
+    mate_rays = integer(mate_meta[4])
+    even_count = integer(jnp.where(core == 0, own_meta[0], mate_meta[0]))
+    shift_x = own_meta[5]
+    shift_y = own_meta[6]
+
+    tgt_ref[core] = own_tile[...]
+    tgt_ref[1 - core] = mate_tile[...]
     img_ref[...] = jnp.zeros(img_ref.shape, F32)
     mom_acc[...] = jnp.zeros(mom_acc.shape, F32)
     col_acc[...] = jnp.zeros(col_acc.shape, F32)
@@ -159,9 +194,10 @@
     col = lax.broadcasted_iota(jnp.int32, (GB, GB), 1)
     perm = as_bf16((col == (row & (CHAINS - 1)) * STEPS + (row >> 3)).astype(F32))
 
-    def prepare(q, carry):
-        par = own_pick[q] + mate_pick[q]
-        par_ref[q] = par
+    for q in range(SEGS):
+        flat = own_pick[q : q + 1] + mate_pick[q : q + 1]
+        par = jnp.concatenate([flat[:, GB * p : GB * p + GB] for p in range(9)], axis=0)
+        par_ref[q, 0:9] = par
         mx = par[0:1] + shift_x
         my = par[1:2] + shift_y
         a, b, c, o = par[2:3], par[3:4], par[4:5], par[5:6]
@@ -183,9 +219,6 @@
         for ch in range(3):
             one = cols[:, ch : ch + 1] + cols[:, 8 + ch : 9 + ch] + cols[:, 16 + ch : 17 + ch]
             colb_ref[q, ch] = jnp.broadcast_to(one, (GB, 128))
-        return carry
-
-    lax.fori_loop(0, SEGS, prepare, 0)
 
     def task(index, carry):
         tile = index // (GROUPS // 2)
@@ -239,8 +272,12 @@
             resid = []
             for ch, value in enumerate((i0, i1, i2)):
                 value = value * live
-                img_ref[tile, ch : ch + 1, pl.ds(start, GRP)] = value
-                r = (value - tgt_ref[tile, ch : ch + 1, pl.ds(start, GRP)]) * live
+                base = CHUNKS * ch + LANES * group
+                goal = []
+                for v in range(LANES):
+                    img_ref[tile, pl.ds(base + v, 1), :] = value[:, 128 * v : 128 * v + 128]
+                    goal.append(tgt_ref[tile, pl.ds(base + v, 1), :])
+                r = (value - jnp.concatenate(goal, axis=1)) * live
                 resid.append(jnp.broadcast_to(r, (8, GRP)))
                 for n, piece in enumerate(pieces(r)):
                     for m in range(3):
@@ -301,7 +338,7 @@
 
     lax.fori_loop(0, GROUPS, task, 0)
 
-    def finish(q, carry):
+    for q in range(SEGS):
         par = par_ref[q]
         m = sum(dot(as_bf16(p), perm, ((0,), (0,))) for p in pieces(mom_acc[q]))
         g = sum(dot(as_bf16(p), perm, ((0,), (0,))) for p in pieces(col_acc[q]))
@@ -323,42 +360,37 @@
             -0.5 * square_y,
             m0 / o,
         ]
-        for i, value in enumerate(rows):
-            grad_ref[q, i : i + 1] = value
-        grad_ref[q, 6:9] = g[0:3] + g[8:11] + g[16:19]
-        grad_ref[q, 9:10] = own_pick[q, 9:10]
-        grad_ref[q, 10:16] = jnp.zeros((6, GB), F32)
-        return carry
-
-    lax.fori_loop(0, SEGS, finish, 0)
+        rows += [g[ch : ch + 1] + g[8 + ch : 9 + ch] + g[16 + ch : 17 + ch] for ch in range(3)]
+        block = own_pick[q : q + 1, PIX:]
+        home = jnp.floor(block * (1.0 / BLOCKS_DEV))
+        parity = home - 2.0 * jnp.floor(home * 0.5)
+        mine = parity == core.astype(F32)
+        for p, value in enumerate(rows):
+            at = (slice(q, q + 1), slice(GB * p, GB * p + GB))
+            keep_ref[at] = jnp.where(mine, value, 0.0)
+            send_ref[at] = jnp.where(mine, 0.0, value)
+        keep_ref[q : q + 1, PIX:] = block
+        send_ref[q : q + 1, PIX:] = jnp.zeros((1, GB), F32)
     own_image[...] = img_ref[core]
     mate_image[...] = img_ref[1 - core]
-    for n in range(SEGS // 2):
-        keep_ref[n] = grad_ref[core * 2 + n]
-        send_ref[n] = grad_ref[(1 - core) * 2 + n]
-        send_ref[n, 9:10] = jnp.zeros((1, GB), F32)
-
-
-def gather_kernel(where_ref, own_ref, prev_ref, next_ref, own_out, mate_out, acc_ref):
-    core = where_ref[0]
-    cell = where_ref[3]
-    per_block = own_out.shape[0]
-    own_first = cell * per_block
-    even_first = (cell - core) * per_block
-    acc_ref[...] = jnp.zeros(acc_ref.shape, F32)
-    names = []
-    for ref in (own_ref, prev_ref, next_ref):
-        for s in range(ref.shape[0]):
-            block = ref[s, 9:10, 0:1][0, 0].astype(jnp.int32)
-            names.append((ref, s, block - even_first))
-    for ref, s, spot in names:
-
-        @pl.when((spot >= 0) & (spot < 2 * per_block))
-        def _():
-            acc_ref[spot] += ref[s, 0:9]
-
-    own_out[...] = acc_ref[pl.ds(core * per_block, per_block)]
-    mate_out[...] = acc_ref[pl.ds((1 - core) * per_block, per_block)]
+
+
+def gather_kernel(own_ref, prev_ref, next_ref, own_image, mate_image, image_ref, out_ref):
+    per_block = out_ref.shape[1]
+    first = (lax.axis_index("cell") * per_block).astype(F32)
+    for ch in range(3):
+        for n in range(CHUNKS):
+            at = slice(CHUNKS * ch + n, CHUNKS * ch + n + 1)
+            image_ref[ch, :, 128 * n : 128 * n + 128] = own_image[at] + mate_image[at]
+    slots = own_ref.shape[0]
+    spot = lax.broadcasted_iota(jnp.int32, (slots, per_block), 1).astype(F32) + first
+    refs = (own_ref, prev_ref, next_ref)
+    hot = [as_bf16((ref[:, PIX : PIX + 1] == spot).astype(F32)) for ref in refs]
+    hot = jnp.concatenate(hot, axis=0)
+    for p in range(9):
+        at = (slice(None), slice(GB * p, GB * p + GB))
+        values = jnp.concatenate([ref[at] for ref in refs], axis=0)
+        out_ref[p] = sum(dot(hot, as_bf16(v), ((0,), (0,))) for v in pieces(values))
 
 
 def smem():
@@ -382,30 +414,48 @@
     return jax.ShapeDtypeStruct(dims, F32)
 
 
-def pick_call(where, own_meta, mate_meta, own, prev, after):
+def vmem_shape(*dims):
+    return pltpu.VMEM(dims, F32)
+
+
+def near(x):
+    return pltpu.with_memory_space_constraint(x, pltpu.VMEM)
+
+
+def pack_call(seg_count, seg_block, ray_count, camera_shift, target):
+    return pl.pallas_call(
+        pack_kernel,
+        out_shape=vmem_shape(ROWS + 2, 128),
+        in_specs=[smem()] * 4 + [vmem()],
+        out_specs=vmem(),
+        name="pack",
+    )(seg_count, seg_block, ray_count, camera_shift, target)
+
+
+def pick_call(own_tile, mate_tile, own, prev, after):
     return pl.pallas_call(
         pick_kernel,
-        out_shape=shape(SEGS, 16, GB),
-        in_specs=[smem()] * 3 + [vmem()] * 3,
+        out_shape=vmem_shape(SEGS, PIX + GB),
+        in_specs=[vmem()] * 5,
         out_specs=vmem(),
         name="pick",
-    )(where, own_meta, mate_meta, own, prev, after)
-
-
-def main_call(where, own_meta, mate_meta, shift, own_pick, mate_pick, own_target, mate_target):
+    )(near(own_tile), near(mate_tile), own, near(prev), near(after))
+
+
+def main_call(own_pick, mate_pick, own_tile, mate_tile):
     feats, moments = pixel_features()
     return pl.pallas_call(
         main_kernel,
-        out_shape=(shape(3, PIX), shape(3, PIX), shape(2, 16, GB), shape(2, 16, GB)),
-        in_specs=[smem()] * 4 + [vmem()] * 6,
+        out_shape=(vmem_shape(ROWS, 128),) * 2 + (vmem_shape(SEGS, PIX + GB),) * 2,
+        in_specs=[vmem()] * 6,
         out_specs=(vmem(),) * 4,
         scratch_shapes=[
             pltpu.VMEM((SEGS, 16, GB), F32),
             pltpu.VMEM((SEGS, GB, 48), BF16),
             pltpu.VMEM((SEGS, GB, 72), BF16),
             pltpu.VMEM((SEGS, 3, GB, 128), F32),
-            pltpu.VMEM((2, 3, PIX), F32),
-            pltpu.VMEM((2, 3, PIX), F32),
+            pltpu.VMEM((2, ROWS + 2, 128), F32),
+            pltpu.VMEM((2, ROWS, 128), F32),
             pltpu.VMEM((GB, GRP), F32),
             pltpu.VMEM((SEG_MAX, GB, GRP), F32),
             pltpu.VMEM((SEG_MAX, GB, GRP), F32),
@@ -417,56 +467,54 @@
             pltpu.VMEM((GB, GRP), BF16),
             pltpu.VMEM((SEGS, GB, 16), F32),
             pltpu.VMEM((SEGS, GB, 24), F32),
-            pltpu.VMEM((SEGS, 16, GB), F32),
         ],
         name="splat",
     )(
-        where,
-        own_meta,
-        mate_meta,
-        shift,
-        own_pick,
-        mate_pick,
-        own_target,
-        mate_target,
+        near(own_pick),
+        near(mate_pick),
+        near(own_tile),
+        near(mate_tile),
         jnp.asarray(feats),
         jnp.asarray(moments),
     )
 
 
-def gather_call(where, own, prev, after, per_block):
+def gather_call(own, prev, after, own_image, mate_image, per_block):
     return pl.pallas_call(
         gather_kernel,
-        out_shape=(shape(per_block, 9, GB), shape(per_block, 9, GB)),
-        in_specs=[smem()] + [vmem()] * 3,
-        out_specs=(vmem(),) * 2,
-        scratch_shapes=[pltpu.VMEM((2 * per_block, 9, GB), F32)],
+        grid=(1,),
+        out_shape=(shape(3, 1, PIX), shape(9, per_block, GB)),
+        in_specs=[vmem()] * 5,
+        out_specs=(
+            pl.BlockSpec((3, 1, PIX), lambda i: (0, 0, 0)),
+            pl.BlockSpec((9, per_block, GB), lambda i: (0, 0, 0)),
+        ),
         name="gather",
-    )(where, own, prev, after)
+    )(near(own), near(prev), near(after), near(own_image), near(mate_image))
 
 
 def shards(gaussians, seg_count, seg_block, ray_count, camera_shift, target):
-    cell = lax.axis_index("cell")
-    chips = lax.axis_size("cell") // 2
-    where = jnp.stack([cell % 2, cell // 2, jnp.int32(chips), cell]).astype(jnp.int32)
-    own_meta = jnp.concatenate([seg_count[0], seg_block[0, 0], ray_count[0]])
-    mate_meta = mate(own_meta)
-    prev = shifted(gaussians, "cell", 2)
-    after = shifted(gaussians, "cell", -2)
-    mate_target = mate(target)
-    own_pick = pick_call(where, own_meta, mate_meta, gaussians, prev, after)
+    table = gaussians.transpose(1, 0, 2)
+    prev = shifted(table, "cell", 2)
+    after = shifted(table, "cell", -2)
+    tile = pack_call(seg_count, seg_block, ray_count, camera_shift, target[0].transpose(1, 0, 2))
+    mate_tile = mate(tile)
+    own_pick = pick_call(tile, mate_tile, table, prev, after)
     mate_pick = mate(own_pick)
-    own_image, mate_image, keep, send = main_call(
-        where, own_meta, mate_meta, camera_shift, own_pick, mate_pick, target, mate_target
-    )
+    own_image, mate_image, keep, send = main_call(own_pick, mate_pick, tile, mate_tile)
     grads = keep + mate(send)
-    image = own_image + mate(mate_image)
+    other_image = mate(mate_image)
     views = [grads] + [shifted(grads, "view", d) for d in (1, 2, 3)]
     stack = jnp.concatenate(views, axis=0)
-    own_out, mate_out = gather_call(
-        where, stack, shifted(stack, "cell", 2), shifted(stack, "cell", -2), gaussians.shape[0]
+    image, total = gather_call(
+        stack,
+        shifted(stack, "cell", 2),
+        shifted(stack, "cell", -2),
+        own_image,
+        other_image,
+        gaussians.shape[0],
     )
-    return image[None, None], own_out + mate(mate_out)
+    return image.transpose(1, 0, 2)[None], total.transpose(1, 0, 2)
 
 
 def solution(mesh):

time: 70.5 us -> 53.6 us (0.76)
  local copies, waits for them, and re-layouts: 5.67 us -> 0 us
  Pallas kernels: 19.5 us -> 14.7 us
  waiting for transfers between devices: 16.8 us -> 14.2 us
  other arithmetic: 2.45 us -> 0.05 us
  starting transfers between devices: 23.7 us -> 22.4 us
    unnamed x34 -> x0, local copies, waits for them, and re-layouts: 5.67 us -> none
    pallas_call x3 -> x4, Pallas kernels: 19.5 us -> 14.7 us  [the longest x1 11.8 us: main_call(): pl.pallas_call(main_kernel, out_shape=(vmem_shape(ROWS, 128),) * 2 + (vme...]
    ppermute x7, waiting for transfers between devices: 13.6 us -> 10.7 us  [shifted(): lax.ppermute(block, axis, [((i - distance) % size, i) for i in range(size)])]
    add x1 -> x0, other arithmetic: 0.99 us -> none  [shards(): return (image[None, None], own_out + mate(mate_out))]
    add x1, other arithmetic: 0.76 us -> 0.01 us  [shards(): grads = keep + mate(send)]
    ppermute x6 -> x4, starting transfers between devices: 9.62 us -> 8.88 us  [mate(): lax.ppermute(block, 'cell', [(i ^ 1, i) for i in range(lax.axis_size('cel...]
    ppermute x6 -> x4, waiting for transfers between devices: 3.2 us -> 3.45 us  [mate(): lax.ppermute(block, 'cell', [(i ^ 1, i) for i in range(lax.axis_size('cel...]
  transfers between devices with their start and end apart: 13 -> 11, of which waited for: 9 -> 8; matrix products, arithmetic and copies ran while one was open for 2% -> 0% of each run, Pallas kernels for 3% -> 1%
where the time goes in v2:
time: 53.6 us; the launch traced here: 53.3 us
  starting transfers between devices  22.4 us (42%)
  Pallas kernels  14.7 us (27%)
  waiting for transfers between devices  14.2 us (26%)
  between operations  1.98 us (4%)
    ppermute x7, starting transfers between devices, shifted(): lax.ppermute(block, axis, [((i - distance) % size, i) for i in range(size)])  13.5 us
    pallas_call x1, Pallas kernels, main_call(): pl.pallas_call(main_kernel, out_shape=(vmem_shape(ROWS, 128),) * 2 + (vme...  11.8 us
    ppermute x7, waiting for transfers between devices, shifted(): lax.ppermute(block, axis, [((i - distance) % size, i) for i in range(size)])  10.7 us
    ppermute x4, starting transfers between devices, mate(): lax.ppermute(block, 'cell', [(i ^ 1, i) for i in range(lax.axis_size('cel...  8.88 us
    ppermute x4, waiting for transfers between devices, mate(): lax.ppermute(block, 'cell', [(i ^ 1, i) for i in range(lax.axis_size('cel...  3.45 us
    pallas_call x1, Pallas kernels, pick_call(): pl.pallas_call(pick_kernel, out_shape=vmem_shape(SEGS, PIX + GB), in_spec...  1.19 us
  transfers between devices with their start and end apart: 11, of which 8 were waited for; matrix products, arithmetic and copies ran while one was open for 0% of the time, Pallas kernels for 1%

profile of v2, /device:TPU:1, one launch (start us, length us, event | category | flops | bytes accessed | tf_op | source)
XLA Modules:
  0.0 53.3 jit_solution(13683480969193450674)
XLA Ops:
  0.6 8.9 %collective-permute-start.2 = (f32[9,16,256]{2,1,0:T(8,128)}, f32[9,16,256]{2,1,0:T(8,128)S(1)}, u32[]{:S(2)}, u32[]{:S(2)}) collective-permute-start(f32[9,16,256]{2,1,0:T(8,128)} %bitcast.6), channel_id=1, source_target_pairs={{8,0},{12,4},{16,8},{20,12},{24,16},{28,20},{32,24},{36,28},{40,32... | collective-permute-start | bytes 442376 | tf_op jit(solution)/shard_map/ppermute | solution.py:406
  9.6 0.0 collective-permute-start.1
  10.9 0.8 %pack.1.own_tile = f32[56,128]{1,0:T(8,128)S(1)} custom-call(s32[1,1]{1,0:T(1,128)S(6)} %copy.11.count_ref, s32[1,1,3]{2,1,0:T(1,128)} %block_ref.1, s32[1,1]{1,0:T(1,128)S(6)} %copy.12.rays_ref, f32[1,2]{1,0:T(1,128)} %shift_ref.1, f32[3,1,2304]{2,1,0:T(1,128)} %bitcast.9), custom_call_target="tpu_custom_call" | custom-call | tf_op jit(solution)/shard_map/pack/pallas_call | solution.py:426
  11.6 1.0 %collective-permute-start = (f32[56,128]{1,0:T(8,128)S(1)}, f32[56,128]{1,0:T(8,128)S(1)}, u32[]{:S(2)}, u32[]{:S(2)}) collective-permute-start(f32[56,128]{1,0:T(8,128)S(1)} %pack.1.own_tile), channel_id=1, source_target_pairs={{4,0},{0,4},{12,8},{8,12},{20,16},{16,20},{28,24},{24,28},{36,32},... | collective-permute-start | bytes 86024 | tf_op jit(solution)/shard_map/ppermute | solution.py:410
  12.7 0.9 %collective-permute-done.mate_tile = f32[56,128]{1,0:T(8,128)S(1)} collective-permute-done((f32[56,128]{1,0:T(8,128)S(1)}, f32[56,128]{1,0:T(8,128)S(1)}, u32[]{:S(2)}, u32[]{:S(2)}) %collective-permute-start) | collective-permute-done | bytes 28704 | tf_op jit(solution)/shard_map/ppermute | solution.py:410
  13.5 0.0 collective-permute-done.2.next_ref
  13.5 4.0 %collective-permute-done.1.prev_ref = f32[9,16,256]{2,1,0:T(8,128)S(1)} collective-permute-done((f32[9,16,256]{2,1,0:T(8,128)}, f32[9,16,256]{2,1,0:T(8,128)S(1)}, u32[]{:S(2)}, u32[]{:S(2)}) %collective-permute-start.1) | collective-permute-done | bytes 147488 | tf_op jit(solution)/shard_map/ppermute | solution.py:406
  17.5 1.2 %pick.1.own_pick = f32[4,2560]{1,0:T(4,128)S(1)} custom-call(f32[56,128]{1,0:T(8,128)S(1)} %pack.1.own_tile, f32[56,128]{1,0:T(8,128)S(1)} %collective-permute-done.mate_tile, f32[9,16,256]{2,1,0:T(8,128)} %bitcast.8, f32[9,16,256]{2,1,0:T(8,128)S(1)} %collective-permute-done.1.prev_ref, f32[9,16,256]{2,1,0:T(8,128)S(1)} %collective-permute-done.2.next_ref), custom_call_target="tpu_custom_call" | custom-call | tf_op jit(solution)/shard_map/pick/pallas_call | solution.py:436
  18.7 1.9 %collective-permute-start.3 = (f32[4,2560]{1,0:T(4,128)S(1)}, f32[4,2560]{1,0:T(4,128)S(1)}, u32[]{:S(2)}, u32[]{:S(2)}) collective-permute-start(f32[4,2560]{1,0:T(4,128)S(1)} %pick.1.own_pick), channel_id=1, source_target_pairs={{4,0},{0,4},{12,8},{8,12},{20,16},{16,20},{28,24},{24,28},{36,32},... | collective-permute-start | bytes 122888 | tf_op jit(solution)/shard_map/ppermute | solution.py:410
  20.6 0.9 %collective-permute-done.3.mate_pick = f32[4,2560]{1,0:T(4,128)S(1)} collective-permute-done((f32[4,2560]{1,0:T(4,128)S(1)}, f32[4,2560]{1,0:T(4,128)S(1)}, u32[]{:S(2)}, u32[]{:S(2)}) %collective-permute-start.3) | collective-permute-done | bytes 40992 | tf_op jit(solution)/shard_map/ppermute | solution.py:410
  21.5 11.8 %splat.1 = (f32[54,128]{1,0:T(8,128)S(1)}, f32[54,128]{1,0:T(8,128)S(1)}, f32[4,2560]{1,0:T(4,128)S(1)}, f32[4,2560]{1,0:T(4,128)S(1)}) custom-call(f32[4,2560]{1,0:T(4,128)S(1)} %pick.1.own_pick, f32[4,2560]{1,0:T(4,128)S(1)} %collective-permute-done.3.mate_pick, f32[56,128]{1,0:T(8,128)S(1)} %pack.1.own_tile, ...), custom_call_target="tpu_custom_call" | custom-call | tf_op jit(solution)/shard_map/splat/pallas_call | solution.py:447
  33.3 3.3 %collective-permute-start.4 = (f32[4,2560]{1,0:T(4,128)S(1)}, f32[4,2560]{1,0:T(4,128)S(1)}, u32[]{:S(2)}, u32[]{:S(2)}) collective-permute-start(f32[4,2560]{1,0:T(4,128)S(1)} %get-tuple-element.9), channel_id=1, source_target_pairs={{4,0},{0,4},{12,8},{8,12},{20,16},{16,20},{28,24},{24,28},{36,32},... | collective-permute-start | bytes 122888 | tf_op jit(solution)/shard_map/ppermute | solution.py:410
  36.6 0.9 %collective-permute-done.4 = f32[4,2560]{1,0:T(4,128)S(1)} collective-permute-done((f32[4,2560]{1,0:T(4,128)S(1)}, f32[4,2560]{1,0:T(4,128)S(1)}, u32[]{:S(2)}, u32[]{:S(2)}) %collective-permute-start.4) | collective-permute-done | bytes 40992 | tf_op jit(solution)/shard_map/ppermute | solution.py:410
  37.5 0.1 collective-permute-start.7
  37.6 3.0 %collective-permute-start.6 = (f32[4,2560]{1,0:T(4,128)S(1)}, f32[4,2560]{1,0:T(4,128)S(1)}, u32[]{:S(2)}, u32[]{:S(2)}) collective-permute-start(f32[4,2560]{1,0:T(4,128)S(1)} %add.3), channel_id=1, source_target_pairs={{2,0},{3,1},{0,2},{1,3},{6,4},{7,5},{4,6},{5,7},{10,8},{11,9},{8,1... | collective-permute-start | bytes 122888 | tf_op jit(solution)/shard_map/ppermute | solution.py:406
  40.5 0.0 collective-permute-start.5
  40.5 0.0 collective-permute-done.7
  40.5 1.5 %collective-permute-done.6 = f32[4,2560]{1,0:T(4,128)S(1)} collective-permute-done((f32[4,2560]{1,0:T(4,128)S(1)}, f32[4,2560]{1,0:T(4,128)S(1)}, u32[]{:S(2)}, u32[]{:S(2)}) %collective-permute-start.6) | collective-permute-done | bytes 40992 | tf_op jit(solution)/shard_map/ppermute | solution.py:406
  42.0 2.6 %collective-permute-done.5 = f32[4,2560]{1,0:T(4,128)S(1)} collective-permute-done((f32[4,2560]{1,0:T(4,128)S(1)}, f32[4,2560]{1,0:T(4,128)S(1)}, u32[]{:S(2)}, u32[]{:S(2)}) %collective-permute-start.5) | collective-permute-done | bytes 40992 | tf_op jit(solution)/shard_map/ppermute | solution.py:406
  44.6 0.1 collective-permute-start.9
  44.7 1.5 %collective-permute-start.8 = (f32[16,2560]{1,0:T(8,128)S(1)}, f32[16,2560]{1,0:T(8,128)S(1)}, u32[]{:S(2)}, u32[]{:S(2)}) collective-permute-start(f32[16,2560]{1,0:T(8,128)S(1)} %pad_maximum_fusion.own_ref), channel_id=1, source_target_pairs={{248,0},{252,4},{0,8},{4,12},{8,16},{12,20},{16,24},{20,28},{24,32... | collective-permute-start | bytes 491528 | tf_op jit(solution)/shard_map/ppermute | solution.py:406
  46.2 2.6 %collective-permute-start.10 = (f32[54,128]{1,0:T(8,128)S(1)}, f32[54,128]{1,0:T(8,128)S(1)}, u32[]{:S(2)}, u32[]{:S(2)}) collective-permute-start(f32[54,128]{1,0:T(8,128)S(1)} %get-tuple-element.11), channel_id=1, source_target_pairs={{4,0},{0,4},{12,8},{8,12},{20,16},{16,20},{28,24},{24,28},{36,32},... | collective-permute-start | bytes 82952 | tf_op jit(solution)/shard_map/ppermute | solution.py:410
  48.8 0.9 %collective-permute-done.10.mate_image = f32[54,128]{1,0:T(8,128)S(1)} collective-permute-done((f32[54,128]{1,0:T(8,128)S(1)}, f32[54,128]{1,0:T(8,128)S(1)}, u32[]{:S(2)}, u32[]{:S(2)}) %collective-permute-start.10) | collective-permute-done | bytes 27680 | tf_op jit(solution)/shard_map/ppermute | solution.py:410
  49.7 0.0 collective-permute-done.9.next_ref
  49.7 2.6 %collective-permute-done.8.prev_ref = f32[16,2560]{1,0:T(8,128)S(1)} collective-permute-done((f32[16,2560]{1,0:T(8,128)S(1)}, f32[16,2560]{1,0:T(8,128)S(1)}, u32[]{:S(2)}, u32[]{:S(2)}) %collective-permute-start.8) | collective-permute-done | bytes 163872 | tf_op jit(solution)/shard_map/ppermute | solution.py:406
  52.3 1.0 %gather.1 = (f32[3,1,2304]{2,1,0:T(1,128)}, f32[9,16,256]{2,1,0:T(8,128)}) custom-call(f32[16,2560]{1,0:T(8,128)S(1)} %pad_maximum_fusion.own_ref, f32[16,2560]{1,0:T(8,128)S(1)} %collective-permute-done.8.prev_ref, f32[16,2560]{1,0:T(8,128)S(1)} %collective-permute-done.9.next_ref, f32[54,128]{1,0:T(8,128)S(1)} %get-tuple-element.10.own_image, ...), custom_call_target="tpu_custom_call" | custom-call | tf_op jit(solution)/shard_map/gather/pallas_call | solution.py:483
  (2 shorter events, 0.1 us)
Async XLA Ops:
  0.6 12.9 %collective-permute-start.2 = (f32[9,16,256]{2,1,0:T(8,128)}, f32[9,16,256]{2,1,0:T(8,128)S(1)}, u32[]{:S(2)}, u32[]{:S(2)}) collective-permute-start(f32[9,16,256]{2,1,0:T(8,128)} %bitcast.6), channel_id=1, source_target_pairs={{8,0},{12,4},{16,8},{20,12},{24,16},{28,20},{32,24},{36,28},{40,32... | collective-permute-start | bytes 442376 | tf_op jit(solution)/shard_map/ppermute | solution.py:406
  9.6 8.0 %collective-permute-start.1 = (f32[9,16,256]{2,1,0:T(8,128)}, f32[9,16,256]{2,1,0:T(8,128)S(1)}, u32[]{:S(2)}, u32[]{:S(2)}) collective-permute-start(f32[9,16,256]{2,1,0:T(8,128)} %bitcast.7), channel_id=1, source_target_pairs={{248,0},{252,4},{0,8},{4,12},{8,16},{12,20},{16,24},{20,28},{24,32... | collective-permute-start | bytes 442376 | tf_op jit(solution)/shard_map/ppermute | solution.py:406
  11.6 1.9 %collective-permute-start = (f32[56,128]{1,0:T(8,128)S(1)}, f32[56,128]{1,0:T(8,128)S(1)}, u32[]{:S(2)}, u32[]{:S(2)}) collective-permute-start(f32[56,128]{1,0:T(8,128)S(1)} %pack.1.own_tile), channel_id=1, source_target_pairs={{4,0},{0,4},{12,8},{8,12},{20,16},{16,20},{28,24},{24,28},{36,32},... | collective-permute-start | bytes 86024 | tf_op jit(solution)/shard_map/ppermute | solution.py:410
  18.7 2.8 %collective-permute-start.3 = (f32[4,2560]{1,0:T(4,128)S(1)}, f32[4,2560]{1,0:T(4,128)S(1)}, u32[]{:S(2)}, u32[]{:S(2)}) collective-permute-start(f32[4,2560]{1,0:T(4,128)S(1)} %pick.1.own_pick), channel_id=1, source_target_pairs={{4,0},{0,4},{12,8},{8,12},{20,16},{16,20},{28,24},{24,28},{36,32},... | collective-permute-start | bytes 122888 | tf_op jit(solution)/shard_map/ppermute | solution.py:410
  33.3 4.2 %collective-permute-start.4 = (f32[4,2560]{1,0:T(4,128)S(1)}, f32[4,2560]{1,0:T(4,128)S(1)}, u32[]{:S(2)}, u32[]{:S(2)}) collective-permute-start(f32[4,2560]{1,0:T(4,128)S(1)} %get-tuple-element.9), channel_id=1, source_target_pairs={{4,0},{0,4},{12,8},{8,12},{20,16},{16,20},{28,24},{24,28},{36,32},... | collective-permute-start | bytes 122888 | tf_op jit(solution)/shard_map/ppermute | solution.py:410
  37.5 3.1 %collective-permute-start.7 = (f32[4,2560]{1,0:T(4,128)S(1)}, f32[4,2560]{1,0:T(4,128)S(1)}, u32[]{:S(2)}, u32[]{:S(2)}) collective-permute-start(f32[4,2560]{1,0:T(4,128)S(1)} %add.3), channel_id=1, source_target_pairs={{1,0},{2,1},{3,2},{0,3},{5,4},{6,5},{7,6},{4,7},{9,8},{10,9},{11,1... | collective-permute-start | bytes 122888 | tf_op jit(solution)/shard_map/ppermute | solution.py:406
  37.6 4.4 %collective-permute-start.6 = (f32[4,2560]{1,0:T(4,128)S(1)}, f32[4,2560]{1,0:T(4,128)S(1)}, u32[]{:S(2)}, u32[]{:S(2)}) collective-permute-start(f32[4,2560]{1,0:T(4,128)S(1)} %add.3), channel_id=1, source_target_pairs={{2,0},{3,1},{0,2},{1,3},{6,4},{7,5},{4,6},{5,7},{10,8},{11,9},{8,1... | collective-permute-start | bytes 122888 | tf_op jit(solution)/shard_map/ppermute | solution.py:406
  40.5 4.1 %collective-permute-start.5 = (f32[4,2560]{1,0:T(4,128)S(1)}, f32[4,2560]{1,0:T(4,128)S(1)}, u32[]{:S(2)}, u32[]{:S(2)}) collective-permute-start(f32[4,2560]{1,0:T(4,128)S(1)} %add.3), channel_id=1, source_target_pairs={{3,0},{0,1},{1,2},{2,3},{7,4},{4,5},{5,6},{6,7},{11,8},{8,9},{9,10... | collective-permute-start | bytes 122888 | tf_op jit(solution)/shard_map/ppermute | solution.py:406
  44.6 5.0 %collective-permute-start.9 = (f32[16,2560]{1,0:T(8,128)S(1)}, f32[16,2560]{1,0:T(8,128)S(1)}, u32[]{:S(2)}, u32[]{:S(2)}) collective-permute-start(f32[16,2560]{1,0:T(8,128)S(1)} %pad_maximum_fusion.own_ref), channel_id=1, source_target_pairs={{8,0},{12,4},{16,8},{20,12},{24,16},{28,20},{32,24},{36,28},{40,32... | collective-permute-start | bytes 491528 | tf_op jit(solution)/shard_map/ppermute | solution.py:406
  44.7 7.6 %collective-permute-start.8 = (f32[16,2560]{1,0:T(8,128)S(1)}, f32[16,2560]{1,0:T(8,128)S(1)}, u32[]{:S(2)}, u32[]{:S(2)}) collective-permute-start(f32[16,2560]{1,0:T(8,128)S(1)} %pad_maximum_fusion.own_ref), channel_id=1, source_target_pairs={{248,0},{252,4},{0,8},{4,12},{8,16},{12,20},{16,24},{20,28},{24,32... | collective-permute-start | bytes 491528 | tf_op jit(solution)/shard_map/ppermute | solution.py:406
  46.2 3.5 %collective-permute-start.10 = (f32[54,128]{1,0:T(8,128)S(1)}, f32[54,128]{1,0:T(8,128)S(1)}, u32[]{:S(2)}, u32[]{:S(2)}) collective-permute-start(f32[54,128]{1,0:T(8,128)S(1)} %get-tuple-element.11), channel_id=1, source_target_pairs={{4,0},{0,4},{12,8},{8,12},{20,16},{16,20},{28,24},{24,28},{36,32},... | collective-permute-start | bytes 82952 | tf_op jit(solution)/shard_map/ppermute | solution.py:410

commit v3 on v2

--- a/solution.py
+++ b/solution.py
@@ -18,7 +18,7 @@
 ROWS = 3 * PIX // 128
 CHUNKS = PIX // 128
 LANES = GRP // 128
-CHAINS = 8
+CHAINS = 16
 STEPS = GB // CHAINS
 LOG2E = math.log2(math.e)
 F32 = jnp.float32
@@ -42,9 +42,8 @@
     xx, xy, yy = split(x * x), split(x * y), split(y * y)
     first = np.stack([np.ones_like(x), x, y, xx[0], xy[0], yy[0], zero, zero])
     second = np.stack([zero, zero, zero, xx[1], xy[1], yy[1], zero, zero])
-    feats = np.concatenate([first] * 3 + [second] * 3)
-    moments = np.concatenate([first, second])
-    return feats.astype(jnp.bfloat16), moments.astype(jnp.bfloat16)
+    feats = np.concatenate([first, second] * 3 + [np.zeros((24, PIX))])
+    return feats.astype(jnp.bfloat16)
 
 
 def pieces(x):
@@ -151,7 +150,6 @@
     own_tile,
     mate_tile,
     feats_ref,
-    mom_ref,
     own_image,
     mate_image,
     keep_ref,
@@ -163,16 +161,20 @@
     tgt_ref,
     img_ref,
     e_ref,
+    u_ref,
     alpha_ref,
     w_ref,
     chain_ref,
     r_ref,
-    hh_ref,
-    hl_ref,
-    wh_ref,
-    wl_ref,
-    mom_acc,
-    col_acc,
+    hwa_ref,
+    hwb_ref,
+    rmat_ref,
+    resid_ref,
+    after_ref,
+    rhs_ref,
+    acc_ref,
+    pend_ref,
+    tr_ref,
 ):
     core = my_core()
     own_meta = meta_of(own_tile)
@@ -186,13 +188,20 @@
     tgt_ref[core] = own_tile[...]
     tgt_ref[1 - core] = mate_tile[...]
     img_ref[...] = jnp.zeros(img_ref.shape, F32)
-    mom_acc[...] = jnp.zeros(mom_acc.shape, F32)
-    col_acc[...] = jnp.zeros(col_acc.shape, F32)
+    acc_ref[...] = jnp.zeros(acc_ref.shape, F32)
     r_ref[...] = jnp.zeros(r_ref.shape, F32)
-
-    row = lax.broadcasted_iota(jnp.int32, (GB, GB), 0)
-    col = lax.broadcasted_iota(jnp.int32, (GB, GB), 1)
-    perm = as_bf16((col == (row & (CHAINS - 1)) * STEPS + (row >> 3)).astype(F32))
+    hwa_ref[...] = jnp.zeros(hwa_ref.shape, BF16)
+    rhs_ref[...] = jnp.zeros(rhs_ref.shape, BF16)
+    pend_ref[0] = 0
+    pend_ref[1] = 1
+    pend_ref[2] = 0
+    row = lax.broadcasted_iota(jnp.int32, (72, 3 * 128), 0)
+    lane = lax.broadcasted_iota(jnp.int32, (72, 3 * 128), 1)
+    spread = as_bf16(((row >= 48) & ((row & 7) == lane // 128)).astype(F32))
+    pad = jnp.zeros((56, GB), F32)
+
+    def step_rows(s):
+        return pl.ds(s, CHAINS, STEPS)
 
     for q in range(SEGS):
         flat = own_pick[q : q + 1] + mate_pick[q : q + 1]
@@ -208,17 +217,19 @@
         k = jnp.concatenate(
             [k0, k1, k2, (-0.5 * LOG2E) * a, -LOG2E * b, (-0.5 * LOG2E) * c, zero, zero], axis=0
         )
+        colour = jnp.concatenate([par[6:9], jnp.zeros((5, GB), F32)], axis=0)
         ka, kb, kc = pieces(k)
-        coef = as_bf16(jnp.concatenate([ka, kb, kc, ka, kb, kc], axis=0))
-        exp_ref[q] = as_bf16(dot(perm, coef, ((1,), (1,))))
-        colour = jnp.concatenate([par[6:9], jnp.zeros((5, GB), F32)], axis=0)
         ca, cb, cc = pieces(colour)
-        coef = as_bf16(jnp.concatenate([ca, cb, cc] * 3, axis=0))
-        cols = dot(perm, coef, ((1,), (1,)))
-        col_ref[q] = as_bf16(cols)
-        for ch in range(3):
-            one = cols[:, ch : ch + 1] + cols[:, 8 + ch : 9 + ch] + cols[:, 16 + ch : 17 + ch]
-            colb_ref[q, ch] = jnp.broadcast_to(one, (GB, 128))
+        tr_ref[0] = jnp.concatenate([ka, ka, kb, kb, kc, kc, ca, cb, cc, pad], axis=0).T
+        tr_ref[1] = jnp.concatenate([ca, cb, cc] * 3 + [pad], axis=0).T
+        for s in range(STEPS):
+            rows = slice(CHAINS * s, CHAINS * s + CHAINS)
+            exp_ref[q, rows] = as_bf16(tr_ref[0, step_rows(s)][:, :72])
+            col_ref[q, rows] = as_bf16(tr_ref[1, step_rows(STEPS - 1 - s)][:, :72])
+        colb_ref[q] = dot(exp_ref[q], spread, ((1,), (0,)))
+
+    def flush(hw_ref):
+        acc_ref[pend_ref[0]] += dot(rhs_ref[pend_ref[1]], hw_ref[...], ((1,), (1,)))
 
     def task(index, carry):
         tile = index // (GROUPS // 2)
@@ -236,12 +247,13 @@
                 before, i0, i1, i2 = carry
                 q = first + k
                 e_ref[...] = dot(exp_ref[q], feats, ((1,), (0,)))
-                t = [jnp.ones((8, 128), F32)] * LANES
-                acc = [[jnp.zeros((8, 128), F32)] * LANES for _ in range(3)]
+                t = [jnp.ones((CHAINS, 128), F32)] * LANES
+                acc = [[jnp.zeros((CHAINS, 128), F32)] * LANES for _ in range(3)]
                 for j in range(STEPS):
-                    cols = [colb_ref[q, ch, 8 * j : 8 * j + 8] for ch in range(3)]
+                    rows = slice(CHAINS * j, CHAINS * j + CHAINS)
+                    cols = [colb_ref[q, rows, 128 * ch : 128 * ch + 128] for ch in range(3)]
                     for v in range(LANES):
-                        at = (slice(8 * j, 8 * j + 8), slice(128 * v, 128 * v + 128))
+                        at = (rows, slice(128 * v, 128 * v + 128))
                         alpha = jnp.exp2(e_ref[at])
                         w = alpha * t[v]
                         t[v] = t[v] - w
@@ -251,7 +263,7 @@
                             acc[ch][v] = acc[ch][v] + w * cols[ch]
                 through = jnp.concatenate(t, axis=1)
                 scan = through
-                for n in (1, 2, 4):
+                for n in (1, 2, 4, 8):
                     scan = scan * down(scan, n, 1.0)
                 begin = before * down(scan, 1, 1.0)
                 chain_ref[k, 3] = through
@@ -265,11 +277,10 @@
 
             blank = jnp.zeros((1, GRP), F32)
             _, i0, i1, i2 = lax.fori_loop(
-                0, count, forward, (jnp.ones((8, GRP), F32), blank, blank, blank)
+                0, count, forward, (jnp.ones((CHAINS, GRP), F32), blank, blank, blank)
             )
             pixel = start + lax.broadcasted_iota(jnp.int32, (1, GRP), 1)
             live = (pixel < rays).astype(F32)
-            resid = []
             for ch, value in enumerate((i0, i1, i2)):
                 value = value * live
                 base = CHUNKS * ch + LANES * group
@@ -278,70 +289,84 @@
                     img_ref[tile, pl.ds(base + v, 1), :] = value[:, 128 * v : 128 * v + 128]
                     goal.append(tgt_ref[tile, pl.ds(base + v, 1), :])
                 r = (value - jnp.concatenate(goal, axis=1)) * live
-                resid.append(jnp.broadcast_to(r, (8, GRP)))
+                resid_ref[ch] = jnp.broadcast_to(r, (CHAINS, GRP))
                 for n, piece in enumerate(pieces(r)):
                     for m in range(3):
                         r_ref[24 * n + 8 * m + ch : 24 * n + 8 * m + ch + 1] = piece
-            rmat = as_bf16(r_ref[...])
-            rsum = jnp.concatenate([rmat[0:8], rmat[24:32], rmat[48:56]], axis=0)
-            moments = mom_ref[:, pl.ds(start, GRP)]
-
-            def backward(index, after):
+            rmat_ref[...] = as_bf16(r_ref[...])
+            after_ref[...] = jnp.zeros((CHAINS, GRP), F32)
+            rsum = as_bf16(jnp.concatenate([r_ref[0:8], r_ref[24:32], r_ref[48:56]], axis=0))
+            moments = feats_ref[0:16, pl.ds(start, GRP)]
+            side = 1 - pend_ref[1]
+            rhs_ref[side, 0:16, 0:GRP] = moments
+            rhs_ref[side, 0:16, GRP : 2 * GRP] = moments
+            rhs_ref[side, 16:40, 2 * GRP :] = rsum
+
+            def backward(index, carry):
                 k = count - 1 - index
                 q = first + k
-                e_ref[...] = dot(col_ref[q], rmat, ((1,), (0,)))
-                value = (
-                    resid[0] * chain_ref[k, 0]
-                    + resid[1] * chain_ref[k, 1]
-                    + resid[2] * chain_ref[k, 2]
-                )
-                scale = chain_ref[k, 3]
-                for n in (1, 2, 4):
-                    value = value + scale * up(value, n, 0.0)
-                    scale = scale * up(scale, n, 1.0)
-                entry = value + scale * after
-                rows = lax.broadcasted_iota(jnp.int32, entry.shape, 0)
-                leave = jnp.where(rows < CHAINS - 1, pltpu.roll(entry, CHAINS - 1, 0), after)
-                begin = chain_ref[k, 4]
-                behind = [leave[:, 128 * v : 128 * v + 128] for v in range(LANES)]
-                scale = [begin[:, 128 * v : 128 * v + 128] for v in range(LANES)]
-                for j in range(STEPS - 1, 0, -2):
-                    for v in range(LANES):
-                        ws, hs = [None, None], [None, None]
-                        for i in (1, 0):
-                            jj = j - 1 + i
-                            at = (slice(8 * jj, 8 * jj + 8), slice(128 * v, 128 * v + 128))
-                            d = e_ref[at] - behind[v]
-                            ws[i] = w_ref[(k,) + at] * scale[v]
-                            hs[i] = ws[i] * d
-                            behind[v] = behind[v] + alpha_ref[(k,) + at] * d
-                        at = (slice(8 * j - 8, 8 * j + 8), slice(128 * v, 128 * v + 128))
-                        w2 = jnp.concatenate(ws, axis=0)
-                        h2 = jnp.concatenate(hs, axis=0)
-                        wh = as_bf16(w2)
-                        hh = as_bf16(h2)
-                        wh_ref[at] = wh
-                        hh_ref[at] = hh
-                        wl_ref[at] = as_bf16(w2 - wh.astype(F32))
-                        hl_ref[at] = as_bf16(h2 - hh.astype(F32))
-                mom_acc[q] += dot(hh_ref[...], moments, ((1,), (1,))) + dot(
-                    hl_ref[...], moments, ((1,), (1,))
-                )
-                col_acc[q] += dot(wh_ref[...], rsum, ((1,), (1,))) + dot(
-                    wl_ref[...], rsum, ((1,), (1,))
-                )
-                return row_of(entry, 0)
-
-            lax.fori_loop(0, count, backward, jnp.zeros((8, GRP), F32))
+
+                def step(old_ref, new_ref):
+                    after = after_ref[...]
+                    u_ref[...] = dot(col_ref[q], rmat_ref[...], ((1,), (0,)))
+                    value = jnp.zeros((CHAINS, GRP), F32)
+                    for ch in range(3):
+                        value = value + resid_ref[ch] * chain_ref[k, ch]
+                    scale = chain_ref[k, 3]
+                    for n in (1, 2, 4, 8):
+                        value = value + scale * up(value, n, 0.0)
+                        scale = scale * up(scale, n, 1.0)
+                    entry = value + scale * after
+                    rows = lax.broadcasted_iota(jnp.int32, entry.shape, 0)
+                    leave = jnp.where(rows < CHAINS - 1, pltpu.roll(entry, CHAINS - 1, 0), after)
+                    begin = chain_ref[k, 4]
+                    behind = [leave[:, 128 * v : 128 * v + 128] for v in range(LANES)]
+                    scale = [begin[:, 128 * v : 128 * v + 128] for v in range(LANES)]
+                    flush(old_ref)
+                    for i in range(STEPS):
+                        rows = slice(CHAINS * i, CHAINS * i + CHAINS)
+                        j = CHAINS * (STEPS - 1 - i)
+                        for v in range(LANES):
+                            lanes = slice(128 * v, 128 * v + 128)
+                            at = (k, slice(j, j + CHAINS), lanes)
+                            d = u_ref[rows, lanes] - behind[v]
+                            w = w_ref[at] * scale[v]
+                            h = w * d
+                            behind[v] = behind[v] + alpha_ref[at] * d
+                            high = as_bf16(h)
+                            new_ref[rows, 128 * v : 128 * v + 128] = high
+                            low = as_bf16(h - high.astype(F32))
+                            new_ref[rows, GRP + 128 * v : GRP + 128 * v + 128] = low
+                            wide = as_bf16(w)
+                            new_ref[rows, 2 * GRP + 128 * v : 2 * GRP + 128 * v + 128] = wide
+                    after_ref[...] = row_of(entry, 0)
+
+                turn = pend_ref[2]
+                pl.when(turn == 0)(lambda: step(hwa_ref, hwb_ref))
+                pl.when(turn == 1)(lambda: step(hwb_ref, hwa_ref))
+                pend_ref[0] = q
+                pend_ref[1] = side
+                pend_ref[2] = 1 - turn
+                return carry
+
+            lax.fori_loop(0, count, backward, 0)
 
         return carry
 
     lax.fori_loop(0, GROUPS, task, 0)
-
+    pl.when(pend_ref[2] == 0)(lambda: flush(hwa_ref))
+    pl.when(pend_ref[2] == 1)(lambda: flush(hwb_ref))
+
+    moved = []
+    for n in range(SEGS // 2):
+        both = [acc_ref[2 * n], acc_ref[2 * n + 1], jnp.zeros((32, GB), F32)]
+        both = jnp.concatenate(both, axis=0).T
+        for s in range(STEPS):
+            tr_ref[n, step_rows(STEPS - 1 - s)] = both[CHAINS * s : CHAINS * s + CHAINS]
+        moved.append(tr_ref[n].T)
     for q in range(SEGS):
         par = par_ref[q]
-        m = sum(dot(as_bf16(p), perm, ((0,), (0,))) for p in pieces(mom_acc[q]))
-        g = sum(dot(as_bf16(p), perm, ((0,), (0,))) for p in pieces(col_acc[q]))
+        m = moved[q // 2][48 * (q % 2) : 48 * (q % 2) + 48]
         mx = par[0:1] + shift_x
         my = par[1:2] + shift_y
         a, b, c, o = par[2:3], par[3:4], par[4:5], par[5:6]
@@ -360,7 +385,7 @@
             -0.5 * square_y,
             m0 / o,
         ]
-        rows += [g[ch : ch + 1] + g[8 + ch : 9 + ch] + g[16 + ch : 17 + ch] for ch in range(3)]
+        rows += [m[16 + ch : 17 + ch] + m[24 + ch : 25 + ch] + m[32 + ch : 33 + ch] for ch in range(3)]
         block = own_pick[q : q + 1, PIX:]
         home = jnp.floor(block * (1.0 / BLOCKS_DEV))
         parity = home - 2.0 * jnp.floor(home * 0.5)
@@ -443,30 +468,33 @@
 
 
 def main_call(own_pick, mate_pick, own_tile, mate_tile):
-    feats, moments = pixel_features()
     return pl.pallas_call(
         main_kernel,
         out_shape=(vmem_shape(ROWS, 128),) * 2 + (vmem_shape(SEGS, PIX + GB),) * 2,
-        in_specs=[vmem()] * 6,
+        in_specs=[vmem()] * 5,
         out_specs=(vmem(),) * 4,
         scratch_shapes=[
             pltpu.VMEM((SEGS, 16, GB), F32),
-            pltpu.VMEM((SEGS, GB, 48), BF16),
             pltpu.VMEM((SEGS, GB, 72), BF16),
-            pltpu.VMEM((SEGS, 3, GB, 128), F32),
+            pltpu.VMEM((SEGS, GB, 72), BF16),
+            pltpu.VMEM((SEGS, GB, 3 * 128), F32),
             pltpu.VMEM((2, ROWS + 2, 128), F32),
             pltpu.VMEM((2, ROWS, 128), F32),
             pltpu.VMEM((GB, GRP), F32),
+            pltpu.VMEM((GB, GRP), F32),
             pltpu.VMEM((SEG_MAX, GB, GRP), F32),
             pltpu.VMEM((SEG_MAX, GB, GRP), F32),
-            pltpu.VMEM((SEG_MAX, 5, 8, GRP), F32),
+            pltpu.VMEM((SEG_MAX, 5, CHAINS, GRP), F32),
             pltpu.VMEM((72, GRP), F32),
-            pltpu.VMEM((GB, GRP), BF16),
-            pltpu.VMEM((GB, GRP), BF16),
-            pltpu.VMEM((GB, GRP), BF16),
-            pltpu.VMEM((GB, GRP), BF16),
-            pltpu.VMEM((SEGS, GB, 16), F32),
-            pltpu.VMEM((SEGS, GB, 24), F32),
+            pltpu.VMEM((GB, 3 * GRP), BF16),
+            pltpu.VMEM((GB, 3 * GRP), BF16),
+            pltpu.VMEM((72, GRP), BF16),
+            pltpu.VMEM((3, CHAINS, GRP), F32),
+            pltpu.VMEM((CHAINS, GRP), F32),
+            pltpu.VMEM((2, 48, 3 * GRP), BF16),
+            pltpu.VMEM((SEGS, 48, GB), F32),
+            pltpu.SMEM((3,), jnp.int32),
+            pltpu.VMEM((2, GB, 128), F32),
         ],
         name="splat",
     )(
@@ -474,8 +502,7 @@
         near(mate_pick),
         near(own_tile),
         near(mate_tile),
-        jnp.asarray(feats),
-        jnp.asarray(moments),
+        near(jnp.asarray(pixel_features())),
     )
 
 

time: 53.6 us -> 48.4 us (0.903)
  Pallas kernels: 14.7 us -> 9.71 us
  waiting for transfers between devices: 14.2 us -> 15.1 us
  starting transfers between devices: 22.4 us -> 21.7 us
    pallas_call x1, Pallas kernels: 11.8 us -> 6.76 us  [main_call(): pl.pallas_call(main_kernel, out_shape=(vmem_shape(ROWS, 128),) * 2 + (vme...]
    ppermute x7, waiting for transfers between devices: 10.7 us -> 11.7 us  [shifted(): lax.ppermute(block, axis, [((i - distance) % size, i) for i in range(size)])]
    ppermute x4, starting transfers between devices: 8.88 us -> 8.17 us  [mate(): lax.ppermute(block, 'cell', [(i ^ 1, i) for i in range(lax.axis_size('cel...]
  transfers between devices with their start and end apart: 11 -> 11, of which waited for: 8 -> 8; matrix products, arithmetic and copies ran while one was open for 0% -> 0% of each run, Pallas kernels for 1% -> 2%
where the time goes in v3:
time: 48.4 us; the launch traced here: 48.6 us
  starting transfers between devices  21.7 us (45%)
  waiting for transfers between devices  15.1 us (31%)
  Pallas kernels  9.71 us (20%)
  between operations  1.98 us (4%)
    ppermute x7, starting transfers between devices, shifted(): lax.ppermute(block, axis, [((i - distance) % size, i) for i in range(size)])  13.5 us
    ppermute x7, waiting for transfers between devices, shifted(): lax.ppermute(block, axis, [((i - distance) % size, i) for i in range(size)])  11.7 us
    ppermute x4, starting transfers between devices, mate(): lax.ppermute(block, 'cell', [(i ^ 1, i) for i in range(lax.axis_size('cel...  8.17 us
    pallas_call x1, Pallas kernels, main_call(): pl.pallas_call(main_kernel, out_shape=(vmem_shape(ROWS, 128),) * 2 + (vme...  6.76 us
    ppermute x4, waiting for transfers between devices, mate(): lax.ppermute(block, 'cell', [(i ^ 1, i) for i in range(lax.axis_size('cel...  3.45 us
    pallas_call x1, Pallas kernels, pick_call(): pl.pallas_call(pick_kernel, out_shape=vmem_shape(SEGS, PIX + GB), in_spec...  1.18 us
    pallas_call x1, Pallas kernels, gather_call(): pl.pallas_call(gather_kernel, grid=(1,), out_shape=(shape(3, 1, PIX), sha...  1.01 us
  transfers between devices with their start and end apart: 11, of which 8 were waited for; matrix products, arithmetic and copies ran while one was open for 0% of the time, Pallas kernels for 2%

profile of v3, /device:TPU:1, one launch (start us, length us, event | category | flops | bytes accessed | tf_op | source)
XLA Modules:
  0.0 48.6 jit_solution(10136279381867772270)
XLA Ops:
  0.6 0.0 copy-start
  0.6 8.9 %collective-permute-start.2 = (f32[9,16,256]{2,1,0:T(8,128)}, f32[9,16,256]{2,1,0:T(8,128)S(1)}, u32[]{:S(2)}, u32[]{:S(2)}) collective-permute-start(f32[9,16,256]{2,1,0:T(8,128)} %bitcast.6), channel_id=1, source_target_pairs={{8,0},{12,4},{16,8},{20,12},{24,16},{28,20},{32,24},{36,28},{40,32... | collective-permute-start | bytes 442376 | tf_op jit(solution)/shard_map/ppermute | solution.py:431
  9.6 0.0 collective-permute-start.1
  10.9 0.8 %pack.1.own_tile = f32[56,128]{1,0:T(8,128)S(1)} custom-call(s32[1,1]{1,0:T(1,128)S(6)} %copy.10.count_ref, s32[1,1,3]{2,1,0:T(1,128)} %block_ref.1, s32[1,1]{1,0:T(1,128)S(6)} %copy.11.rays_ref, f32[1,2]{1,0:T(1,128)} %shift_ref.1, f32[3,1,2304]{2,1,0:T(1,128)} %bitcast.9), custom_call_target="tpu_custom_call" | custom-call | tf_op jit(solution)/shard_map/pack/pallas_call | solution.py:451
  11.6 1.0 %collective-permute-start = (f32[56,128]{1,0:T(8,128)S(1)}, f32[56,128]{1,0:T(8,128)S(1)}, u32[]{:S(2)}, u32[]{:S(2)}) collective-permute-start(f32[56,128]{1,0:T(8,128)S(1)} %pack.1.own_tile), channel_id=1, source_target_pairs={{4,0},{0,4},{12,8},{8,12},{20,16},{16,20},{28,24},{24,28},{36,32},... | collective-permute-start | bytes 86024 | tf_op jit(solution)/shard_map/ppermute | solution.py:435
  12.7 0.9 %collective-permute-done.mate_tile = f32[56,128]{1,0:T(8,128)S(1)} collective-permute-done((f32[56,128]{1,0:T(8,128)S(1)}, f32[56,128]{1,0:T(8,128)S(1)}, u32[]{:S(2)}, u32[]{:S(2)}) %collective-permute-start) | collective-permute-done | bytes 28704 | tf_op jit(solution)/shard_map/ppermute | solution.py:435
  13.5 0.0 collective-permute-done.2.next_ref
  13.5 4.0 %collective-permute-done.1.prev_ref = f32[9,16,256]{2,1,0:T(8,128)S(1)} collective-permute-done((f32[9,16,256]{2,1,0:T(8,128)}, f32[9,16,256]{2,1,0:T(8,128)S(1)}, u32[]{:S(2)}, u32[]{:S(2)}) %collective-permute-start.1) | collective-permute-done | bytes 147488 | tf_op jit(solution)/shard_map/ppermute | solution.py:431
  17.5 1.2 %pick.1.own_pick = f32[4,2560]{1,0:T(4,128)S(1)} custom-call(f32[56,128]{1,0:T(8,128)S(1)} %pack.1.own_tile, f32[56,128]{1,0:T(8,128)S(1)} %collective-permute-done.mate_tile, f32[9,16,256]{2,1,0:T(8,128)} %bitcast.8, f32[9,16,256]{2,1,0:T(8,128)S(1)} %collective-permute-done.1.prev_ref, f32[9,16,256]{2,1,0:T(8,128)S(1)} %collective-permute-done.2.next_ref), custom_call_target="tpu_custom_call" | custom-call | tf_op jit(solution)/shard_map/pick/pallas_call | solution.py:461
  18.7 1.9 %collective-permute-start.3 = (f32[4,2560]{1,0:T(4,128)S(1)}, f32[4,2560]{1,0:T(4,128)S(1)}, u32[]{:S(2)}, u32[]{:S(2)}) collective-permute-start(f32[4,2560]{1,0:T(4,128)S(1)} %pick.1.own_pick), channel_id=1, source_target_pairs={{4,0},{0,4},{12,8},{8,12},{20,16},{16,20},{28,24},{24,28},{36,32},... | collective-permute-start | bytes 122888 | tf_op jit(solution)/shard_map/ppermute | solution.py:435
  20.6 0.9 %collective-permute-done.3.mate_pick = f32[4,2560]{1,0:T(4,128)S(1)} collective-permute-done((f32[4,2560]{1,0:T(4,128)S(1)}, f32[4,2560]{1,0:T(4,128)S(1)}, u32[]{:S(2)}, u32[]{:S(2)}) %collective-permute-start.3) | collective-permute-done | bytes 40992 | tf_op jit(solution)/shard_map/ppermute | solution.py:435
  21.5 0.0 copy-done
  21.5 6.8 %splat.1 = (f32[54,128]{1,0:T(8,128)S(1)}, f32[54,128]{1,0:T(8,128)S(1)}, f32[4,2560]{1,0:T(4,128)S(1)}, f32[4,2560]{1,0:T(4,128)S(1)}) custom-call(f32[4,2560]{1,0:T(4,128)S(1)} %pick.1.own_pick, f32[4,2560]{1,0:T(4,128)S(1)} %collective-permute-done.3.mate_pick, f32[56,128]{1,0:T(8,128)S(1)} %pack.1.own_tile, ...), custom_call_target="tpu_custom_call" | custom-call | tf_op jit(solution)/shard_map/splat/pallas_call | solution.py:471
  28.3 3.1 %collective-permute-start.4 = (f32[4,2560]{1,0:T(4,128)S(1)}, f32[4,2560]{1,0:T(4,128)S(1)}, u32[]{:S(2)}, u32[]{:S(2)}) collective-permute-start(f32[4,2560]{1,0:T(4,128)S(1)} %get-tuple-element.9), channel_id=1, source_target_pairs={{4,0},{0,4},{12,8},{8,12},{20,16},{16,20},{28,24},{24,28},{36,32},... | collective-permute-start | bytes 122888 | tf_op jit(solution)/shard_map/ppermute | solution.py:435
  31.4 0.9 %collective-permute-done.4 = f32[4,2560]{1,0:T(4,128)S(1)} collective-permute-done((f32[4,2560]{1,0:T(4,128)S(1)}, f32[4,2560]{1,0:T(4,128)S(1)}, u32[]{:S(2)}, u32[]{:S(2)}) %collective-permute-start.4) | collective-permute-done | bytes 40992 | tf_op jit(solution)/shard_map/ppermute | solution.py:435
  32.3 1.9 %collective-permute-start.7 = (f32[4,2560]{1,0:T(4,128)S(1)}, f32[4,2560]{1,0:T(4,128)S(1)}, u32[]{:S(2)}, u32[]{:S(2)}) collective-permute-start(f32[4,2560]{1,0:T(4,128)S(1)} %add.3), channel_id=1, source_target_pairs={{1,0},{2,1},{3,2},{0,3},{5,4},{6,5},{7,6},{4,7},{9,8},{10,9},{11,1... | collective-permute-start | bytes 122888 | tf_op jit(solution)/shard_map/ppermute | solution.py:431
  34.1 1.2 %collective-permute-start.6 = (f32[4,2560]{1,0:T(4,128)S(1)}, f32[4,2560]{1,0:T(4,128)S(1)}, u32[]{:S(2)}, u32[]{:S(2)}) collective-permute-start(f32[4,2560]{1,0:T(4,128)S(1)} %add.3), channel_id=1, source_target_pairs={{2,0},{3,1},{0,2},{1,3},{6,4},{7,5},{4,6},{5,7},{10,8},{11,9},{8,1... | collective-permute-start | bytes 122888 | tf_op jit(solution)/shard_map/ppermute | solution.py:431
  35.3 0.0 collective-permute-start.5
  35.3 0.0 collective-permute-done.7
  35.3 3.2 %collective-permute-done.6 = f32[4,2560]{1,0:T(4,128)S(1)} collective-permute-done((f32[4,2560]{1,0:T(4,128)S(1)}, f32[4,2560]{1,0:T(4,128)S(1)}, u32[]{:S(2)}, u32[]{:S(2)}) %collective-permute-start.6) | collective-permute-done | bytes 40992 | tf_op jit(solution)/shard_map/ppermute | solution.py:431
  38.5 1.4 %collective-permute-done.5 = f32[4,2560]{1,0:T(4,128)S(1)} collective-permute-done((f32[4,2560]{1,0:T(4,128)S(1)}, f32[4,2560]{1,0:T(4,128)S(1)}, u32[]{:S(2)}, u32[]{:S(2)}) %collective-permute-start.5) | collective-permute-done | bytes 40992 | tf_op jit(solution)/shard_map/ppermute | solution.py:431
  39.9 0.1 collective-permute-start.9
  40.0 1.5 %collective-permute-start.8 = (f32[16,2560]{1,0:T(8,128)S(1)}, f32[16,2560]{1,0:T(8,128)S(1)}, u32[]{:S(2)}, u32[]{:S(2)}) collective-permute-start(f32[16,2560]{1,0:T(8,128)S(1)} %pad_maximum_fusion.own_ref), channel_id=1, source_target_pairs={{248,0},{252,4},{0,8},{4,12},{8,16},{12,20},{16,24},{20,28},{24,32... | collective-permute-start | bytes 491528 | tf_op jit(solution)/shard_map/ppermute | solution.py:431
  41.5 2.1 %collective-permute-start.10 = (f32[54,128]{1,0:T(8,128)S(1)}, f32[54,128]{1,0:T(8,128)S(1)}, u32[]{:S(2)}, u32[]{:S(2)}) collective-permute-start(f32[54,128]{1,0:T(8,128)S(1)} %get-tuple-element.11), channel_id=1, source_target_pairs={{4,0},{0,4},{12,8},{8,12},{20,16},{16,20},{28,24},{24,28},{36,32},... | collective-permute-start | bytes 82952 | tf_op jit(solution)/shard_map/ppermute | solution.py:435
  43.6 0.9 %collective-permute-done.10.mate_image = f32[54,128]{1,0:T(8,128)S(1)} collective-permute-done((f32[54,128]{1,0:T(8,128)S(1)}, f32[54,128]{1,0:T(8,128)S(1)}, u32[]{:S(2)}, u32[]{:S(2)}) %collective-permute-start.10) | collective-permute-done | bytes 27680 | tf_op jit(solution)/shard_map/ppermute | solution.py:435
  44.5 0.0 collective-permute-done.9.next_ref
  44.5 3.1 %collective-permute-done.8.prev_ref = f32[16,2560]{1,0:T(8,128)S(1)} collective-permute-done((f32[16,2560]{1,0:T(8,128)S(1)}, f32[16,2560]{1,0:T(8,128)S(1)}, u32[]{:S(2)}, u32[]{:S(2)}) %collective-permute-start.8) | collective-permute-done | bytes 163872 | tf_op jit(solution)/shard_map/ppermute | solution.py:431
  47.6 1.0 %gather.1 = (f32[3,1,2304]{2,1,0:T(1,128)}, f32[9,16,256]{2,1,0:T(8,128)}) custom-call(f32[16,2560]{1,0:T(8,128)S(1)} %pad_maximum_fusion.own_ref, f32[16,2560]{1,0:T(8,128)S(1)} %collective-permute-done.8.prev_ref, f32[16,2560]{1,0:T(8,128)S(1)} %collective-permute-done.9.next_ref, f32[54,128]{1,0:T(8,128)S(1)} %get-tuple-element.10.own_image, ...), custom_call_target="tpu_custom_call" | custom-call | tf_op jit(solution)/shard_map/gather/pallas_call | solution.py:510
  (2 shorter events, 0.1 us)
Async XLA Ops:
  0.6 20.9 %copy-start = (bf16[72,2304]{1,0:T(8,128)(2,1)S(1)}, bf16[72,2304]{1,0:T(8,128)(2,1)}, u32[]{:S(2)}) copy-start(bf16[72,2304]{1,0:T(8,128)(2,1)} %constant.2.clone.feats_ref) | copy-start | bytes 995332
  0.6 12.9 %collective-permute-start.2 = (f32[9,16,256]{2,1,0:T(8,128)}, f32[9,16,256]{2,1,0:T(8,128)S(1)}, u32[]{:S(2)}, u32[]{:S(2)}) collective-permute-start(f32[9,16,256]{2,1,0:T(8,128)} %bitcast.6), channel_id=1, source_target_pairs={{8,0},{12,4},{16,8},{20,12},{24,16},{28,20},{32,24},{36,28},{40,32... | collective-permute-start | bytes 442376 | tf_op jit(solution)/shard_map/ppermute | solution.py:431
  9.6 8.0 %collective-permute-start.1 = (f32[9,16,256]{2,1,0:T(8,128)}, f32[9,16,256]{2,1,0:T(8,128)S(1)}, u32[]{:S(2)}, u32[]{:S(2)}) collective-permute-start(f32[9,16,256]{2,1,0:T(8,128)} %bitcast.7), channel_id=1, source_target_pairs={{248,0},{252,4},{0,8},{4,12},{8,16},{12,20},{16,24},{20,28},{24,32... | collective-permute-start | bytes 442376 | tf_op jit(solution)/shard_map/ppermute | solution.py:431
  11.6 1.9 %collective-permute-start = (f32[56,128]{1,0:T(8,128)S(1)}, f32[56,128]{1,0:T(8,128)S(1)}, u32[]{:S(2)}, u32[]{:S(2)}) collective-permute-start(f32[56,128]{1,0:T(8,128)S(1)} %pack.1.own_tile), channel_id=1, source_target_pairs={{4,0},{0,4},{12,8},{8,12},{20,16},{16,20},{28,24},{24,28},{36,32},... | collective-permute-start | bytes 86024 | tf_op jit(solution)/shard_map/ppermute | solution.py:435
  18.7 2.8 %collective-permute-start.3 = (f32[4,2560]{1,0:T(4,128)S(1)}, f32[4,2560]{1,0:T(4,128)S(1)}, u32[]{:S(2)}, u32[]{:S(2)}) collective-permute-start(f32[4,2560]{1,0:T(4,128)S(1)} %pick.1.own_pick), channel_id=1, source_target_pairs={{4,0},{0,4},{12,8},{8,12},{20,16},{16,20},{28,24},{24,28},{36,32},... | collective-permute-start | bytes 122888 | tf_op jit(solution)/shard_map/ppermute | solution.py:435
  28.3 4.0 %collective-permute-start.4 = (f32[4,2560]{1,0:T(4,128)S(1)}, f32[4,2560]{1,0:T(4,128)S(1)}, u32[]{:S(2)}, u32[]{:S(2)}) collective-permute-start(f32[4,2560]{1,0:T(4,128)S(1)} %get-tuple-element.9), channel_id=1, source_target_pairs={{4,0},{0,4},{12,8},{8,12},{20,16},{16,20},{28,24},{24,28},{36,32},... | collective-permute-start | bytes 122888 | tf_op jit(solution)/shard_map/ppermute | solution.py:435
  32.3 3.1 %collective-permute-start.7 = (f32[4,2560]{1,0:T(4,128)S(1)}, f32[4,2560]{1,0:T(4,128)S(1)}, u32[]{:S(2)}, u32[]{:S(2)}) collective-permute-start(f32[4,2560]{1,0:T(4,128)S(1)} %add.3), channel_id=1, source_target_pairs={{1,0},{2,1},{3,2},{0,3},{5,4},{6,5},{7,6},{4,7},{9,8},{10,9},{11,1... | collective-permute-start | bytes 122888 | tf_op jit(solution)/shard_map/ppermute | solution.py:431
  34.1 4.4 %collective-permute-start.6 = (f32[4,2560]{1,0:T(4,128)S(1)}, f32[4,2560]{1,0:T(4,128)S(1)}, u32[]{:S(2)}, u32[]{:S(2)}) collective-permute-start(f32[4,2560]{1,0:T(4,128)S(1)} %add.3), channel_id=1, source_target_pairs={{2,0},{3,1},{0,2},{1,3},{6,4},{7,5},{4,6},{5,7},{10,8},{11,9},{8,1... | collective-permute-start | bytes 122888 | tf_op jit(solution)/shard_map/ppermute | solution.py:431
  35.3 4.6 %collective-permute-start.5 = (f32[4,2560]{1,0:T(4,128)S(1)}, f32[4,2560]{1,0:T(4,128)S(1)}, u32[]{:S(2)}, u32[]{:S(2)}) collective-permute-start(f32[4,2560]{1,0:T(4,128)S(1)} %add.3), channel_id=1, source_target_pairs={{3,0},{0,1},{1,2},{2,3},{7,4},{4,5},{5,6},{6,7},{11,8},{8,9},{9,10... | collective-permute-start | bytes 122888 | tf_op jit(solution)/shard_map/ppermute | solution.py:431
  39.9 4.5 %collective-permute-start.9 = (f32[16,2560]{1,0:T(8,128)S(1)}, f32[16,2560]{1,0:T(8,128)S(1)}, u32[]{:S(2)}, u32[]{:S(2)}) collective-permute-start(f32[16,2560]{1,0:T(8,128)S(1)} %pad_maximum_fusion.own_ref), channel_id=1, source_target_pairs={{8,0},{12,4},{16,8},{20,12},{24,16},{28,20},{32,24},{36,28},{40,32... | collective-permute-start | bytes 491528 | tf_op jit(solution)/shard_map/ppermute | solution.py:431
  40.0 7.6 %collective-permute-start.8 = (f32[16,2560]{1,0:T(8,128)S(1)}, f32[16,2560]{1,0:T(8,128)S(1)}, u32[]{:S(2)}, u32[]{:S(2)}) collective-permute-start(f32[16,2560]{1,0:T(8,128)S(1)} %pad_maximum_fusion.own_ref), channel_id=1, source_target_pairs={{248,0},{252,4},{0,8},{4,12},{8,16},{12,20},{16,24},{20,28},{24,32... | collective-permute-start | bytes 491528 | tf_op jit(solution)/shard_map/ppermute | solution.py:431
  41.5 3.0 %collective-permute-start.10 = (f32[54,128]{1,0:T(8,128)S(1)}, f32[54,128]{1,0:T(8,128)S(1)}, u32[]{:S(2)}, u32[]{:S(2)}) collective-permute-start(f32[54,128]{1,0:T(8,128)S(1)} %get-tuple-element.11), channel_id=1, source_target_pairs={{4,0},{0,4},{12,8},{8,12},{20,16},{16,20},{28,24},{24,28},{36,32},... | collective-permute-start | bytes 82952 | tf_op jit(solution)/shard_map/ppermute | solution.py:435

commit v4 on v3

--- a/solution.py
+++ b/solution.py
@@ -17,7 +17,9 @@
 GROUPS = PIX // GRP
 ROWS = 3 * PIX // 128
 CHUNKS = PIX // 128
+
 LANES = GRP // 128
+PARTS = (3 * LANES + 1) // 2
 CHAINS = 16
 STEPS = GB // CHAINS
 LOG2E = math.log2(math.e)
@@ -79,7 +81,10 @@
     return lax.axis_index("cell") % 2
 
 
-def pack_kernel(count_ref, block_ref, rays_ref, shift_ref, target_ref, tile_ref):
+def pack_kernel(
+    count_ref, block_ref, rays_ref, shift_ref, target_ref, table_ref, tile_ref, near_ref
+):
+    near_ref[...] = table_ref[...]
     for ch in range(3):
         for n in range(CHUNKS):
             at = CHUNKS * ch + n
@@ -190,15 +195,12 @@
     img_ref[...] = jnp.zeros(img_ref.shape, F32)
     acc_ref[...] = jnp.zeros(acc_ref.shape, F32)
     r_ref[...] = jnp.zeros(r_ref.shape, F32)
-    hwa_ref[...] = jnp.zeros(hwa_ref.shape, BF16)
     rhs_ref[...] = jnp.zeros(rhs_ref.shape, BF16)
     pend_ref[0] = 0
     pend_ref[1] = 1
     pend_ref[2] = 0
-    row = lax.broadcasted_iota(jnp.int32, (72, 3 * 128), 0)
-    lane = lax.broadcasted_iota(jnp.int32, (72, 3 * 128), 1)
-    spread = as_bf16(((row >= 48) & ((row & 7) == lane // 128)).astype(F32))
-    pad = jnp.zeros((56, GB), F32)
+    pend_ref[3] = 0
+    pad = jnp.zeros((48, GB), F32)
 
     def step_rows(s):
         return pl.ds(s, CHAINS, STEPS)
@@ -220,16 +222,27 @@
         colour = jnp.concatenate([par[6:9], jnp.zeros((5, GB), F32)], axis=0)
         ka, kb, kc = pieces(k)
         ca, cb, cc = pieces(colour)
-        tr_ref[0] = jnp.concatenate([ka, ka, kb, kb, kc, kc, ca, cb, cc, pad], axis=0).T
-        tr_ref[1] = jnp.concatenate([ca, cb, cc] * 3 + [pad], axis=0).T
+        tr_ref[0] = jnp.concatenate([ka, ka, kb, kb, kc, kc, ca, cb, cc, colour, pad], axis=0).T
+        tr_ref[1] = jnp.concatenate([ca, cb, cc] * 3 + [pad, pad[:8]], axis=0).T
         for s in range(STEPS):
             rows = slice(CHAINS * s, CHAINS * s + CHAINS)
-            exp_ref[q, rows] = as_bf16(tr_ref[0, step_rows(s)][:, :72])
+            here = tr_ref[0, step_rows(s)]
+            exp_ref[q, rows] = as_bf16(here[:, :72])
+            colb_ref[q, rows] = here
             col_ref[q, rows] = as_bf16(tr_ref[1, step_rows(STEPS - 1 - s)][:, :72])
-        colb_ref[q] = dot(exp_ref[q], spread, ((1,), (0,)))
+
+    def partial(hw_ref, n):
+        wide = range(2 * n, min(2 * n + 2, 3 * LANES))
+        rows = jnp.concatenate([hw_ref[m] for m in wide], axis=1)
+        lanes = slice(256 * n, 256 * n + 128 * len(wide))
+        return dot(rhs_ref[pend_ref[1], :, lanes], rows, ((1,), (1,)))
+
+    def settle(parts):
+        old = acc_ref[pend_ref[0]]
+        acc_ref[pend_ref[0]] = jnp.where(pend_ref[3] > 0, old + sum(parts), old)
 
     def flush(hw_ref):
-        acc_ref[pend_ref[0]] += dot(rhs_ref[pend_ref[1]], hw_ref[...], ((1,), (1,)))
+        settle([partial(hw_ref, n) for n in range(PARTS)])
 
     def task(index, carry):
         tile = index // (GROUPS // 2)
@@ -251,7 +264,10 @@
                 acc = [[jnp.zeros((CHAINS, 128), F32)] * LANES for _ in range(3)]
                 for j in range(STEPS):
                     rows = slice(CHAINS * j, CHAINS * j + CHAINS)
-                    cols = [colb_ref[q, rows, 128 * ch : 128 * ch + 128] for ch in range(3)]
+                    here = colb_ref[q, rows]
+                    cols = [
+                        jnp.broadcast_to(here[:, 72 + ch : 73 + ch], (CHAINS, 128)) for ch in range(3)
+                    ]
                     for v in range(LANES):
                         at = (rows, slice(128 * v, 128 * v + 128))
                         alpha = jnp.exp2(e_ref[at])
@@ -322,8 +338,10 @@
                     begin = chain_ref[k, 4]
                     behind = [leave[:, 128 * v : 128 * v + 128] for v in range(LANES)]
                     scale = [begin[:, 128 * v : 128 * v + 128] for v in range(LANES)]
-                    flush(old_ref)
+                    parts = []
                     for i in range(STEPS):
+                        if i % 2 == 1 and len(parts) < PARTS:
+                            parts.append(partial(old_ref, len(parts)))
                         rows = slice(CHAINS * i, CHAINS * i + CHAINS)
                         j = CHAINS * (STEPS - 1 - i)
                         for v in range(LANES):
@@ -334,11 +352,11 @@
                             h = w * d
                             behind[v] = behind[v] + alpha_ref[at] * d
                             high = as_bf16(h)
-                            new_ref[rows, 128 * v : 128 * v + 128] = high
+                            new_ref[v, rows] = high
                             low = as_bf16(h - high.astype(F32))
-                            new_ref[rows, GRP + 128 * v : GRP + 128 * v + 128] = low
-                            wide = as_bf16(w)
-                            new_ref[rows, 2 * GRP + 128 * v : 2 * GRP + 128 * v + 128] = wide
+                            new_ref[LANES + v, rows] = low
+                            new_ref[2 * LANES + v, rows] = as_bf16(w)
+                    settle(parts)
                     after_ref[...] = row_of(entry, 0)
 
                 turn = pend_ref[2]
@@ -347,6 +365,7 @@
                 pend_ref[0] = q
                 pend_ref[1] = side
                 pend_ref[2] = 1 - turn
+                pend_ref[3] = 1
                 return carry
 
             lax.fori_loop(0, count, backward, 0)
@@ -447,14 +466,14 @@
     return pltpu.with_memory_space_constraint(x, pltpu.VMEM)
 
 
-def pack_call(seg_count, seg_block, ray_count, camera_shift, target):
+def pack_call(seg_count, seg_block, ray_count, camera_shift, target, table):
     return pl.pallas_call(
         pack_kernel,
-        out_shape=vmem_shape(ROWS + 2, 128),
-        in_specs=[smem()] * 4 + [vmem()],
-        out_specs=vmem(),
+        out_shape=(vmem_shape(ROWS + 2, 128), vmem_shape(*table.shape)),
+        in_specs=[smem()] * 4 + [vmem()] * 2,
+        out_specs=(vmem(),) * 2,
         name="pack",
-    )(seg_count, seg_block, ray_count, camera_shift, target)
+    )(seg_count, seg_block, ray_count, camera_shift, target, table)
 
 
 def pick_call(own_tile, mate_tile, own, prev, after):
@@ -464,7 +483,7 @@
         in_specs=[vmem()] * 5,
         out_specs=vmem(),
         name="pick",
-    )(near(own_tile), near(mate_tile), own, near(prev), near(after))
+    )(near(own_tile), near(mate_tile), near(own), near(prev), near(after))
 
 
 def main_call(own_pick, mate_pick, own_tile, mate_tile):
@@ -477,7 +496,7 @@
             pltpu.VMEM((SEGS, 16, GB), F32),
             pltpu.VMEM((SEGS, GB, 72), BF16),
             pltpu.VMEM((SEGS, GB, 72), BF16),
-            pltpu.VMEM((SEGS, GB, 3 * 128), F32),
+            pltpu.VMEM((SEGS, GB, 128), F32),
             pltpu.VMEM((2, ROWS + 2, 128), F32),
             pltpu.VMEM((2, ROWS, 128), F32),
             pltpu.VMEM((GB, GRP), F32),
@@ -486,14 +505,14 @@
             pltpu.VMEM((SEG_MAX, GB, GRP), F32),
             pltpu.VMEM((SEG_MAX, 5, CHAINS, GRP), F32),
             pltpu.VMEM((72, GRP), F32),
-            pltpu.VMEM((GB, 3 * GRP), BF16),
-            pltpu.VMEM((GB, 3 * GRP), BF16),
+            pltpu.VMEM((3 * LANES, GB, 128), BF16),
+            pltpu.VMEM((3 * LANES, GB, 128), BF16),
             pltpu.VMEM((72, GRP), BF16),
             pltpu.VMEM((3, CHAINS, GRP), F32),
             pltpu.VMEM((CHAINS, GRP), F32),
             pltpu.VMEM((2, 48, 3 * GRP), BF16),
             pltpu.VMEM((SEGS, 48, GB), F32),
-            pltpu.SMEM((3,), jnp.int32),
+            pltpu.SMEM((4,), jnp.int32),
             pltpu.VMEM((2, GB, 128), F32),
         ],
         name="splat",
@@ -524,9 +543,10 @@
     table = gaussians.transpose(1, 0, 2)
     prev = shifted(table, "cell", 2)
     after = shifted(table, "cell", -2)
-    tile = pack_call(seg_count, seg_block, ray_count, camera_shift, target[0].transpose(1, 0, 2))
+    goal = target[0].transpose(1, 0, 2)
+    tile, own = pack_call(seg_count, seg_block, ray_count, camera_shift, goal, table)
     mate_tile = mate(tile)
-    own_pick = pick_call(tile, mate_tile, table, prev, after)
+    own_pick = pick_call(tile, mate_tile, own, prev, after)
     mate_pick = mate(own_pick)
     own_image, mate_image, keep, send = main_call(own_pick, mate_pick, tile, mate_tile)
     grads = keep + mate(send)

time: 48.4 us -> 47 us (0.971)
  waiting for transfers between devices: 15.1 us -> 13.8 us
  starting transfers between devices: 21.7 us -> 22.5 us
  Pallas kernels: 9.71 us -> 9.02 us
    ppermute x7, starting transfers between devices: 13.5 us -> 16.8 us  [shifted(): lax.ppermute(block, axis, [((i - distance) % size, i) for i in range(size)])]
    ppermute x4, starting transfers between devices: 8.17 us -> 5.72 us  [mate(): lax.ppermute(block, 'cell', [(i ^ 1, i) for i in range(lax.axis_size('cel...]
    ppermute x7, waiting for transfers between devices: 11.7 us -> 10.4 us  [shifted(): lax.ppermute(block, axis, [((i - distance) % size, i) for i in range(size)])]
    pallas_call x1, Pallas kernels: 1.18 us -> 0.27 us  [pick_call(): pl.pallas_call(pick_kernel, out_shape=vmem_shape(SEGS, PIX + GB), in_spec...]
where the time goes in v4:
time: 47 us; the launch traced here: 47.4 us
  starting transfers between devices  22.5 us (48%)
  waiting for transfers between devices  13.8 us (29%)
  Pallas kernels  9.02 us (19%)
  between operations  1.99 us (4%)
    ppermute x7, starting transfers between devices, shifted(): lax.ppermute(block, axis, [((i - distance) % size, i) for i in range(size)])  16.8 us
    ppermute x7, waiting for transfers between devices, shifted(): lax.ppermute(block, axis, [((i - distance) % size, i) for i in range(size)])  10.4 us
    pallas_call x1, Pallas kernels, main_call(): pl.pallas_call(main_kernel, out_shape=(vmem_shape(ROWS, 128),) * 2 + (vme...  6.75 us
    ppermute x4, starting transfers between devices, mate(): lax.ppermute(block, 'cell', [(i ^ 1, i) for i in range(lax.axis_size('cel...  5.72 us
    ppermute x4, waiting for transfers between devices, mate(): lax.ppermute(block, 'cell', [(i ^ 1, i) for i in range(lax.axis_size('cel...  3.45 us
    pallas_call x1, Pallas kernels, gather_call(): pl.pallas_call(gather_kernel, grid=(1,), out_shape=(shape(3, 1, PIX), sha...  1 us
    pallas_call x1, Pallas kernels, pack_call(): pl.pallas_call(pack_kernel, out_shape=(vmem_shape(ROWS + 2, 128), vmem_sh...  1 us
  transfers between devices with their start and end apart: 11, of which 8 were waited for; matrix products, arithmetic and copies ran while one was open for 0% of the time, Pallas kernels for 2%

profile of v4, /device:TPU:1, one launch (start us, length us, event | category | flops | bytes accessed | tf_op | source)
XLA Modules:
  0.0 47.4 jit_solution(10807255268196893839)
XLA Ops:
  0.6 8.9 %collective-permute-start.2 = (f32[9,16,256]{2,1,0:T(8,128)}, f32[9,16,256]{2,1,0:T(8,128)S(1)}, u32[]{:S(2)}, u32[]{:S(2)}) collective-permute-start(f32[9,16,256]{2,1,0:T(8,128)} %bitcast.6), channel_id=1, source_target_pairs={{8,0},{12,4},{16,8},{20,12},{24,16},{28,20},{32,24},{36,28},{40,32... | collective-permute-start | bytes 442376 | tf_op jit(solution)/shard_map/ppermute | solution.py:450
  9.6 0.0 collective-permute-start.1
  10.9 0.0 copy-start
  10.9 1.0 %pack.1 = (f32[56,128]{1,0:T(8,128)S(1)}, f32[9,16,256]{2,1,0:T(8,128)S(1)}) custom-call(s32[1,1]{1,0:T(1,128)S(6)} %copy.10.count_ref, s32[1,1,3]{2,1,0:T(1,128)} %block_ref.1, s32[1,1]{1,0:T(1,128)S(6)} %copy.11.rays_ref, f32[1,2]{1,0:T(1,128)} %shift_ref.1, f32[3,1,2304]{2,1,0:T(1,128)} %bitcast.9, f32[9,16,256]{2,1,0:T(8,128)} %bitcast.8), custom_call_target="tpu_custom_call" | custom-call | tf_op jit(solution)/shard_map/pack/pallas_call | solution.py:470
  11.9 1.0 %collective-permute-start = (f32[56,128]{1,0:T(8,128)S(1)}, f32[56,128]{1,0:T(8,128)S(1)}, u32[]{:S(2)}, u32[]{:S(2)}) collective-permute-start(f32[56,128]{1,0:T(8,128)S(1)} %get-tuple-element.10.own_tile), channel_id=1, source_target_pairs={{4,0},{0,4},{12,8},{8,12},{20,16},{16,20},{28,24},{24,28},{36,32},... | collective-permute-start | bytes 86024 | tf_op jit(solution)/shard_map/ppermute | solution.py:454
  12.9 0.9 %collective-permute-done.mate_tile = f32[56,128]{1,0:T(8,128)S(1)} collective-permute-done((f32[56,128]{1,0:T(8,128)S(1)}, f32[56,128]{1,0:T(8,128)S(1)}, u32[]{:S(2)}, u32[]{:S(2)}) %collective-permute-start) | collective-permute-done | bytes 28704 | tf_op jit(solution)/shard_map/ppermute | solution.py:454
  13.8 0.0 collective-permute-done.2.next_ref
  13.8 3.8 %collective-permute-done.1.prev_ref = f32[9,16,256]{2,1,0:T(8,128)S(1)} collective-permute-done((f32[9,16,256]{2,1,0:T(8,128)}, f32[9,16,256]{2,1,0:T(8,128)S(1)}, u32[]{:S(2)}, u32[]{:S(2)}) %collective-permute-start.1) | collective-permute-done | bytes 147488 | tf_op jit(solution)/shard_map/ppermute | solution.py:450
  17.5 0.3 pick.1.own_pick
  17.8 1.9 %collective-permute-start.3 = (f32[4,2560]{1,0:T(4,128)S(1)}, f32[4,2560]{1,0:T(4,128)S(1)}, u32[]{:S(2)}, u32[]{:S(2)}) collective-permute-start(f32[4,2560]{1,0:T(4,128)S(1)} %pick.1.own_pick), channel_id=1, source_target_pairs={{4,0},{0,4},{12,8},{8,12},{20,16},{16,20},{28,24},{24,28},{36,32},... | collective-permute-start | bytes 122888 | tf_op jit(solution)/shard_map/ppermute | solution.py:454
  19.7 0.9 %collective-permute-done.3.mate_pick = f32[4,2560]{1,0:T(4,128)S(1)} collective-permute-done((f32[4,2560]{1,0:T(4,128)S(1)}, f32[4,2560]{1,0:T(4,128)S(1)}, u32[]{:S(2)}, u32[]{:S(2)}) %collective-permute-start.3) | collective-permute-done | bytes 40992 | tf_op jit(solution)/shard_map/ppermute | solution.py:454
  20.6 0.0 copy-done
  20.6 6.7 %splat.1 = (f32[54,128]{1,0:T(8,128)S(1)}, f32[54,128]{1,0:T(8,128)S(1)}, f32[4,2560]{1,0:T(4,128)S(1)}, f32[4,2560]{1,0:T(4,128)S(1)}) custom-call(f32[4,2560]{1,0:T(4,128)S(1)} %pick.1.own_pick, f32[4,2560]{1,0:T(4,128)S(1)} %collective-permute-done.3.mate_pick, f32[56,128]{1,0:T(8,128)S(1)} %get-tuple-element.10.own_tile, ...), custom_call_target="tpu_custom_call" | custom-call | tf_op jit(solution)/shard_map/splat/pallas_call | solution.py:490
  27.4 0.4 collective-permute-start.4
  27.8 0.9 %collective-permute-done.4 = f32[4,2560]{1,0:T(4,128)S(1)} collective-permute-done((f32[4,2560]{1,0:T(4,128)S(1)}, f32[4,2560]{1,0:T(4,128)S(1)}, u32[]{:S(2)}, u32[]{:S(2)}) %collective-permute-start.4) | collective-permute-done | bytes 40992 | tf_op jit(solution)/shard_map/ppermute | solution.py:454
  28.7 5.2 %collective-permute-start.7 = (f32[4,2560]{1,0:T(4,128)S(1)}, f32[4,2560]{1,0:T(4,128)S(1)}, u32[]{:S(2)}, u32[]{:S(2)}) collective-permute-start(f32[4,2560]{1,0:T(4,128)S(1)} %add.3), channel_id=1, source_target_pairs={{1,0},{2,1},{3,2},{0,3},{5,4},{6,5},{7,6},{4,7},{9,8},{10,9},{11,1... | collective-permute-start | bytes 122888 | tf_op jit(solution)/shard_map/ppermute | solution.py:450
  33.9 0.4 collective-permute-start.6
  34.3 0.8 %collective-permute-start.5 = (f32[4,2560]{1,0:T(4,128)S(1)}, f32[4,2560]{1,0:T(4,128)S(1)}, u32[]{:S(2)}, u32[]{:S(2)}) collective-permute-start(f32[4,2560]{1,0:T(4,128)S(1)} %add.3), channel_id=1, source_target_pairs={{3,0},{0,1},{1,2},{2,3},{7,4},{4,5},{5,6},{6,7},{11,8},{8,9},{9,10... | collective-permute-start | bytes 122888 | tf_op jit(solution)/shard_map/ppermute | solution.py:450
  35.0 0.0 collective-permute-done.7
  35.0 3.3 %collective-permute-done.6 = f32[4,2560]{1,0:T(4,128)S(1)} collective-permute-done((f32[4,2560]{1,0:T(4,128)S(1)}, f32[4,2560]{1,0:T(4,128)S(1)}, u32[]{:S(2)}, u32[]{:S(2)}) %collective-permute-start.6) | collective-permute-done | bytes 40992 | tf_op jit(solution)/shard_map/ppermute | solution.py:450
  38.3 0.4 collective-permute-done.5
  38.8 0.1 collective-permute-start.9
  38.9 1.5 %collective-permute-start.8 = (f32[16,2560]{1,0:T(8,128)S(1)}, f32[16,2560]{1,0:T(8,128)S(1)}, u32[]{:S(2)}, u32[]{:S(2)}) collective-permute-start(f32[16,2560]{1,0:T(8,128)S(1)} %pad_maximum_fusion.own_ref), channel_id=1, source_target_pairs={{248,0},{252,4},{0,8},{4,12},{8,16},{12,20},{16,24},{20,28},{24,32... | collective-permute-start | bytes 491528 | tf_op jit(solution)/shard_map/ppermute | solution.py:450
  40.3 2.3 %collective-permute-start.10 = (f32[54,128]{1,0:T(8,128)S(1)}, f32[54,128]{1,0:T(8,128)S(1)}, u32[]{:S(2)}, u32[]{:S(2)}) collective-permute-start(f32[54,128]{1,0:T(8,128)S(1)} %get-tuple-element.15), channel_id=1, source_target_pairs={{4,0},{0,4},{12,8},{8,12},{20,16},{16,20},{28,24},{24,28},{36,32},... | collective-permute-start | bytes 82952 | tf_op jit(solution)/shard_map/ppermute | solution.py:454
  42.6 0.9 %collective-permute-done.10.mate_image = f32[54,128]{1,0:T(8,128)S(1)} collective-permute-done((f32[54,128]{1,0:T(8,128)S(1)}, f32[54,128]{1,0:T(8,128)S(1)}, u32[]{:S(2)}, u32[]{:S(2)}) %collective-permute-start.10) | collective-permute-done | bytes 27680 | tf_op jit(solution)/shard_map/ppermute | solution.py:454
  43.5 0.0 collective-permute-done.9.next_ref
  43.5 2.9 %collective-permute-done.8.prev_ref = f32[16,2560]{1,0:T(8,128)S(1)} collective-permute-done((f32[16,2560]{1,0:T(8,128)S(1)}, f32[16,2560]{1,0:T(8,128)S(1)}, u32[]{:S(2)}, u32[]{:S(2)}) %collective-permute-start.8) | collective-permute-done | bytes 163872 | tf_op jit(solution)/shard_map/ppermute | solution.py:450
  46.4 1.0 %gather.1 = (f32[3,1,2304]{2,1,0:T(1,128)}, f32[9,16,256]{2,1,0:T(8,128)}) custom-call(f32[16,2560]{1,0:T(8,128)S(1)} %pad_maximum_fusion.own_ref, f32[16,2560]{1,0:T(8,128)S(1)} %collective-permute-done.8.prev_ref, f32[16,2560]{1,0:T(8,128)S(1)} %collective-permute-done.9.next_ref, f32[54,128]{1,0:T(8,128)S(1)} %get-tuple-element.14.own_image, ...), custom_call_target="tpu_custom_call" | custom-call | tf_op jit(solution)/shard_map/gather/pallas_call | solution.py:529
  (2 shorter events, 0.1 us)
Async XLA Ops:
  0.6 13.1 %collective-permute-start.2 = (f32[9,16,256]{2,1,0:T(8,128)}, f32[9,16,256]{2,1,0:T(8,128)S(1)}, u32[]{:S(2)}, u32[]{:S(2)}) collective-permute-start(f32[9,16,256]{2,1,0:T(8,128)} %bitcast.6), channel_id=1, source_target_pairs={{8,0},{12,4},{16,8},{20,12},{24,16},{28,20},{32,24},{36,28},{40,32... | collective-permute-start | bytes 442376 | tf_op jit(solution)/shard_map/ppermute | solution.py:450
  9.6 8.0 %collective-permute-start.1 = (f32[9,16,256]{2,1,0:T(8,128)}, f32[9,16,256]{2,1,0:T(8,128)S(1)}, u32[]{:S(2)}, u32[]{:S(2)}) collective-permute-start(f32[9,16,256]{2,1,0:T(8,128)} %bitcast.7), channel_id=1, source_target_pairs={{248,0},{252,4},{0,8},{4,12},{8,16},{12,20},{16,24},{20,28},{24,32... | collective-permute-start | bytes 442376 | tf_op jit(solution)/shard_map/ppermute | solution.py:450
  10.9 9.7 %copy-start = (bf16[72,2304]{1,0:T(8,128)(2,1)S(1)}, bf16[72,2304]{1,0:T(8,128)(2,1)}, u32[]{:S(2)}) copy-start(bf16[72,2304]{1,0:T(8,128)(2,1)} %constant.2.clone.feats_ref) | copy-start | bytes 995332
  11.9 1.9 %collective-permute-start = (f32[56,128]{1,0:T(8,128)S(1)}, f32[56,128]{1,0:T(8,128)S(1)}, u32[]{:S(2)}, u32[]{:S(2)}) collective-permute-start(f32[56,128]{1,0:T(8,128)S(1)} %get-tuple-element.10.own_tile), channel_id=1, source_target_pairs={{4,0},{0,4},{12,8},{8,12},{20,16},{16,20},{28,24},{24,28},{36,32},... | collective-permute-start | bytes 86024 | tf_op jit(solution)/shard_map/ppermute | solution.py:454
  17.8 2.8 %collective-permute-start.3 = (f32[4,2560]{1,0:T(4,128)S(1)}, f32[4,2560]{1,0:T(4,128)S(1)}, u32[]{:S(2)}, u32[]{:S(2)}) collective-permute-start(f32[4,2560]{1,0:T(4,128)S(1)} %pick.1.own_pick), channel_id=1, source_target_pairs={{4,0},{0,4},{12,8},{8,12},{20,16},{16,20},{28,24},{24,28},{36,32},... | collective-permute-start | bytes 122888 | tf_op jit(solution)/shard_map/ppermute | solution.py:454
  27.4 1.3 %collective-permute-start.4 = (f32[4,2560]{1,0:T(4,128)S(1)}, f32[4,2560]{1,0:T(4,128)S(1)}, u32[]{:S(2)}, u32[]{:S(2)}) collective-permute-start(f32[4,2560]{1,0:T(4,128)S(1)} %get-tuple-element.13), channel_id=1, source_target_pairs={{4,0},{0,4},{12,8},{8,12},{20,16},{16,20},{28,24},{24,28},{36,32},... | collective-permute-start | bytes 122888 | tf_op jit(solution)/shard_map/ppermute | solution.py:454
  28.7 6.4 %collective-permute-start.7 = (f32[4,2560]{1,0:T(4,128)S(1)}, f32[4,2560]{1,0:T(4,128)S(1)}, u32[]{:S(2)}, u32[]{:S(2)}) collective-permute-start(f32[4,2560]{1,0:T(4,128)S(1)} %add.3), channel_id=1, source_target_pairs={{1,0},{2,1},{3,2},{0,3},{5,4},{6,5},{7,6},{4,7},{9,8},{10,9},{11,1... | collective-permute-start | bytes 122888 | tf_op jit(solution)/shard_map/ppermute | solution.py:450
  33.9 4.4 %collective-permute-start.6 = (f32[4,2560]{1,0:T(4,128)S(1)}, f32[4,2560]{1,0:T(4,128)S(1)}, u32[]{:S(2)}, u32[]{:S(2)}) collective-permute-start(f32[4,2560]{1,0:T(4,128)S(1)} %add.3), channel_id=1, source_target_pairs={{2,0},{3,1},{0,2},{1,3},{6,4},{7,5},{4,6},{5,7},{10,8},{11,9},{8,1... | collective-permute-start | bytes 122888 | tf_op jit(solution)/shard_map/ppermute | solution.py:450
  34.3 4.4 %collective-permute-start.5 = (f32[4,2560]{1,0:T(4,128)S(1)}, f32[4,2560]{1,0:T(4,128)S(1)}, u32[]{:S(2)}, u32[]{:S(2)}) collective-permute-start(f32[4,2560]{1,0:T(4,128)S(1)} %add.3), channel_id=1, source_target_pairs={{3,0},{0,1},{1,2},{2,3},{7,4},{4,5},{5,6},{6,7},{11,8},{8,9},{9,10... | collective-permute-start | bytes 122888 | tf_op jit(solution)/shard_map/ppermute | solution.py:450
  38.8 4.7 %collective-permute-start.9 = (f32[16,2560]{1,0:T(8,128)S(1)}, f32[16,2560]{1,0:T(8,128)S(1)}, u32[]{:S(2)}, u32[]{:S(2)}) collective-permute-start(f32[16,2560]{1,0:T(8,128)S(1)} %pad_maximum_fusion.own_ref), channel_id=1, source_target_pairs={{8,0},{12,4},{16,8},{20,12},{24,16},{28,20},{32,24},{36,28},{40,32... | collective-permute-start | bytes 491528 | tf_op jit(solution)/shard_map/ppermute | solution.py:450
  38.9 7.6 %collective-permute-start.8 = (f32[16,2560]{1,0:T(8,128)S(1)}, f32[16,2560]{1,0:T(8,128)S(1)}, u32[]{:S(2)}, u32[]{:S(2)}) collective-permute-start(f32[16,2560]{1,0:T(8,128)S(1)} %pad_maximum_fusion.own_ref), channel_id=1, source_target_pairs={{248,0},{252,4},{0,8},{4,12},{8,16},{12,20},{16,24},{20,28},{24,32... | collective-permute-start | bytes 491528 | tf_op jit(solution)/shard_map/ppermute | solution.py:450
  40.3 3.2 %collective-permute-start.10 = (f32[54,128]{1,0:T(8,128)S(1)}, f32[54,128]{1,0:T(8,128)S(1)}, u32[]{:S(2)}, u32[]{:S(2)}) collective-permute-start(f32[54,128]{1,0:T(8,128)S(1)} %get-tuple-element.15), channel_id=1, source_target_pairs={{4,0},{0,4},{12,8},{8,12},{20,16},{16,20},{28,24},{24,28},{36,32},... | collective-permute-start | bytes 82952 | tf_op jit(solution)/shard_map/ppermute | solution.py:454

commit v5 on v4

--- a/solution.py
+++ b/solution.py
@@ -42,9 +42,8 @@
         return high, v - high
 
     xx, xy, yy = split(x * x), split(x * y), split(y * y)
-    first = np.stack([np.ones_like(x), x, y, xx[0], xy[0], yy[0], zero, zero])
-    second = np.stack([zero, zero, zero, xx[1], xy[1], yy[1], zero, zero])
-    feats = np.concatenate([first, second] * 3 + [np.zeros((24, PIX))])
+    high = [np.ones_like(x), x, y, xx[0], xy[0], yy[0]]
+    feats = np.stack((high + [xx[1], xy[1], yy[1]]) * 3 + [zero] * 5)
     return feats.astype(jnp.bfloat16)
 
 
@@ -200,7 +199,7 @@
     pend_ref[1] = 1
     pend_ref[2] = 0
     pend_ref[3] = 0
-    pad = jnp.zeros((48, GB), F32)
+    pad = jnp.zeros((104, GB), F32)
 
     def step_rows(s):
         return pl.ds(s, CHAINS, STEPS)
@@ -215,21 +214,17 @@
         k0 = jnp.log2(o) - (0.5 * LOG2E) * (a * mx * mx + 2.0 * b * mx * my + c * my * my)
         k1 = LOG2E * (a * mx + b * my)
         k2 = LOG2E * (b * mx + c * my)
-        zero = jnp.zeros_like(k0)
-        k = jnp.concatenate(
-            [k0, k1, k2, (-0.5 * LOG2E) * a, -LOG2E * b, (-0.5 * LOG2E) * c, zero, zero], axis=0
-        )
-        colour = jnp.concatenate([par[6:9], jnp.zeros((5, GB), F32)], axis=0)
-        ka, kb, kc = pieces(k)
-        ca, cb, cc = pieces(colour)
-        tr_ref[0] = jnp.concatenate([ka, ka, kb, kb, kc, kc, ca, cb, cc, colour, pad], axis=0).T
-        tr_ref[1] = jnp.concatenate([ca, cb, cc] * 3 + [pad, pad[:8]], axis=0).T
+        k3, k4, k5 = (-0.5 * LOG2E) * a, -LOG2E * b, (-0.5 * LOG2E) * c
+        k = jnp.concatenate([k0, k1, k2, k3, k4, k5, k3, k4, k5], axis=0)
+        colour = par[6:9]
+        tr_ref[0] = jnp.concatenate([*pieces(k), pad[:5], colour, pad[:93]], axis=0).T
+        tr_ref[1] = jnp.concatenate([*pieces(colour)] * 3 + [pad[:101]], axis=0).T
         for s in range(STEPS):
             rows = slice(CHAINS * s, CHAINS * s + CHAINS)
             here = tr_ref[0, step_rows(s)]
-            exp_ref[q, rows] = as_bf16(here[:, :72])
+            exp_ref[q, rows] = as_bf16(here[:, :32])
             colb_ref[q, rows] = here
-            col_ref[q, rows] = as_bf16(tr_ref[1, step_rows(STEPS - 1 - s)][:, :72])
+            col_ref[q, rows] = as_bf16(tr_ref[1, step_rows(STEPS - 1 - s)][:, :32])
 
     def partial(hw_ref, n):
         wide = range(2 * n, min(2 * n + 2, 3 * LANES))
@@ -266,7 +261,7 @@
                     rows = slice(CHAINS * j, CHAINS * j + CHAINS)
                     here = colb_ref[q, rows]
                     cols = [
-                        jnp.broadcast_to(here[:, 72 + ch : 73 + ch], (CHAINS, 128)) for ch in range(3)
+                        jnp.broadcast_to(here[:, 32 + ch : 33 + ch], (CHAINS, 128)) for ch in range(3)
                     ]
                     for v in range(LANES):
                         at = (rows, slice(128 * v, 128 * v + 128))
@@ -308,15 +303,14 @@
                 resid_ref[ch] = jnp.broadcast_to(r, (CHAINS, GRP))
                 for n, piece in enumerate(pieces(r)):
                     for m in range(3):
-                        r_ref[24 * n + 8 * m + ch : 24 * n + 8 * m + ch + 1] = piece
+                        r_ref[9 * n + 3 * m + ch : 9 * n + 3 * m + ch + 1] = piece
             rmat_ref[...] = as_bf16(r_ref[...])
             after_ref[...] = jnp.zeros((CHAINS, GRP), F32)
-            rsum = as_bf16(jnp.concatenate([r_ref[0:8], r_ref[24:32], r_ref[48:56]], axis=0))
             moments = feats_ref[0:16, pl.ds(start, GRP)]
             side = 1 - pend_ref[1]
             rhs_ref[side, 0:16, 0:GRP] = moments
             rhs_ref[side, 0:16, GRP : 2 * GRP] = moments
-            rhs_ref[side, 16:40, 2 * GRP :] = rsum
+            rhs_ref[side, 16:48, 2 * GRP :] = as_bf16(r_ref[...])
 
             def backward(index, carry):
                 k = count - 1 - index
@@ -390,7 +384,7 @@
         my = par[1:2] + shift_y
         a, b, c, o = par[2:3], par[3:4], par[4:5], par[5:6]
         m0, m1, m2 = m[0:1], m[1:2], m[2:3]
-        m3, m4, m5 = m[3:4] + m[11:12], m[4:5] + m[12:13], m[5:6] + m[13:14]
+        m3, m4, m5 = m[3:4] + m[6:7], m[4:5] + m[7:8], m[5:6] + m[8:9]
         along_x = m1 - mx * m0
         along_y = m2 - my * m0
         square_x = m3 - 2.0 * mx * m1 + mx * mx * m0
@@ -404,7 +398,7 @@
             -0.5 * square_y,
             m0 / o,
         ]
-        rows += [m[16 + ch : 17 + ch] + m[24 + ch : 25 + ch] + m[32 + ch : 33 + ch] for ch in range(3)]
+        rows += [m[16 + ch : 17 + ch] + m[25 + ch : 26 + ch] + m[34 + ch : 35 + ch] for ch in range(3)]
         block = own_pick[q : q + 1, PIX:]
         home = jnp.floor(block * (1.0 / BLOCKS_DEV))
         parity = home - 2.0 * jnp.floor(home * 0.5)
@@ -494,8 +488,8 @@
         out_specs=(vmem(),) * 4,
         scratch_shapes=[
             pltpu.VMEM((SEGS, 16, GB), F32),
-            pltpu.VMEM((SEGS, GB, 72), BF16),
-            pltpu.VMEM((SEGS, GB, 72), BF16),
+            pltpu.VMEM((SEGS, GB, 32), BF16),
+            pltpu.VMEM((SEGS, GB, 32), BF16),
             pltpu.VMEM((SEGS, GB, 128), F32),
             pltpu.VMEM((2, ROWS + 2, 128), F32),
             pltpu.VMEM((2, ROWS, 128), F32),
@@ -504,10 +498,10 @@
             pltpu.VMEM((SEG_MAX, GB, GRP), F32),
             pltpu.VMEM((SEG_MAX, GB, GRP), F32),
             pltpu.VMEM((SEG_MAX, 5, CHAINS, GRP), F32),
-            pltpu.VMEM((72, GRP), F32),
+            pltpu.VMEM((32, GRP), F32),
             pltpu.VMEM((3 * LANES, GB, 128), BF16),
             pltpu.VMEM((3 * LANES, GB, 128), BF16),
-            pltpu.VMEM((72, GRP), BF16),
+            pltpu.VMEM((32, GRP), BF16),
             pltpu.VMEM((3, CHAINS, GRP), F32),
             pltpu.VMEM((CHAINS, GRP), F32),
             pltpu.VMEM((2, 48, 3 * GRP), BF16),

time: 47 us -> 47.6 us (1.013); the launches traced: 47.4 us -> 46.9 us
  Pallas kernels: 9.02 us -> 6.25 us
  starting transfers between devices: 22.5 us -> 24.1 us
  waiting for transfers between devices: 13.8 us -> 14.5 us
    pallas_call x1, Pallas kernels: 6.75 us -> 4.01 us  [main_call(): pl.pallas_call(main_kernel, out_shape=(vmem_shape(ROWS, 128),) * 2 + (vme...]
    ppermute x7, starting transfers between devices: 16.8 us -> 18.7 us  [shifted(): lax.ppermute(block, axis, [((i - distance) % size, i) for i in range(size)])]
    ppermute x7, waiting for transfers between devices: 10.4 us -> 11 us  [shifted(): lax.ppermute(block, axis, [((i - distance) % size, i) for i in range(size)])]
where the time goes in v5:
time: 47.6 us; the launch traced here: 46.9 us
  starting transfers between devices  24.1 us (51%)
  waiting for transfers between devices  14.5 us (30%)
  Pallas kernels  6.25 us (13%)
  between operations  1.97 us (4%)
    ppermute x7, starting transfers between devices, shifted(): lax.ppermute(block, axis, [((i - distance) % size, i) for i in range(size)])  18.7 us
    ppermute x7, waiting for transfers between devices, shifted(): lax.ppermute(block, axis, [((i - distance) % size, i) for i in range(size)])  11 us
    ppermute x4, starting transfers between devices, mate(): lax.ppermute(block, 'cell', [(i ^ 1, i) for i in range(lax.axis_size('cel...  5.4 us
    pallas_call x1, Pallas kernels, main_call(): pl.pallas_call(main_kernel, out_shape=(vmem_shape(ROWS, 128),) * 2 + (vme...  4.01 us
    ppermute x4, waiting for transfers between devices, mate(): lax.ppermute(block, 'cell', [(i ^ 1, i) for i in range(lax.axis_size('cel...  3.45 us
    pallas_call x1, Pallas kernels, gather_call(): pl.pallas_call(gather_kernel, grid=(1,), out_shape=(shape(3, 1, PIX), sha...  1 us
    pallas_call x1, Pallas kernels, pack_call(): pl.pallas_call(pack_kernel, out_shape=(vmem_shape(ROWS + 2, 128), vmem_sh...  0.95 us
  transfers between devices with their start and end apart: 11, of which 8 were waited for; matrix products, arithmetic and copies ran while one was open for 0% of the time, Pallas kernels for 2%

profile of v5, /device:TPU:1, one launch (start us, length us, event | category | flops | bytes accessed | tf_op | source)
XLA Modules:
  0.0 46.9 jit_solution(14678248492613853932)
XLA Ops:
  0.6 8.9 %collective-permute-start.2 = (f32[9,16,256]{2,1,0:T(8,128)}, f32[9,16,256]{2,1,0:T(8,128)S(1)}, u32[]{:S(2)}, u32[]{:S(2)}) collective-permute-start(f32[9,16,256]{2,1,0:T(8,128)} %bitcast.6), channel_id=1, source_target_pairs={{8,0},{12,4},{16,8},{20,12},{24,16},{28,20},{32,24},{36,28},{40,32... | collective-permute-start | bytes 442376 | tf_op jit(solution)/shard_map/ppermute | solution.py:444
  9.6 0.0 collective-permute-start.1
  10.9 1.0 %pack.1 = (f32[56,128]{1,0:T(8,128)S(1)}, f32[9,16,256]{2,1,0:T(8,128)S(1)}) custom-call(s32[1,1]{1,0:T(1,128)S(6)} %copy.10.count_ref, s32[1,1,3]{2,1,0:T(1,128)} %block_ref.1, s32[1,1]{1,0:T(1,128)S(6)} %copy.11.rays_ref, f32[1,2]{1,0:T(1,128)} %shift_ref.1, f32[3,1,2304]{2,1,0:T(1,128)} %bitcast.9, f32[9,16,256]{2,1,0:T(8,128)} %bitcast.8), custom_call_target="tpu_custom_call" | custom-call | tf_op jit(solution)/shard_map/pack/pallas_call | solution.py:464
  11.8 1.0 %collective-permute-start = (f32[56,128]{1,0:T(8,128)S(1)}, f32[56,128]{1,0:T(8,128)S(1)}, u32[]{:S(2)}, u32[]{:S(2)}) collective-permute-start(f32[56,128]{1,0:T(8,128)S(1)} %get-tuple-element.10.own_tile), channel_id=1, source_target_pairs={{4,0},{0,4},{12,8},{8,12},{20,16},{16,20},{28,24},{24,28},{36,32},... | collective-permute-start | bytes 86024 | tf_op jit(solution)/shard_map/ppermute | solution.py:448
  12.9 0.9 %collective-permute-done.mate_tile = f32[56,128]{1,0:T(8,128)S(1)} collective-permute-done((f32[56,128]{1,0:T(8,128)S(1)}, f32[56,128]{1,0:T(8,128)S(1)}, u32[]{:S(2)}, u32[]{:S(2)}) %collective-permute-start) | collective-permute-done | bytes 28704 | tf_op jit(solution)/shard_map/ppermute | solution.py:448
  13.7 0.0 collective-permute-done.2.next_ref
  13.7 3.8 %collective-permute-done.1.prev_ref = f32[9,16,256]{2,1,0:T(8,128)S(1)} collective-permute-done((f32[9,16,256]{2,1,0:T(8,128)}, f32[9,16,256]{2,1,0:T(8,128)S(1)}, u32[]{:S(2)}, u32[]{:S(2)}) %collective-permute-start.1) | collective-permute-done | bytes 147488 | tf_op jit(solution)/shard_map/ppermute | solution.py:444
  17.5 0.0 copy-start
  17.5 0.3 pick.1.own_pick
  17.8 1.9 %collective-permute-start.3 = (f32[4,2560]{1,0:T(4,128)S(1)}, f32[4,2560]{1,0:T(4,128)S(1)}, u32[]{:S(2)}, u32[]{:S(2)}) collective-permute-start(f32[4,2560]{1,0:T(4,128)S(1)} %pick.1.own_pick), channel_id=1, source_target_pairs={{4,0},{0,4},{12,8},{8,12},{20,16},{16,20},{28,24},{24,28},{36,32},... | collective-permute-start | bytes 122888 | tf_op jit(solution)/shard_map/ppermute | solution.py:448
  19.7 0.9 %collective-permute-done.3.mate_pick = f32[4,2560]{1,0:T(4,128)S(1)} collective-permute-done((f32[4,2560]{1,0:T(4,128)S(1)}, f32[4,2560]{1,0:T(4,128)S(1)}, u32[]{:S(2)}, u32[]{:S(2)}) %collective-permute-start.3) | collective-permute-done | bytes 40992 | tf_op jit(solution)/shard_map/ppermute | solution.py:448
  20.6 0.0 copy-done
  20.6 4.0 %splat.1 = (f32[54,128]{1,0:T(8,128)S(1)}, f32[54,128]{1,0:T(8,128)S(1)}, f32[4,2560]{1,0:T(4,128)S(1)}, f32[4,2560]{1,0:T(4,128)S(1)}) custom-call(f32[4,2560]{1,0:T(4,128)S(1)} %pick.1.own_pick, f32[4,2560]{1,0:T(4,128)S(1)} %collective-permute-done.3.mate_pick, f32[56,128]{1,0:T(8,128)S(1)} %get-tuple-element.10.own_tile, ...), custom_call_target="tpu_custom_call" | custom-call | tf_op jit(solution)/shard_map/splat/pallas_call | solution.py:484
  24.6 0.4 collective-permute-start.4
  25.0 0.9 %collective-permute-done.4 = f32[4,2560]{1,0:T(4,128)S(1)} collective-permute-done((f32[4,2560]{1,0:T(4,128)S(1)}, f32[4,2560]{1,0:T(4,128)S(1)}, u32[]{:S(2)}, u32[]{:S(2)}) %collective-permute-start.4) | collective-permute-done | bytes 40992 | tf_op jit(solution)/shard_map/ppermute | solution.py:448
  25.9 6.5 %collective-permute-start.7 = (f32[4,2560]{1,0:T(4,128)S(1)}, f32[4,2560]{1,0:T(4,128)S(1)}, u32[]{:S(2)}, u32[]{:S(2)}) collective-permute-start(f32[4,2560]{1,0:T(4,128)S(1)} %add.3), channel_id=1, source_target_pairs={{1,0},{2,1},{3,2},{0,3},{5,4},{6,5},{7,6},{4,7},{9,8},{10,9},{11,1... | collective-permute-start | bytes 122888 | tf_op jit(solution)/shard_map/ppermute | solution.py:444
  32.5 1.0 %collective-permute-start.6 = (f32[4,2560]{1,0:T(4,128)S(1)}, f32[4,2560]{1,0:T(4,128)S(1)}, u32[]{:S(2)}, u32[]{:S(2)}) collective-permute-start(f32[4,2560]{1,0:T(4,128)S(1)} %add.3), channel_id=1, source_target_pairs={{2,0},{3,1},{0,2},{1,3},{6,4},{7,5},{4,6},{5,7},{10,8},{11,9},{8,1... | collective-permute-start | bytes 122888 | tf_op jit(solution)/shard_map/ppermute | solution.py:444
  33.5 0.8 %collective-permute-start.5 = (f32[4,2560]{1,0:T(4,128)S(1)}, f32[4,2560]{1,0:T(4,128)S(1)}, u32[]{:S(2)}, u32[]{:S(2)}) collective-permute-start(f32[4,2560]{1,0:T(4,128)S(1)} %add.3), channel_id=1, source_target_pairs={{3,0},{0,1},{1,2},{2,3},{7,4},{4,5},{5,6},{6,7},{11,8},{8,9},{9,10... | collective-permute-start | bytes 122888 | tf_op jit(solution)/shard_map/ppermute | solution.py:444
  34.2 0.0 collective-permute-done.7
  34.2 2.6 %collective-permute-done.6 = f32[4,2560]{1,0:T(4,128)S(1)} collective-permute-done((f32[4,2560]{1,0:T(4,128)S(1)}, f32[4,2560]{1,0:T(4,128)S(1)}, u32[]{:S(2)}, u32[]{:S(2)}) %collective-permute-start.6) | collective-permute-done | bytes 40992 | tf_op jit(solution)/shard_map/ppermute | solution.py:444
  36.8 1.0 %collective-permute-done.5 = f32[4,2560]{1,0:T(4,128)S(1)} collective-permute-done((f32[4,2560]{1,0:T(4,128)S(1)}, f32[4,2560]{1,0:T(4,128)S(1)}, u32[]{:S(2)}, u32[]{:S(2)}) %collective-permute-start.5) | collective-permute-done | bytes 40992 | tf_op jit(solution)/shard_map/ppermute | solution.py:444
  37.9 0.5 %collective-permute-start.9 = (f32[16,2560]{1,0:T(8,128)S(1)}, f32[16,2560]{1,0:T(8,128)S(1)}, u32[]{:S(2)}, u32[]{:S(2)}) collective-permute-start(f32[16,2560]{1,0:T(8,128)S(1)} %pad_maximum_fusion.own_ref), channel_id=1, source_target_pairs={{8,0},{12,4},{16,8},{20,12},{24,16},{28,20},{32,24},{36,28},{40,32... | collective-permute-start | bytes 491528 | tf_op jit(solution)/shard_map/ppermute | solution.py:444
  38.4 1.0 %collective-permute-start.8 = (f32[16,2560]{1,0:T(8,128)S(1)}, f32[16,2560]{1,0:T(8,128)S(1)}, u32[]{:S(2)}, u32[]{:S(2)}) collective-permute-start(f32[16,2560]{1,0:T(8,128)S(1)} %pad_maximum_fusion.own_ref), channel_id=1, source_target_pairs={{248,0},{252,4},{0,8},{4,12},{8,16},{12,20},{16,24},{20,28},{24,32... | collective-permute-start | bytes 491528 | tf_op jit(solution)/shard_map/ppermute | solution.py:444
  39.4 2.0 %collective-permute-start.10 = (f32[54,128]{1,0:T(8,128)S(1)}, f32[54,128]{1,0:T(8,128)S(1)}, u32[]{:S(2)}, u32[]{:S(2)}) collective-permute-start(f32[54,128]{1,0:T(8,128)S(1)} %get-tuple-element.15), channel_id=1, source_target_pairs={{4,0},{0,4},{12,8},{8,12},{20,16},{16,20},{28,24},{24,28},{36,32},... | collective-permute-start | bytes 82952 | tf_op jit(solution)/shard_map/ppermute | solution.py:448
  41.4 0.9 %collective-permute-done.10.mate_image = f32[54,128]{1,0:T(8,128)S(1)} collective-permute-done((f32[54,128]{1,0:T(8,128)S(1)}, f32[54,128]{1,0:T(8,128)S(1)}, u32[]{:S(2)}, u32[]{:S(2)}) %collective-permute-start.10) | collective-permute-done | bytes 27680 | tf_op jit(solution)/shard_map/ppermute | solution.py:448
  42.3 0.0 collective-permute-done.9.next_ref
  42.3 3.6 %collective-permute-done.8.prev_ref = f32[16,2560]{1,0:T(8,128)S(1)} collective-permute-done((f32[16,2560]{1,0:T(8,128)S(1)}, f32[16,2560]{1,0:T(8,128)S(1)}, u32[]{:S(2)}, u32[]{:S(2)}) %collective-permute-start.8) | collective-permute-done | bytes 163872 | tf_op jit(solution)/shard_map/ppermute | solution.py:444
  45.9 1.0 %gather.1 = (f32[3,1,2304]{2,1,0:T(1,128)}, f32[9,16,256]{2,1,0:T(8,128)}) custom-call(f32[16,2560]{1,0:T(8,128)S(1)} %pad_maximum_fusion.own_ref, f32[16,2560]{1,0:T(8,128)S(1)} %collective-permute-done.8.prev_ref, f32[16,2560]{1,0:T(8,128)S(1)} %collective-permute-done.9.next_ref, f32[54,128]{1,0:T(8,128)S(1)} %get-tuple-element.14.own_image, ...), custom_call_target="tpu_custom_call" | custom-call | tf_op jit(solution)/shard_map/gather/pallas_call | solution.py:523
  (2 shorter events, 0.1 us)
Async XLA Ops:
  0.6 13.1 %collective-permute-start.2 = (f32[9,16,256]{2,1,0:T(8,128)}, f32[9,16,256]{2,1,0:T(8,128)S(1)}, u32[]{:S(2)}, u32[]{:S(2)}) collective-permute-start(f32[9,16,256]{2,1,0:T(8,128)} %bitcast.6), channel_id=1, source_target_pairs={{8,0},{12,4},{16,8},{20,12},{24,16},{28,20},{32,24},{36,28},{40,32... | collective-permute-start | bytes 442376 | tf_op jit(solution)/shard_map/ppermute | solution.py:444
  9.6 8.0 %collective-permute-start.1 = (f32[9,16,256]{2,1,0:T(8,128)}, f32[9,16,256]{2,1,0:T(8,128)S(1)}, u32[]{:S(2)}, u32[]{:S(2)}) collective-permute-start(f32[9,16,256]{2,1,0:T(8,128)} %bitcast.7), channel_id=1, source_target_pairs={{248,0},{252,4},{0,8},{4,12},{8,16},{12,20},{16,24},{20,28},{24,32... | collective-permute-start | bytes 442376 | tf_op jit(solution)/shard_map/ppermute | solution.py:444
  11.8 1.9 %collective-permute-start = (f32[56,128]{1,0:T(8,128)S(1)}, f32[56,128]{1,0:T(8,128)S(1)}, u32[]{:S(2)}, u32[]{:S(2)}) collective-permute-start(f32[56,128]{1,0:T(8,128)S(1)} %get-tuple-element.10.own_tile), channel_id=1, source_target_pairs={{4,0},{0,4},{12,8},{8,12},{20,16},{16,20},{28,24},{24,28},{36,32},... | collective-permute-start | bytes 86024 | tf_op jit(solution)/shard_map/ppermute | solution.py:448
  17.5 3.1 %copy-start = (bf16[32,2304]{1,0:T(8,128)(2,1)S(1)}, bf16[32,2304]{1,0:T(8,128)(2,1)}, u32[]{:S(2)}) copy-start(bf16[32,2304]{1,0:T(8,128)(2,1)} %constant.2.clone.feats_ref) | copy-start | bytes 442372
  17.8 2.8 %collective-permute-start.3 = (f32[4,2560]{1,0:T(4,128)S(1)}, f32[4,2560]{1,0:T(4,128)S(1)}, u32[]{:S(2)}, u32[]{:S(2)}) collective-permute-start(f32[4,2560]{1,0:T(4,128)S(1)} %pick.1.own_pick), channel_id=1, source_target_pairs={{4,0},{0,4},{12,8},{8,12},{20,16},{16,20},{28,24},{24,28},{36,32},... | collective-permute-start | bytes 122888 | tf_op jit(solution)/shard_map/ppermute | solution.py:448
  24.6 1.3 %collective-permute-start.4 = (f32[4,2560]{1,0:T(4,128)S(1)}, f32[4,2560]{1,0:T(4,128)S(1)}, u32[]{:S(2)}, u32[]{:S(2)}) collective-permute-start(f32[4,2560]{1,0:T(4,128)S(1)} %get-tuple-element.13), channel_id=1, source_target_pairs={{4,0},{0,4},{12,8},{8,12},{20,16},{16,20},{28,24},{24,28},{36,32},... | collective-permute-start | bytes 122888 | tf_op jit(solution)/shard_map/ppermute | solution.py:448
  25.9 8.3 %collective-permute-start.7 = (f32[4,2560]{1,0:T(4,128)S(1)}, f32[4,2560]{1,0:T(4,128)S(1)}, u32[]{:S(2)}, u32[]{:S(2)}) collective-permute-start(f32[4,2560]{1,0:T(4,128)S(1)} %add.3), channel_id=1, source_target_pairs={{1,0},{2,1},{3,2},{0,3},{5,4},{6,5},{7,6},{4,7},{9,8},{10,9},{11,1... | collective-permute-start | bytes 122888 | tf_op jit(solution)/shard_map/ppermute | solution.py:444
  32.5 4.4 %collective-permute-start.6 = (f32[4,2560]{1,0:T(4,128)S(1)}, f32[4,2560]{1,0:T(4,128)S(1)}, u32[]{:S(2)}, u32[]{:S(2)}) collective-permute-start(f32[4,2560]{1,0:T(4,128)S(1)} %add.3), channel_id=1, source_target_pairs={{2,0},{3,1},{0,2},{1,3},{6,4},{7,5},{4,6},{5,7},{10,8},{11,9},{8,1... | collective-permute-start | bytes 122888 | tf_op jit(solution)/shard_map/ppermute | solution.py:444
  33.5 4.4 %collective-permute-start.5 = (f32[4,2560]{1,0:T(4,128)S(1)}, f32[4,2560]{1,0:T(4,128)S(1)}, u32[]{:S(2)}, u32[]{:S(2)}) collective-permute-start(f32[4,2560]{1,0:T(4,128)S(1)} %add.3), channel_id=1, source_target_pairs={{3,0},{0,1},{1,2},{2,3},{7,4},{4,5},{5,6},{6,7},{11,8},{8,9},{9,10... | collective-permute-start | bytes 122888 | tf_op jit(solution)/shard_map/ppermute | solution.py:444
  37.9 4.4 %collective-permute-start.9 = (f32[16,2560]{1,0:T(8,128)S(1)}, f32[16,2560]{1,0:T(8,128)S(1)}, u32[]{:S(2)}, u32[]{:S(2)}) collective-permute-start(f32[16,2560]{1,0:T(8,128)S(1)} %pad_maximum_fusion.own_ref), channel_id=1, source_target_pairs={{8,0},{12,4},{16,8},{20,12},{24,16},{28,20},{32,24},{36,28},{40,32... | collective-permute-start | bytes 491528 | tf_op jit(solution)/shard_map/ppermute | solution.py:444
  38.4 7.5 %collective-permute-start.8 = (f32[16,2560]{1,0:T(8,128)S(1)}, f32[16,2560]{1,0:T(8,128)S(1)}, u32[]{:S(2)}, u32[]{:S(2)}) collective-permute-start(f32[16,2560]{1,0:T(8,128)S(1)} %pad_maximum_fusion.own_ref), channel_id=1, source_target_pairs={{248,0},{252,4},{0,8},{4,12},{8,16},{12,20},{16,24},{20,28},{24,32... | collective-permute-start | bytes 491528 | tf_op jit(solution)/shard_map/ppermute | solution.py:444
  39.4 2.9 %collective-permute-start.10 = (f32[54,128]{1,0:T(8,128)S(1)}, f32[54,128]{1,0:T(8,128)S(1)}, u32[]{:S(2)}, u32[]{:S(2)}) collective-permute-start(f32[54,128]{1,0:T(8,128)S(1)} %get-tuple-element.15), channel_id=1, source_target_pairs={{4,0},{0,4},{12,8},{8,12},{20,16},{16,20},{28,24},{24,28},{36,32},... | collective-permute-start | bytes 82952 | tf_op jit(solution)/shard_map/ppermute | solution.py:448

commit v6 on v5

--- a/solution.py
+++ b/solution.py
@@ -217,14 +217,16 @@
         k3, k4, k5 = (-0.5 * LOG2E) * a, -LOG2E * b, (-0.5 * LOG2E) * c
         k = jnp.concatenate([k0, k1, k2, k3, k4, k5, k3, k4, k5], axis=0)
         colour = par[6:9]
-        tr_ref[0] = jnp.concatenate([*pieces(k), pad[:5], colour, pad[:93]], axis=0).T
-        tr_ref[1] = jnp.concatenate([*pieces(colour)] * 3 + [pad[:101]], axis=0).T
+        shades = [*pieces(colour)] * 3
+        stack = [*pieces(k), pad[:5], colour, pad[:29], *shades, pad[:37]]
+        tr_ref[q % 2, :GB] = jnp.concatenate(stack, axis=0).T
         for s in range(STEPS):
             rows = slice(CHAINS * s, CHAINS * s + CHAINS)
-            here = tr_ref[0, step_rows(s)]
+            here = tr_ref[q % 2, step_rows(s)]
+            back = slice(GB - CHAINS * s - CHAINS, GB - CHAINS * s)
             exp_ref[q, rows] = as_bf16(here[:, :32])
             colb_ref[q, rows] = here
-            col_ref[q, rows] = as_bf16(tr_ref[1, step_rows(STEPS - 1 - s)][:, :32])
+            col_ref[q, back] = as_bf16(here[:, 64:96])
 
     def partial(hw_ref, n):
         wide = range(2 * n, min(2 * n + 2, 3 * LANES))

time: 47.6 us -> 46.6 us (0.979); the launches traced: 46.9 us -> 46.9 us
  starting transfers between devices: 24.1 us -> 24.7 us
  waiting for transfers between devices: 14.5 us -> 14 us
    ppermute x4, starting transfers between devices: 5.4 us -> 8.35 us  [mate(): lax.ppermute(block, 'cell', [(i ^ 1, i) for i in range(lax.axis_size('cel...]
    ppermute x7, starting transfers between devices: 18.7 us -> 16.3 us  [shifted(): lax.ppermute(block, axis, [((i - distance) % size, i) for i in range(size)])]
where the time goes in v6:
time: 46.6 us; the launch traced here: 46.9 us
  starting transfers between devices  24.7 us (53%)
  waiting for transfers between devices  14 us (30%)
  Pallas kernels  6.21 us (13%)
  between operations  1.98 us (4%)
    ppermute x7, starting transfers between devices, shifted(): lax.ppermute(block, axis, [((i - distance) % size, i) for i in range(size)])  16.3 us
    ppermute x7, waiting for transfers between devices, shifted(): lax.ppermute(block, axis, [((i - distance) % size, i) for i in range(size)])  10.6 us
    ppermute x4, starting transfers between devices, mate(): lax.ppermute(block, 'cell', [(i ^ 1, i) for i in range(lax.axis_size('cel...  8.35 us
    pallas_call x1, Pallas kernels, main_call(): pl.pallas_call(main_kernel, out_shape=(vmem_shape(ROWS, 128),) * 2 + (vme...  3.97 us
    ppermute x4, waiting for transfers between devices, mate(): lax.ppermute(block, 'cell', [(i ^ 1, i) for i in range(lax.axis_size('cel...  3.45 us
    pallas_call x1, Pallas kernels, gather_call(): pl.pallas_call(gather_kernel, grid=(1,), out_shape=(shape(3, 1, PIX), sha...  1.01 us
    pallas_call x1, Pallas kernels, pack_call(): pl.pallas_call(pack_kernel, out_shape=(vmem_shape(ROWS + 2, 128), vmem_sh...  0.95 us
  transfers between devices with their start and end apart: 11, of which 8 were waited for; matrix products, arithmetic and copies ran while one was open for 0% of the time, Pallas kernels for 2%

profile of v6, /device:TPU:1, one launch (start us, length us, event | category | flops | bytes accessed | tf_op | source)
XLA Modules:
  0.0 46.9 jit_solution(13749009502106144327)
XLA Ops:
  0.6 8.9 %collective-permute-start.2 = (f32[9,16,256]{2,1,0:T(8,128)}, f32[9,16,256]{2,1,0:T(8,128)S(1)}, u32[]{:S(2)}, u32[]{:S(2)}) collective-permute-start(f32[9,16,256]{2,1,0:T(8,128)} %bitcast.6), channel_id=1, source_target_pairs={{8,0},{12,4},{16,8},{20,12},{24,16},{28,20},{32,24},{36,28},{40,32... | collective-permute-start | bytes 442376 | tf_op jit(solution)/shard_map/ppermute | solution.py:446
  9.6 0.0 collective-permute-start.1
  10.9 1.0 %pack.1 = (f32[56,128]{1,0:T(8,128)S(1)}, f32[9,16,256]{2,1,0:T(8,128)S(1)}) custom-call(s32[1,1]{1,0:T(1,128)S(6)} %copy.10.count_ref, s32[1,1,3]{2,1,0:T(1,128)} %block_ref.1, s32[1,1]{1,0:T(1,128)S(6)} %copy.11.rays_ref, f32[1,2]{1,0:T(1,128)} %shift_ref.1, f32[3,1,2304]{2,1,0:T(1,128)} %bitcast.9, f32[9,16,256]{2,1,0:T(8,128)} %bitcast.8), custom_call_target="tpu_custom_call" | custom-call | tf_op jit(solution)/shard_map/pack/pallas_call | solution.py:466
  11.8 1.0 %collective-permute-start = (f32[56,128]{1,0:T(8,128)S(1)}, f32[56,128]{1,0:T(8,128)S(1)}, u32[]{:S(2)}, u32[]{:S(2)}) collective-permute-start(f32[56,128]{1,0:T(8,128)S(1)} %get-tuple-element.10.own_tile), channel_id=1, source_target_pairs={{4,0},{0,4},{12,8},{8,12},{20,16},{16,20},{28,24},{24,28},{36,32},... | collective-permute-start | bytes 86024 | tf_op jit(solution)/shard_map/ppermute | solution.py:450
  12.9 0.9 %collective-permute-done.mate_tile = f32[56,128]{1,0:T(8,128)S(1)} collective-permute-done((f32[56,128]{1,0:T(8,128)S(1)}, f32[56,128]{1,0:T(8,128)S(1)}, u32[]{:S(2)}, u32[]{:S(2)}) %collective-permute-start) | collective-permute-done | bytes 28704 | tf_op jit(solution)/shard_map/ppermute | solution.py:450
  13.7 0.0 collective-permute-done.2.next_ref
  13.7 3.8 %collective-permute-done.1.prev_ref = f32[9,16,256]{2,1,0:T(8,128)S(1)} collective-permute-done((f32[9,16,256]{2,1,0:T(8,128)}, f32[9,16,256]{2,1,0:T(8,128)S(1)}, u32[]{:S(2)}, u32[]{:S(2)}) %collective-permute-start.1) | collective-permute-done | bytes 147488 | tf_op jit(solution)/shard_map/ppermute | solution.py:446
  17.5 0.0 copy-start
  17.5 0.3 pick.1.own_pick
  17.8 1.9 %collective-permute-start.3 = (f32[4,2560]{1,0:T(4,128)S(1)}, f32[4,2560]{1,0:T(4,128)S(1)}, u32[]{:S(2)}, u32[]{:S(2)}) collective-permute-start(f32[4,2560]{1,0:T(4,128)S(1)} %pick.1.own_pick), channel_id=1, source_target_pairs={{4,0},{0,4},{12,8},{8,12},{20,16},{16,20},{28,24},{24,28},{36,32},... | collective-permute-start | bytes 122888 | tf_op jit(solution)/shard_map/ppermute | solution.py:450
  19.7 0.9 %collective-permute-done.3.mate_pick = f32[4,2560]{1,0:T(4,128)S(1)} collective-permute-done((f32[4,2560]{1,0:T(4,128)S(1)}, f32[4,2560]{1,0:T(4,128)S(1)}, u32[]{:S(2)}, u32[]{:S(2)}) %collective-permute-start.3) | collective-permute-done | bytes 40992 | tf_op jit(solution)/shard_map/ppermute | solution.py:450
  20.6 0.0 copy-done
  20.6 4.0 %splat.1 = (f32[54,128]{1,0:T(8,128)S(1)}, f32[54,128]{1,0:T(8,128)S(1)}, f32[4,2560]{1,0:T(4,128)S(1)}, f32[4,2560]{1,0:T(4,128)S(1)}) custom-call(f32[4,2560]{1,0:T(4,128)S(1)} %pick.1.own_pick, f32[4,2560]{1,0:T(4,128)S(1)} %collective-permute-done.3.mate_pick, f32[56,128]{1,0:T(8,128)S(1)} %get-tuple-element.10.own_tile, ...), custom_call_target="tpu_custom_call" | custom-call | tf_op jit(solution)/shard_map/splat/pallas_call | solution.py:486
  24.6 3.1 %collective-permute-start.4 = (f32[4,2560]{1,0:T(4,128)S(1)}, f32[4,2560]{1,0:T(4,128)S(1)}, u32[]{:S(2)}, u32[]{:S(2)}) collective-permute-start(f32[4,2560]{1,0:T(4,128)S(1)} %get-tuple-element.13), channel_id=1, source_target_pairs={{4,0},{0,4},{12,8},{8,12},{20,16},{16,20},{28,24},{24,28},{36,32},... | collective-permute-start | bytes 122888 | tf_op jit(solution)/shard_map/ppermute | solution.py:450
  27.6 0.9 %collective-permute-done.4 = f32[4,2560]{1,0:T(4,128)S(1)} collective-permute-done((f32[4,2560]{1,0:T(4,128)S(1)}, f32[4,2560]{1,0:T(4,128)S(1)}, u32[]{:S(2)}, u32[]{:S(2)}) %collective-permute-start.4) | collective-permute-done | bytes 40992 | tf_op jit(solution)/shard_map/ppermute | solution.py:450
  28.5 5.2 %collective-permute-start.7 = (f32[4,2560]{1,0:T(4,128)S(1)}, f32[4,2560]{1,0:T(4,128)S(1)}, u32[]{:S(2)}, u32[]{:S(2)}) collective-permute-start(f32[4,2560]{1,0:T(4,128)S(1)} %add.3), channel_id=1, source_target_pairs={{1,0},{2,1},{3,2},{0,3},{5,4},{6,5},{7,6},{4,7},{9,8},{10,9},{11,1... | collective-permute-start | bytes 122888 | tf_op jit(solution)/shard_map/ppermute | solution.py:446
  33.7 0.0 collective-permute-start.6
  33.7 0.7 %collective-permute-start.5 = (f32[4,2560]{1,0:T(4,128)S(1)}, f32[4,2560]{1,0:T(4,128)S(1)}, u32[]{:S(2)}, u32[]{:S(2)}) collective-permute-start(f32[4,2560]{1,0:T(4,128)S(1)} %add.3), channel_id=1, source_target_pairs={{3,0},{0,1},{1,2},{2,3},{7,4},{4,5},{5,6},{6,7},{11,8},{8,9},{9,10... | collective-permute-start | bytes 122888 | tf_op jit(solution)/shard_map/ppermute | solution.py:446
  34.4 0.4 collective-permute-done.7
  34.8 3.4 %collective-permute-done.6 = f32[4,2560]{1,0:T(4,128)S(1)} collective-permute-done((f32[4,2560]{1,0:T(4,128)S(1)}, f32[4,2560]{1,0:T(4,128)S(1)}, u32[]{:S(2)}, u32[]{:S(2)}) %collective-permute-start.6) | collective-permute-done | bytes 40992 | tf_op jit(solution)/shard_map/ppermute | solution.py:446
  38.2 0.0 collective-permute-done.5
  38.3 0.1 collective-permute-start.9
  38.4 1.5 %collective-permute-start.8 = (f32[16,2560]{1,0:T(8,128)S(1)}, f32[16,2560]{1,0:T(8,128)S(1)}, u32[]{:S(2)}, u32[]{:S(2)}) collective-permute-start(f32[16,2560]{1,0:T(8,128)S(1)} %pad_maximum_fusion.own_ref), channel_id=1, source_target_pairs={{248,0},{252,4},{0,8},{4,12},{8,16},{12,20},{16,24},{20,28},{24,32... | collective-permute-start | bytes 491528 | tf_op jit(solution)/shard_map/ppermute | solution.py:446
  39.8 2.3 %collective-permute-start.10 = (f32[54,128]{1,0:T(8,128)S(1)}, f32[54,128]{1,0:T(8,128)S(1)}, u32[]{:S(2)}, u32[]{:S(2)}) collective-permute-start(f32[54,128]{1,0:T(8,128)S(1)} %get-tuple-element.15), channel_id=1, source_target_pairs={{4,0},{0,4},{12,8},{8,12},{20,16},{16,20},{28,24},{24,28},{36,32},... | collective-permute-start | bytes 82952 | tf_op jit(solution)/shard_map/ppermute | solution.py:450
  42.1 0.9 %collective-permute-done.10.mate_image = f32[54,128]{1,0:T(8,128)S(1)} collective-permute-done((f32[54,128]{1,0:T(8,128)S(1)}, f32[54,128]{1,0:T(8,128)S(1)}, u32[]{:S(2)}, u32[]{:S(2)}) %collective-permute-start.10) | collective-permute-done | bytes 27680 | tf_op jit(solution)/shard_map/ppermute | solution.py:450
  43.0 0.0 collective-permute-done.9.next_ref
  43.0 2.9 %collective-permute-done.8.prev_ref = f32[16,2560]{1,0:T(8,128)S(1)} collective-permute-done((f32[16,2560]{1,0:T(8,128)S(1)}, f32[16,2560]{1,0:T(8,128)S(1)}, u32[]{:S(2)}, u32[]{:S(2)}) %collective-permute-start.8) | collective-permute-done | bytes 163872 | tf_op jit(solution)/shard_map/ppermute | solution.py:446
  45.9 1.0 %gather.1 = (f32[3,1,2304]{2,1,0:T(1,128)}, f32[9,16,256]{2,1,0:T(8,128)}) custom-call(f32[16,2560]{1,0:T(8,128)S(1)} %pad_maximum_fusion.own_ref, f32[16,2560]{1,0:T(8,128)S(1)} %collective-permute-done.8.prev_ref, f32[16,2560]{1,0:T(8,128)S(1)} %collective-permute-done.9.next_ref, f32[54,128]{1,0:T(8,128)S(1)} %get-tuple-element.14.own_image, ...), custom_call_target="tpu_custom_call" | custom-call | tf_op jit(solution)/shard_map/gather/pallas_call | solution.py:525
  (2 shorter events, 0.1 us)
Async XLA Ops:
  0.6 13.1 %collective-permute-start.2 = (f32[9,16,256]{2,1,0:T(8,128)}, f32[9,16,256]{2,1,0:T(8,128)S(1)}, u32[]{:S(2)}, u32[]{:S(2)}) collective-permute-start(f32[9,16,256]{2,1,0:T(8,128)} %bitcast.6), channel_id=1, source_target_pairs={{8,0},{12,4},{16,8},{20,12},{24,16},{28,20},{32,24},{36,28},{40,32... | collective-permute-start | bytes 442376 | tf_op jit(solution)/shard_map/ppermute | solution.py:446
  9.6 8.0 %collective-permute-start.1 = (f32[9,16,256]{2,1,0:T(8,128)}, f32[9,16,256]{2,1,0:T(8,128)S(1)}, u32[]{:S(2)}, u32[]{:S(2)}) collective-permute-start(f32[9,16,256]{2,1,0:T(8,128)} %bitcast.7), channel_id=1, source_target_pairs={{248,0},{252,4},{0,8},{4,12},{8,16},{12,20},{16,24},{20,28},{24,32... | collective-permute-start | bytes 442376 | tf_op jit(solution)/shard_map/ppermute | solution.py:446
  11.8 1.9 %collective-permute-start = (f32[56,128]{1,0:T(8,128)S(1)}, f32[56,128]{1,0:T(8,128)S(1)}, u32[]{:S(2)}, u32[]{:S(2)}) collective-permute-start(f32[56,128]{1,0:T(8,128)S(1)} %get-tuple-element.10.own_tile), channel_id=1, source_target_pairs={{4,0},{0,4},{12,8},{8,12},{20,16},{16,20},{28,24},{24,28},{36,32},... | collective-permute-start | bytes 86024 | tf_op jit(solution)/shard_map/ppermute | solution.py:450
  17.5 3.1 %copy-start = (bf16[32,2304]{1,0:T(8,128)(2,1)S(1)}, bf16[32,2304]{1,0:T(8,128)(2,1)}, u32[]{:S(2)}) copy-start(bf16[32,2304]{1,0:T(8,128)(2,1)} %constant.2.clone.feats_ref) | copy-start | bytes 442372
  17.8 2.8 %collective-permute-start.3 = (f32[4,2560]{1,0:T(4,128)S(1)}, f32[4,2560]{1,0:T(4,128)S(1)}, u32[]{:S(2)}, u32[]{:S(2)}) collective-permute-start(f32[4,2560]{1,0:T(4,128)S(1)} %pick.1.own_pick), channel_id=1, source_target_pairs={{4,0},{0,4},{12,8},{8,12},{20,16},{16,20},{28,24},{24,28},{36,32},... | collective-permute-start | bytes 122888 | tf_op jit(solution)/shard_map/ppermute | solution.py:450
  24.6 3.9 %collective-permute-start.4 = (f32[4,2560]{1,0:T(4,128)S(1)}, f32[4,2560]{1,0:T(4,128)S(1)}, u32[]{:S(2)}, u32[]{:S(2)}) collective-permute-start(f32[4,2560]{1,0:T(4,128)S(1)} %get-tuple-element.13), channel_id=1, source_target_pairs={{4,0},{0,4},{12,8},{8,12},{20,16},{16,20},{28,24},{24,28},{36,32},... | collective-permute-start | bytes 122888 | tf_op jit(solution)/shard_map/ppermute | solution.py:450
  28.5 6.3 %collective-permute-start.7 = (f32[4,2560]{1,0:T(4,128)S(1)}, f32[4,2560]{1,0:T(4,128)S(1)}, u32[]{:S(2)}, u32[]{:S(2)}) collective-permute-start(f32[4,2560]{1,0:T(4,128)S(1)} %add.3), channel_id=1, source_target_pairs={{1,0},{2,1},{3,2},{0,3},{5,4},{6,5},{7,6},{4,7},{9,8},{10,9},{11,1... | collective-permute-start | bytes 122888 | tf_op jit(solution)/shard_map/ppermute | solution.py:446
  33.7 4.5 %collective-permute-start.6 = (f32[4,2560]{1,0:T(4,128)S(1)}, f32[4,2560]{1,0:T(4,128)S(1)}, u32[]{:S(2)}, u32[]{:S(2)}) collective-permute-start(f32[4,2560]{1,0:T(4,128)S(1)} %add.3), channel_id=1, source_target_pairs={{2,0},{3,1},{0,2},{1,3},{6,4},{7,5},{4,6},{5,7},{10,8},{11,9},{8,1... | collective-permute-start | bytes 122888 | tf_op jit(solution)/shard_map/ppermute | solution.py:446
  33.7 4.5 %collective-permute-start.5 = (f32[4,2560]{1,0:T(4,128)S(1)}, f32[4,2560]{1,0:T(4,128)S(1)}, u32[]{:S(2)}, u32[]{:S(2)}) collective-permute-start(f32[4,2560]{1,0:T(4,128)S(1)} %add.3), channel_id=1, source_target_pairs={{3,0},{0,1},{1,2},{2,3},{7,4},{4,5},{5,6},{6,7},{11,8},{8,9},{9,10... | collective-permute-start | bytes 122888 | tf_op jit(solution)/shard_map/ppermute | solution.py:446
  38.3 4.7 %collective-permute-start.9 = (f32[16,2560]{1,0:T(8,128)S(1)}, f32[16,2560]{1,0:T(8,128)S(1)}, u32[]{:S(2)}, u32[]{:S(2)}) collective-permute-start(f32[16,2560]{1,0:T(8,128)S(1)} %pad_maximum_fusion.own_ref), channel_id=1, source_target_pairs={{8,0},{12,4},{16,8},{20,12},{24,16},{28,20},{32,24},{36,28},{40,32... | collective-permute-start | bytes 491528 | tf_op jit(solution)/shard_map/ppermute | solution.py:446
  38.4 7.6 %collective-permute-start.8 = (f32[16,2560]{1,0:T(8,128)S(1)}, f32[16,2560]{1,0:T(8,128)S(1)}, u32[]{:S(2)}, u32[]{:S(2)}) collective-permute-start(f32[16,2560]{1,0:T(8,128)S(1)} %pad_maximum_fusion.own_ref), channel_id=1, source_target_pairs={{248,0},{252,4},{0,8},{4,12},{8,16},{12,20},{16,24},{20,28},{24,32... | collective-permute-start | bytes 491528 | tf_op jit(solution)/shard_map/ppermute | solution.py:446
  39.8 3.2 %collective-permute-start.10 = (f32[54,128]{1,0:T(8,128)S(1)}, f32[54,128]{1,0:T(8,128)S(1)}, u32[]{:S(2)}, u32[]{:S(2)}) collective-permute-start(f32[54,128]{1,0:T(8,128)S(1)} %get-tuple-element.15), channel_id=1, source_target_pairs={{4,0},{0,4},{12,8},{8,12},{20,16},{16,20},{28,24},{24,28},{36,32},... | collective-permute-start | bytes 82952 | tf_op jit(solution)/shard_map/ppermute | solution.py:450
